TPU v7x, 32 devices: a whole 2x2x4 slice. The times are simulated.
32 devices in a mesh: groups: 2 (over y), seq: 4 (over z), section: 2 (over x), head: 2 (over core).
Axes of the slice: x: 2, y: 2, z: 4, core: 2. Of those that a mesh axis runs over, the one named last changes fastest.
Arguments:
- queries: bfloat16 [64, 64, 128], P(('groups', 'seq'), ('section', 'head')), parts along dimension 0, may hold values from -56 to 56
- key_cache: bfloat16 [15872, 8, 128], P(('groups', 'seq'), ('section', 'head')), parts along dimension 0, may hold values from -5 to 5
- value_cache: bfloat16 [15872, 8, 128], P(('groups', 'seq'), ('section', 'head')), parts along dimension 0, may hold values from -5 to 5
- new_features: bfloat16 [512, 8192], P(('groups', 'seq')), parts along dimension 0, may hold values from -60 to 60
- key_weight: bfloat16 [8192, 1024], P('seq', ('section', 'head')), may hold values from -2 to 2
- value_weight: bfloat16 [8192, 1024], P('seq', ('section', 'head')), may hold values from -0.0625 to 0.0625
- key_gain: float32 [128], replicated, may hold values from 0.5 to 2
- out_weight: bfloat16 [8192, 8192], P(('section', 'head'), 'seq'), may hold values from -0.5 to 0.5
- frame_length: int32 [128], P('groups'), parts along dimension 0, may hold values from 1 to 256, 8192 in all
- text_frame: int32 [64], P(('groups', 'seq')), parts along dimension 0, may hold values from 0 to 63
Outputs:
- layer_output: bfloat16 [64, 8192], P(('groups', 'section', 'head'), 'seq'), parts along dimension 0
- new_keys: bfloat16 [512, 8, 128], P(('groups', 'seq'), ('section', 'head')), parts along dimension 0
- new_values: bfloat16 [512, 8, 128], P(('groups', 'seq'), ('section', 'head')), parts along dimension 0
There are 2 independent parts, one for each index of `groups`. A program takes and returns all parts, laid end to end along the dimension named above; an argument that names none is the same for every part. Nothing has to cross between parts.
Inputs may be any that keep to these rules, and one draw needn't show every extreme that they name: `frame_length`: they sum to 8192.
All inputs are finite; a program needn't handle non-finite values.
Results may differ from a plain program's by a relative error of at most 0.015.
Values may be sent and summed in bfloat16 or wider, within the bound.
No kernel may reach another device: no remote copies, remote signals or barrier semaphores. Data moves between devices by JAX's collectives and lax.ppermute only.
A program may use at most 64 MiB of HBM per device.

v0:
```python
import jax
import jax.numpy as jnp
from jax import lax
from jax.sharding import PartitionSpec as P

masked_score = -1e30
norm_epsilon = 1e-05


def for_sending(shard):

    def short(part):
        return part.astype(jnp.bfloat16) if part.dtype == jnp.float32 else part

    return jax.tree.map(short, shard)


def passed_along(shard, axis, by):
    peers = lax.axis_size(axis)
    return lax.ppermute(shard, axis, [(i, (i + by) % peers) for i in range(peers)])


def visit_block(query_block, state, key_block, value_block, key_position, score_scale):
    row_peak, row_total, row_accum, row_limit = state
    block_rows, local_heads, head_depth = query_block.shape
    local_kv = key_block.shape[1]
    grouped = query_block.reshape(block_rows, local_kv, local_heads // local_kv, head_depth)
    scores = (
        jnp.einsum("rcgd,kcd->rcgk", grouped, key_block, preferred_element_type=jnp.float32)
        * score_scale
    )
    visible = (key_position[None, :] < row_limit[:, None])[:, None, None, :]
    block_peak = jnp.max(jnp.where(visible, scores, masked_score), axis=3)
    new_peak = jnp.maximum(row_peak, block_peak)
    weights = jnp.where(visible, jnp.exp(scores - new_peak[..., None]), 0.0)
    factor = jnp.exp(row_peak - new_peak)
    row_total = factor * row_total + jnp.sum(weights, axis=3)
    update = jnp.einsum(
        "rcgk,kcd->rcgd",
        weights.astype(jnp.bfloat16),
        value_block,
        preferred_element_type=jnp.float32,
    )
    row_accum = factor[..., None] * row_accum + update
    return (new_peak, row_total, row_accum, row_limit)


def fresh_state(query_block, row_limit, local_kv):
    block_rows, local_heads, head_depth = query_block.shape
    head_shape = (block_rows, local_kv, local_heads // local_kv)
    return (
        jnp.full(head_shape, masked_score, jnp.float32),
        jnp.zeros(head_shape, jnp.float32),
        jnp.zeros(head_shape + (head_depth,), jnp.float32),
        row_limit,
    )


def pass_forward(query_block, state, with_query):
    if with_query:
        query_block = jax.tree.map(
            lambda part, own: part.astype(own.dtype),
            passed_along(for_sending(query_block), "seq", 1),
            query_block,
        )
    state = passed_along(state, "seq", 1)
    return (query_block, state)


def cycle_attend(
    blocks, move_blocks, key_block, value_block, key_position, score_scale, cycle_length
):

    def one_visit(running, with_query):
        moved_list = []
        for member, move_block in zip(running, move_blocks):
            state_now = visit_block(
                member[0], member[1], key_block, value_block, key_position, score_scale
            )
            moved_list.append(move_block(member[0], state_now, with_query))
        return tuple(moved_list)

    def two_visits(turn_index, running):
        return one_visit(one_visit(running, True), True)

    running = lax.fori_loop(0, cycle_length // 2 - 1, two_visits, blocks)
    finished = one_visit(one_visit(running, True), False)
    outputs = []
    for member in finished:
        row_peak, row_total, row_accum, row_limit = member[1]
        attended = (row_accum / row_total[..., None]).astype(jnp.bfloat16)
        outputs.append(attended.reshape(attended.shape[0], -1))
    return outputs[0]


def on_device(
    queries,
    key_cache,
    value_cache,
    new_features,
    key_weight,
    value_weight,
    key_gain,
    out_weight,
    frame_length,
    text_frame,
):
    head_depth = key_cache.shape[2]
    local_kv = key_cache.shape[1]
    kv_width = key_weight.shape[1]
    new_rows = new_features.shape[0]
    spread = lax.all_to_all(new_features, "seq", split_axis=1, concat_axis=0, tiled=True)
    stacked_weight = jnp.concatenate((key_weight, value_weight), axis=1)
    summed = lax.psum_scatter(
        jnp.dot(spread, stacked_weight, preferred_element_type=jnp.float32).astype(jnp.bfloat16),
        "seq",
        scatter_dimension=0,
        tiled=True,
    ).astype(jnp.float32)
    key_raw = summed[:, :kv_width]
    value_raw = summed[:, kv_width:]
    key_heads = key_raw.reshape(new_rows, local_kv, head_depth)
    mean_square = jnp.mean(key_heads * key_heads, axis=2, keepdims=True)
    new_keys = (key_heads * lax.rsqrt(mean_square + norm_epsilon) * key_gain).astype(jnp.bfloat16)
    new_values = value_raw.reshape(new_rows, local_kv, head_depth).astype(jnp.bfloat16)
    key_block = jnp.concatenate((key_cache, new_keys), axis=0)
    value_block = jnp.concatenate((value_cache, new_values), axis=0)
    block_keys = key_block.shape[0]
    key_position = (
        lax.axis_index("seq") * block_keys + jnp.arange(block_keys, dtype=jnp.int32)
    ).astype(jnp.float32)
    frame_index = jnp.arange(frame_length.shape[0], dtype=jnp.int32)
    row_limit = jnp.sum(
        jnp.where(frame_index[None, :] <= text_frame[:, None], frame_length[None, :], 0), axis=1
    ).astype(jnp.float32)
    score_scale = head_depth ** (-0.5)
    cycle_length = lax.axis_size("seq")
    blocks = ((queries, fresh_state(queries, row_limit, local_kv)),)
    attended = cycle_attend(
        blocks, (pass_forward,), key_block, value_block, key_position, score_scale, cycle_length
    )
    partial_terms = jnp.dot(
        lax.all_gather(attended, "seq", axis=0, tiled=True),
        out_weight,
        preferred_element_type=jnp.float32,
    )
    layer_output = lax.psum_scatter(
        partial_terms.astype(jnp.bfloat16), ("section", "head"), scatter_dimension=0, tiled=True
    )
    return (layer_output, new_keys, new_values)


def solution(mesh):
    placed = (
        P(("groups", "seq"), ("section", "head"), None),
        P(("groups", "seq"), ("section", "head"), None),
        P(("groups", "seq"), ("section", "head"), None),
        P(("groups", "seq"), None),
        P("seq", ("section", "head")),
        P("seq", ("section", "head")),
        P(),
        P(("section", "head"), "seq"),
        P("groups"),
        P(("groups", "seq")),
    )
    return jax.shard_map(
        on_device,
        mesh=mesh,
        in_specs=placed,
        out_specs=(
            P(("groups", "section", "head"), "seq"),
            P(("groups", "seq"), ("section", "head"), None),
            P(("groups", "seq"), ("section", "head"), None),
        ),
        check_vma=False,
    )
```

profile of v0, /device:TPU:0, one launch (start us, length us, event | category | flops | bytes accessed | tf_op | source)
XLA Modules:
  0.0 143.7 jit_solution(10098577655566775212)
XLA Ops:
  7.2 2.3 %copy.138 = bf16[8,4,8,2048]{3,2,0,1:T(8,128)(2,1)} copy(bf16[8,4,8,2048]{3,2,1,0:T(8,128)(2,1)} %bitcast.94) | data formatting | bytes 2097152 | tf_op jit(solution)/shard_map/all_to_all | solution.py:112
  9.5 6.3 %all-to-all-start = ((bf16[64,4,2048]{2,0,1:T(8,128)(2,1)}), bf16[64,4,2048]{2,0,1:T(8,128)(2,1)S(1)}, u32[]{:S(2)}, u32[]{:S(2)}) async-start(bf16[64,4,2048]{2,0,1:T(8,128)(2,1)} %bitcast.90), calls=%async_computation | async-start | bytes 2097152 | tf_op jit(solution)/shard_map/all_to_all | solution.py:112
  15.9 0.2 select_reduce_fusion.4
  16.1 2.1 %collective-permute-start.1 = (f32[8]{0:T(128)S(1)}, f32[8]{0:T(128)S(1)}, u32[]{:S(2)}, u32[]{:S(2)}) collective-permute-start(f32[8]{0:T(128)S(1)} %convert_element_type.49), channel_id=1, source_target_pairs={{0,4},{4,8},{8,12},{12,0},{1,5},{5,9},{9,13},{13,1},{2,6},{6,10},{... | collective-permute-start | bytes 104 | tf_op jit(solution)/shard_map/while/body/eval_jaxpr/ppermute | solution.py:20
  18.1 1.5 %collective-permute-start.2 = (bf16[8,16,128]{2,1,0:T(8,128)(2,1)S(1)}, bf16[8,16,128]{2,1,0:T(8,128)(2,1)S(1)}, u32[]{:S(2)}, u32[]{:S(2)}) collective-permute-start(bf16[8,16,128]{2,1,0:T(8,128)(2,1)S(1)} %copy-done.3), channel_id=1, source_target_pairs={{0,4},{4,8},{8,12},{12,0},{1,5},{5,9},{9,13},{13,1},{2,6},{6,10},{... | collective-permute-start | bytes 98312 | tf_op jit(solution)/shard_map/while/body/eval_jaxpr/ppermute | solution.py:20
  19.6 22.7 %all-to-all-done = bf16[64,4,2048]{2,0,1:T(8,128)(2,1)S(1)} async-done(((bf16[64,4,2048]{2,0,1:T(8,128)(2,1)}), bf16[64,4,2048]{2,0,1:T(8,128)(2,1)S(1)}, u32[]{:S(2)}, u32[]{:S(2)}) %all-to-all-start) | async-done | bytes 1048608 | tf_op jit(solution)/shard_map/all_to_all | solution.py:112
  42.3 2.4 %fusion.11 = bf16[256,512]{0,1:T(8,128)(2,1)S(1)} fusion(bf16[256,2048]{1,0:T(8,128)(2,1)S(1)} %bitcast.95, bf16[2048,256]{1,0:T(8,128)(2,1)} %param.15, bf16[2048,256]{1,0:T(8,128)(2,1)} %param.14), kind=kOutput, calls=%fused_computation.14 | convolution fusion | flops 541196288 | bytes 3407872 | tf_op jit(solution)/shard_map/dot_general | solution.py:115
  44.7 0.8 copy.112
  45.6 0.1 copy.98
  45.8 0.2 copy-done.1
  46.0 0.1 copy.104
  46.2 5.4 %collective-permute-done.4 = f32[8]{0:T(128)S(1)} collective-permute-done((f32[8]{0:T(128)S(1)}, f32[8]{0:T(128)S(1)}, u32[]{:S(2)}, u32[]{:S(2)}) %collective-permute-start.4) | collective-permute-done | bytes 64 | tf_op jit(solution)/shard_map/while/body/eval_jaxpr/ppermute | solution.py:20
  51.6 5.4 %collective-permute-done.7 = f32[8]{0:T(128)S(1)} collective-permute-done((f32[8]{0:T(128)S(1)}, f32[8]{0:T(128)S(1)}, u32[]{:S(2)}, u32[]{:S(2)}) %collective-permute-start.7) | collective-permute-done | bytes 64 | tf_op jit(solution)/shard_map/ppermute | solution.py:20
  56.9 0.1 broadcast_compare_fusion
  57.0 0.5 collective-permute-done.5
  57.5 7.0 %reduce-scatter.7.cloned.1.call-done = bf16[64,512]{1,0:T(8,128)(2,1)} async-done(((bf16[256,512]{1,0:T(8,128)(2,1)}), bf16[64,512]{1,0:T(8,128)(2,1)}) %reduce-scatter.7.cloned.1.call-update) | async-done | bytes 65552 | tf_op jit(solution)/shard_map/reduce_scatter | solution.py:114
  64.5 0.8 fusion.58
  65.3 0.1 multiply_reduce_fusion
  65.6 0.6 select_reduce_fusion.3
  66.3 0.4 fusion.15
  66.7 0.1 copy.114
  66.9 0.4 fusion.14
  67.3 1.3 collective-permute-start.9
  68.6 0.5 collective-permute-start.13
  69.1 0.6 select_reduce_fusion.2
  69.7 0.6 select_reduce_fusion.1
  70.3 0.6 select_reduce_fusion
  70.9 0.9 collective-permute-done
  71.7 2.4 %collective-permute-start.3 = (f32[8,2,8]{2,0,1:T(8,128)S(1)}, f32[8,2,8]{2,0,1:T(8,128)S(1)}, u32[]{:S(2)}, u32[]{:S(2)}) collective-permute-start(f32[8,2,8]{2,0,1:T(8,128)S(1)} %max.22), channel_id=1, source_target_pairs={{0,4},{4,8},{8,12},{12,0},{1,5},{5,9},{9,13},{13,1},{2,6},{6,10},{... | collective-permute-start | bytes 1544 | tf_op jit(solution)/shard_map/while/body/eval_jaxpr/ppermute | solution.py:20
  74.1 0.4 fusion.17
  74.5 0.1 collective-permute-start.14
  74.6 2.6 %collective-permute-done.3 = f32[8,2,8]{2,0,1:T(8,128)S(1)} collective-permute-done((f32[8,2,8]{2,0,1:T(8,128)S(1)}, f32[8,2,8]{2,0,1:T(8,128)S(1)}, u32[]{:S(2)}, u32[]{:S(2)}) %collective-permute-start.3) | collective-permute-done | bytes 544 | tf_op jit(solution)/shard_map/while/body/eval_jaxpr/ppermute | solution.py:20
  77.2 0.6 collective-permute-start.6
  77.7 0.4 fusion.19
  78.1 1.9 %collective-permute-done.14 = f32[8,2,8]{2,0,1:T(8,128)S(1)} collective-permute-done((f32[8,2,8]{2,0,1:T(8,128)S(1)}, f32[8,2,8]{2,0,1:T(8,128)S(1)}, u32[]{:S(2)}, u32[]{:S(2)}) %collective-permute-start.14) | collective-permute-done | bytes 544 | tf_op jit(solution)/shard_map/while/body/eval_jaxpr/ppermute | solution.py:20
  80.0 2.7 %collective-permute-done.6 = f32[8,2,8]{2,0,1:T(8,128)S(1)} collective-permute-done((f32[8,2,8]{2,0,1:T(8,128)S(1)}, f32[8,2,8]{2,0,1:T(8,128)S(1)}, u32[]{:S(2)}, u32[]{:S(2)}) %collective-permute-start.6) | collective-permute-done | bytes 544 | tf_op jit(solution)/shard_map/ppermute | solution.py:20
  82.7 0.4 multiply_add_fusion.2
  83.2 0.4 fusion.21
  83.6 5.7 %collective-permute-done.10 = f32[8,2,8,128]{3,2,0,1:T(8,128)S(1)} collective-permute-done((f32[8,2,8,128]{3,2,0,1:T(8,128)S(1)}, f32[8,2,8,128]{3,2,0,1:T(8,128)S(1)}, u32[]{:S(2)}, u32[]{:S(2)}) %collective-permute-start.10) | collective-permute-done | bytes 65568 | tf_op jit(solution)/shard_map/while/body/eval_jaxpr/ppermute | solution.py:20
  89.3 0.4 multiply_add_fusion.1
  89.8 6.0 %collective-permute-done.11 = f32[8,2,8,128]{3,2,0,1:T(8,128)S(1)} collective-permute-done((f32[8,2,8,128]{3,2,0,1:T(8,128)S(1)}, f32[8,2,8,128]{3,2,0,1:T(8,128)S(1)}, u32[]{:S(2)}, u32[]{:S(2)}) %collective-permute-start.11) | collective-permute-done | bytes 65568 | tf_op jit(solution)/shard_map/ppermute | solution.py:20
  95.8 0.4 multiply_add_fusion
  96.3 6.1 %collective-permute-done.16 = f32[8,2,8]{2,0,1:T(8,128)S(1)} collective-permute-done((f32[8,2,8]{2,0,1:T(8,128)S(1)}, f32[8,2,8]{2,0,1:T(8,128)S(1)}, u32[]{:S(2)}, u32[]{:S(2)}) %collective-permute-start.16) | collective-permute-done | bytes 544 | tf_op jit(solution)/shard_map/ppermute | solution.py:20
  102.6 13.3 %all_gather.3 = bf16[32,2048]{1,0:T(8,128)(2,1)S(1)} all-gather(bf16[8,2048]{1,0:T(8,128)(2,1)S(1)} %bitcast.98), channel_id=1, replica_groups=mesh['groups'=2,'seq'=4,'section'=2,'head'=2] {'seq'}, dimensions={0}, use_global_device_ids=true | all-gather | bytes 163840 | tf_op jit(solution)/shard_map/all_gather | solution.py:143
  115.9 2.2 %convolution_convert_fusion = bf16[32,2048]{1,0:T(8,128)(2,1)} fusion(bf16[32,2048]{1,0:T(8,128)(2,1)S(1)} %all_gather.3, bf16[2048,2048]{1,0:T(8,128)(2,1)S(1)} %bitcast.93), kind=kOutput, calls=%fused_computation.8 | convolution fusion | flops 268500992 | bytes 8650752 | tf_op jit(solution)/shard_map/dot_general | solution.py:142
  118.1 0.6 copy.107
  118.8 0.7 copy.110
  119.5 17.3 %reduce-scatter.5.cloned.1.call-done = bf16[8,2048]{1,0:T(8,128)(2,1)} async-done(((bf16[32,2048]{1,0:T(8,128)(2,1)}), bf16[8,2048]{1,0:T(8,128)(2,1)}) %reduce-scatter.5.cloned.1.call-update) | async-done | bytes 32784 | tf_op jit(solution)/shard_map/reduce_scatter | solution.py:147
  (54 shorter events, 1.0 us)
Async XLA Ops:
  7.2 8.7 %copy-start.4 = (s32[64]{0:T(128)S(1)}, s32[64]{0:T(128)}, u32[]{:S(2)}) copy-start(s32[64]{0:T(128)} %param.18) | copy-start | bytes 772
  7.2 8.7 %copy-start.5 = (s32[8]{0:T(128)S(1)}, s32[8]{0:T(128)}, u32[]{:S(2)}) copy-start(s32[8]{0:T(128)} %param.19) | copy-start | bytes 100
  7.2 10.9 %copy-start.3 = (bf16[8,16,128]{2,1,0:T(8,128)(2,1)S(1)}, bf16[8,16,128]{2,1,0:T(8,128)(2,1)}, u32[]{:S(2)}) copy-start(bf16[8,16,128]{2,1,0:T(8,128)(2,1)} %param.10) | copy-start | bytes 98308
  9.5 32.8 %all-to-all-start = ((bf16[64,4,2048]{2,0,1:T(8,128)(2,1)}), bf16[64,4,2048]{2,0,1:T(8,128)(2,1)S(1)}, u32[]{:S(2)}, u32[]{:S(2)}) async-start(bf16[64,4,2048]{2,0,1:T(8,128)(2,1)} %bitcast.90), calls=%async_computation | async-start | bytes 2097152 | tf_op jit(solution)/shard_map/all_to_all | solution.py:112
  15.9 48.6 %reduce-scatter.7.cloned.1.call-start = ((), (), s32[]{:S(2)}) async-start(), calls=%async_computation.4 | async-start | bytes 327680 | tf_op jit(solution)/shard_map/reduce_scatter | solution.py:114
  16.1 30.1 %collective-permute-start.1 = (f32[8]{0:T(128)S(1)}, f32[8]{0:T(128)S(1)}, u32[]{:S(2)}, u32[]{:S(2)}) collective-permute-start(f32[8]{0:T(128)S(1)} %convert_element_type.49), channel_id=1, source_target_pairs={{0,4},{4,8},{8,12},{12,0},{1,5},{5,9},{9,13},{13,1},{2,6},{6,10},{... | collective-permute-start | bytes 104 | tf_op jit(solution)/shard_map/while/body/eval_jaxpr/ppermute | solution.py:20
  18.1 33.4 %collective-permute-start.2 = (bf16[8,16,128]{2,1,0:T(8,128)(2,1)S(1)}, bf16[8,16,128]{2,1,0:T(8,128)(2,1)S(1)}, u32[]{:S(2)}, u32[]{:S(2)}) collective-permute-start(bf16[8,16,128]{2,1,0:T(8,128)(2,1)S(1)} %copy-done.3), channel_id=1, source_target_pairs={{0,4},{4,8},{8,12},{12,0},{1,5},{5,9},{9,13},{13,1},{2,6},{6,10},{... | collective-permute-start | bytes 98312 | tf_op jit(solution)/shard_map/while/body/eval_jaxpr/ppermute | solution.py:20
  42.3 3.3 %copy-start = (bf16[1984,2,128]{2,1,0:T(2,128)(2,1)S(1)}, bf16[1984,2,128]{2,1,0:T(2,128)(2,1)}, u32[]{:S(2)}) copy-start(bf16[1984,2,128]{2,1,0:T(2,128)(2,1)} %param.11) | copy-start | bytes 3047428
  44.7 1.3 copy-start.1
  45.6 91.3 %reduce-scatter.5.cloned.1.call-start = ((), (), s32[]{:S(2)}) async-start(), calls=%async_computation.3 | async-start | bytes 163840 | tf_op jit(solution)/shard_map/reduce_scatter | solution.py:147
  45.6 19.9 %copy-start.2 = (f32[128]{0:T(128)S(1)}, f32[128]{0:T(128)}, u32[]{:S(2)}) copy-start(f32[128]{0:T(128)} %param.16) | copy-start | bytes 1540
  46.1 5.4 %collective-permute-start.4 = (f32[8]{0:T(128)S(1)}, f32[8]{0:T(128)S(1)}, u32[]{:S(2)}, u32[]{:S(2)}) collective-permute-start(f32[8]{0:T(128)S(1)} %collective-permute-done.1), channel_id=1, source_target_pairs={{0,4},{4,8},{8,12},{12,0},{1,5},{5,9},{9,13},{13,1},{2,6},{6,10},{... | collective-permute-start | bytes 104 | tf_op jit(solution)/shard_map/while/body/eval_jaxpr/ppermute | solution.py:20
  51.6 5.4 %collective-permute-start.7 = (f32[8]{0:T(128)S(1)}, f32[8]{0:T(128)S(1)}, u32[]{:S(2)}, u32[]{:S(2)}) collective-permute-start(f32[8]{0:T(128)S(1)} %collective-permute-done.4), channel_id=1, source_target_pairs={{0,4},{4,8},{8,12},{12,0},{1,5},{5,9},{9,13},{13,1},{2,6},{6,10},{... | collective-permute-start | bytes 104 | tf_op jit(solution)/shard_map/ppermute | solution.py:20
  51.6 5.9 %collective-permute-start.5 = (bf16[8,16,128]{2,1,0:T(8,128)(2,1)S(1)}, bf16[8,16,128]{2,1,0:T(8,128)(2,1)S(1)}, u32[]{:S(2)}, u32[]{:S(2)}) collective-permute-start(bf16[8,16,128]{2,1,0:T(8,128)(2,1)S(1)} %collective-permute-done.2), channel_id=1, source_target_pairs={{0,4},{4,8},{8,12},{12,0},{1,5},{5,9},{9,13},{13,1},{2,6},{6,10},{... | collective-permute-start | bytes 98312 | tf_op jit(solution)/shard_map/while/body/eval_jaxpr/ppermute | solution.py:20
  57.5 12.8 %collective-permute-start.8 = (bf16[8,16,128]{2,1,0:T(8,128)(2,1)S(1)}, bf16[8,16,128]{2,1,0:T(8,128)(2,1)S(1)}, u32[]{:S(2)}, u32[]{:S(2)}) collective-permute-start(bf16[8,16,128]{2,1,0:T(8,128)(2,1)S(1)} %collective-permute-done.5), channel_id=1, source_target_pairs={{0,4},{4,8},{8,12},{12,0},{1,5},{5,9},{9,13},{13,1},{2,6},{6,10},{... | collective-permute-start | bytes 98312 | tf_op jit(solution)/shard_map/ppermute | solution.py:20
  66.2 5.5 %collective-permute-start = (f32[8,2,8]{2,0,1:T(8,128)S(1)}, f32[8,2,8]{2,0,1:T(8,128)S(1)}, u32[]{:S(2)}, u32[]{:S(2)}) collective-permute-start(f32[8,2,8]{2,0,1:T(8,128)S(1)} %broadcast_maximum_fusion), channel_id=1, source_target_pairs={{0,4},{4,8},{8,12},{12,0},{1,5},{5,9},{9,13},{13,1},{2,6},{6,10},{... | collective-permute-start | bytes 1544 | tf_op jit(solution)/shard_map/while/body/eval_jaxpr/ppermute | solution.py:20
  67.3 15.4 %collective-permute-start.9 = (f32[8,2,8,128]{3,2,0,1:T(8,128)S(1)}, f32[8,2,8,128]{3,2,0,1:T(8,128)S(1)}, u32[]{:S(2)}, u32[]{:S(2)}) collective-permute-start(f32[8,2,8,128]{3,2,0,1:T(8,128)S(1)} %fusion.14), channel_id=1, source_target_pairs={{0,4},{4,8},{8,12},{12,0},{1,5},{5,9},{9,13},{13,1},{2,6},{6,10},{... | collective-permute-start | bytes 196616 | tf_op jit(solution)/shard_map/while/body/eval_jaxpr/ppermute | solution.py:20
  68.6 5.8 %collective-permute-start.13 = (f32[8,2,8]{2,0,1:T(8,128)S(1)}, f32[8,2,8]{2,0,1:T(8,128)S(1)}, u32[]{:S(2)}, u32[]{:S(2)}) collective-permute-start(f32[8,2,8]{2,0,1:T(8,128)S(1)} %get-tuple-element.67), channel_id=1, source_target_pairs={{0,4},{4,8},{8,12},{12,0},{1,5},{5,9},{9,13},{13,1},{2,6},{6,10},{... | collective-permute-start | bytes 1544 | tf_op jit(solution)/shard_map/while/body/eval_jaxpr/ppermute | solution.py:20
  71.7 5.4 %collective-permute-start.3 = (f32[8,2,8]{2,0,1:T(8,128)S(1)}, f32[8,2,8]{2,0,1:T(8,128)S(1)}, u32[]{:S(2)}, u32[]{:S(2)}) collective-permute-start(f32[8,2,8]{2,0,1:T(8,128)S(1)} %max.22), channel_id=1, source_target_pairs={{0,4},{4,8},{8,12},{12,0},{1,5},{5,9},{9,13},{13,1},{2,6},{6,10},{... | collective-permute-start | bytes 1544 | tf_op jit(solution)/shard_map/while/body/eval_jaxpr/ppermute | solution.py:20
  74.5 5.5 %collective-permute-start.14 = (f32[8,2,8]{2,0,1:T(8,128)S(1)}, f32[8,2,8]{2,0,1:T(8,128)S(1)}, u32[]{:S(2)}, u32[]{:S(2)}) collective-permute-start(f32[8,2,8]{2,0,1:T(8,128)S(1)} %get-tuple-element.58), channel_id=1, source_target_pairs={{0,4},{4,8},{8,12},{12,0},{1,5},{5,9},{9,13},{13,1},{2,6},{6,10},{... | collective-permute-start | bytes 1544 | tf_op jit(solution)/shard_map/while/body/eval_jaxpr/ppermute | solution.py:20
  77.2 5.5 %collective-permute-start.6 = (f32[8,2,8]{2,0,1:T(8,128)S(1)}, f32[8,2,8]{2,0,1:T(8,128)S(1)}, u32[]{:S(2)}, u32[]{:S(2)}) collective-permute-start(f32[8,2,8]{2,0,1:T(8,128)S(1)} %max.23), channel_id=1, source_target_pairs={{0,4},{4,8},{8,12},{12,0},{1,5},{5,9},{9,13},{13,1},{2,6},{6,10},{... | collective-permute-start | bytes 1544 | tf_op jit(solution)/shard_map/ppermute | solution.py:20
  80.0 9.8 %collective-permute-start.15 = (f32[8,2,8]{2,0,1:T(8,128)S(1)}, f32[8,2,8]{2,0,1:T(8,128)S(1)}, u32[]{:S(2)}, u32[]{:S(2)}) collective-permute-start(f32[8,2,8]{2,0,1:T(8,128)S(1)} %get-tuple-element.56), channel_id=1, source_target_pairs={{0,4},{4,8},{8,12},{12,0},{1,5},{5,9},{9,13},{13,1},{2,6},{6,10},{... | collective-permute-start | bytes 1544 | tf_op jit(solution)/shard_map/ppermute | solution.py:20
  83.1 6.1 %collective-permute-start.10 = (f32[8,2,8,128]{3,2,0,1:T(8,128)S(1)}, f32[8,2,8,128]{3,2,0,1:T(8,128)S(1)}, u32[]{:S(2)}, u32[]{:S(2)}) collective-permute-start(f32[8,2,8,128]{3,2,0,1:T(8,128)S(1)} %multiply_add_fusion.2), channel_id=1, source_target_pairs={{0,4},{4,8},{8,12},{12,0},{1,5},{5,9},{9,13},{13,1},{2,6},{6,10},{... | collective-permute-start | bytes 196616 | tf_op jit(solution)/shard_map/while/body/eval_jaxpr/ppermute | solution.py:20
  83.2 32.7 %slice-start = ((s8[8388608]{0:T(1024)(128)(4,1)}), s8[4194304]{0:T(1024)(128)(4,1)S(1)}, s32[]{:S(2)}) async-start(s8[8388608]{0:T(1024)(128)(4,1)} %bitcast.92), calls=%async_computation.5 | async-start | bytes 8388608
  89.2 26.7 %slice-start.1 = ((s8[8388608]{0:T(1024)(128)(4,1)}), s8[4194304]{0:T(1024)(128)(4,1)S(1)}, s32[]{:S(2)}) async-start(s8[8388608]{0:T(1024)(128)(4,1)} %bitcast.92), calls=%async_computation.6 | async-start | bytes 8388608
  89.7 6.1 %collective-permute-start.11 = (f32[8,2,8,128]{3,2,0,1:T(8,128)S(1)}, f32[8,2,8,128]{3,2,0,1:T(8,128)S(1)}, u32[]{:S(2)}, u32[]{:S(2)}) collective-permute-start(f32[8,2,8,128]{3,2,0,1:T(8,128)S(1)} %multiply_add_fusion.1), channel_id=1, source_target_pairs={{0,4},{4,8},{8,12},{12,0},{1,5},{5,9},{9,13},{13,1},{2,6},{6,10},{... | collective-permute-start | bytes 196616 | tf_op jit(solution)/shard_map/ppermute | solution.py:20
  96.2 6.2 %collective-permute-start.12 = (f32[8,2,8,128]{3,2,0,1:T(8,128)S(1)}, f32[8,2,8,128]{3,2,0,1:T(8,128)S(1)}, u32[]{:S(2)}, u32[]{:S(2)}) collective-permute-start(f32[8,2,8,128]{3,2,0,1:T(8,128)S(1)} %multiply_add_fusion), channel_id=1, source_target_pairs={{0,4},{4,8},{8,12},{12,0},{1,5},{5,9},{9,13},{13,1},{2,6},{6,10},{... | collective-permute-start | bytes 196616 | tf_op jit(solution)/shard_map/ppermute | solution.py:20
  96.3 6.2 %collective-permute-start.16 = (f32[8,2,8]{2,0,1:T(8,128)S(1)}, f32[8,2,8]{2,0,1:T(8,128)S(1)}, u32[]{:S(2)}, u32[]{:S(2)}) collective-permute-start(f32[8,2,8]{2,0,1:T(8,128)S(1)} %get-tuple-element.54), channel_id=1, source_target_pairs={{0,4},{4,8},{8,12},{12,0},{1,5},{5,9},{9,13},{13,1},{2,6},{6,10},{... | collective-permute-start | bytes 1544 | tf_op jit(solution)/shard_map/ppermute | solution.py:20
Sparse Core Ops, SparseCore 0:
  45.7 18.7 reduce-scatter.6
  118.3 18.5 reduce-scatter.4
where the time goes:
time: 144 us
  waiting for transfers between devices  84 us (58%)
  starting transfers between devices  15.2 us (11%)
  between operations  14.3 us (10%)
  blocking collectives  13.3 us (9%)
  matrix products  8.47 us (6%)
  local copies, waits for them, and re-layouts  5.37 us (4%)
  other arithmetic  2.99 us (2%)
    ppermute x17, waiting for transfers between devices, passed_along(): lax.ppermute(shard, axis, [(i, (i + by) % peers) for i in range(peers)])  36.9 us
    all_to_all x1, waiting for transfers between devices, on_device(): lax.all_to_all(new_features, 'seq', split_axis=1, concat_axis=0, tiled=True)  22.7 us
    reduce_scatter x1, waiting for transfers between devices, on_device(): lax.psum_scatter(partial_terms.astype(jnp.bfloat16), ('section', 'head'),...  17.3 us
    all_gather x1, blocking collectives, on_device(): lax.all_gather(attended, 'seq', axis=0, tiled=True)  13.3 us
    ppermute x17, starting transfers between devices, passed_along(): lax.ppermute(shard, axis, [(i, (i + by) % peers) for i in range(peers)])  8.83 us
    reduce_scatter x1, waiting for transfers between devices, on_device(): lax.psum_scatter(jnp.dot(spread, stacked_weight, preferred_element_type=j...  6.96 us
    all_to_all x1, starting transfers between devices, on_device(): lax.all_to_all(new_features, 'seq', split_axis=1, concat_axis=0, tiled=True)  6.35 us
  transfers between devices with their start and end apart: 20, of which 13 were waited for; matrix products, arithmetic and copies ran while one was open for 8% of the time, Pallas kernels for 0%

commit v1 on v0

v1 whole, which is shorter than its diff:
```python
import jax
import jax.numpy as jnp
from jax import lax
from jax.sharding import PartitionSpec as P

masked_score = -1e30
norm_epsilon = 1e-05


def shifted(part, axis, by):
    peers = lax.axis_size(axis)
    return lax.ppermute(part, axis, [(i, (i + by) % peers) for i in range(peers)])


def block_at(array, index, axis=0):
    return lax.dynamic_index_in_dim(array, index, axis, keepdims=False)


def gathered(part, axis):
    peers = lax.axis_size(axis)
    return [part] + [shifted(part, axis, by) for by in range(1, peers)]


def summed_rows(partial, axis, dtype):
    peers = lax.axis_size(axis)
    me = lax.axis_index(axis)
    total = block_at(partial, me).astype(jnp.float32)
    for by in range(1, peers):
        piece = block_at(partial, (me + by) % peers).astype(dtype)
        total = total + shifted(piece, axis, by).astype(jnp.float32)
    return total


def split_three(value):
    high = lax.reduce_precision(value, 8, 7)
    rest = value - high
    middle = lax.reduce_precision(rest, 8, 7)
    low = rest - middle
    return [piece.astype(jnp.bfloat16) for piece in (high, middle, low)]


def attend_block(grouped, key_block, value_block, key_position, row_limit, score_scale):
    scores = (
        jnp.einsum("rcgd,kcd->rcgk", grouped, key_block, preferred_element_type=jnp.float32)
        * score_scale
    )
    visible = (key_position[None, :] < row_limit[:, None])[:, None, None, :]
    peak = jnp.max(jnp.where(visible, scores, masked_score), axis=3)
    weights = jnp.where(visible, jnp.exp(scores - peak[..., None]), 0.0)
    total = jnp.sum(weights, axis=3)
    update = jnp.einsum(
        "rcgk,kcd->rcgd",
        weights.astype(jnp.bfloat16),
        value_block,
        preferred_element_type=jnp.float32,
    )
    return update, peak, total


def on_device(
    queries,
    key_cache,
    value_cache,
    new_features,
    key_weight,
    value_weight,
    key_gain,
    out_weight,
    frame_length,
    text_frame,
):
    head_depth = key_cache.shape[2]
    local_kv = key_cache.shape[1]
    kv_width = key_weight.shape[1]
    cached_rows = key_cache.shape[0]
    new_rows = new_features.shape[0]
    text_rows, local_heads, _ = queries.shape
    group_size = local_heads // local_kv
    seq_size = lax.axis_size("seq")
    head_size = lax.axis_size("head")
    seq_index = lax.axis_index("seq")
    head_index = lax.axis_index("head")
    bf16 = jnp.bfloat16
    f32 = jnp.float32

    frame_index = jnp.arange(frame_length.shape[0], dtype=jnp.int32)
    row_limit = jnp.sum(
        jnp.where(frame_index[None, :] <= text_frame[:, None], frame_length[None, :], 0), axis=1
    )

    digits = jnp.stack([row_limit % 256, (row_limit // 256) % 256, row_limit // 65536])
    digits = jnp.pad(digits.astype(bf16), ((0, 0), (0, head_depth - text_rows)))
    query_message = jnp.concatenate(
        (queries.reshape(text_rows * local_heads, head_depth), digits), axis=0
    )

    half_rows = new_rows // head_size
    depth = key_weight.shape[0]
    feature_blocks = new_features.reshape(head_size, half_rows, seq_size, depth)
    my_half = block_at(feature_blocks, head_index)
    sent_features = []
    for by in range(1, seq_size):
        piece = block_at(my_half, (seq_index + by) % seq_size, 1)
        sent_features.append(piece)

    query_messages = gathered(query_message, "seq")
    arrived = [shifted(piece, "seq", by + 1) for by, piece in enumerate(sent_features)]
    stacked_weight = jnp.concatenate((key_weight, value_weight), axis=1)

    own_chunk = block_at(feature_blocks, seq_index, 2)
    own_rows = [block_at(own_chunk, (head_index + by) % head_size) for by in range(head_size)]
    own_rows = jnp.concatenate(own_rows, axis=0)
    raw = jnp.dot(own_rows, stacked_weight, preferred_element_type=f32)
    for by, half in enumerate(arrived):
        whole = jnp.concatenate(
            [half] + [shifted(half, "head", head_size - turn) for turn in range(1, head_size)],
            axis=0,
        )
        term = jnp.dot(whole, stacked_weight, preferred_element_type=f32).astype(bf16)
        raw = raw + shifted(term, "seq", seq_size - (by + 1)).astype(f32)
    raw = raw.reshape(head_size, half_rows, -1)
    raw = jnp.concatenate(
        [block_at(raw, (turn - head_index) % head_size) for turn in range(head_size)], axis=0
    )

    stacked_query = jnp.stack([m[: text_rows * local_heads] for m in query_messages])
    stacked_digit = jnp.stack([m[text_rows * local_heads :, :text_rows] for m in query_messages])
    stacked_digit = stacked_digit.astype(f32)
    limits = stacked_digit[:, 0] + 256.0 * stacked_digit[:, 1] + 65536.0 * stacked_digit[:, 2]
    grouped = stacked_query.reshape(seq_size, text_rows, local_kv, group_size, head_depth)
    score_scale = head_depth ** (-0.5)
    block_keys = cached_rows + new_rows
    key_position = (seq_index * block_keys + jnp.arange(block_keys, dtype=jnp.int32)).astype(f32)

    many = 4
    part_count = seq_size // many if seq_size > many else 1
    part_rows = seq_size // part_count * text_rows
    grouped = grouped.reshape(part_count, part_rows, local_kv, group_size, head_depth)
    limits = limits.reshape(part_count, part_rows)

    def cached_part(operands):
        query_part, limit_part = operands
        return attend_block(
            query_part, key_cache, value_cache, key_position[:cached_rows], limit_part, score_scale
        )

    if part_count == 1:
        cached = cached_part((grouped[0], limits[0]))
    else:
        cached = lax.map(cached_part, (grouped, limits))
    grouped = grouped.reshape(-1, local_kv, group_size, head_depth)
    limits = limits.reshape(-1)
    cached_sum, cached_peak, cached_total = (
        part.reshape(grouped.shape[0], local_kv, group_size, *part.shape[part.ndim - (1 if i == 0 else 0) :])
        for i, part in enumerate(cached)
    )

    key_heads = raw[:, :kv_width].reshape(new_rows, local_kv, head_depth)
    mean_square = jnp.mean(key_heads * key_heads, axis=2, keepdims=True)
    new_keys = (key_heads * lax.rsqrt(mean_square + norm_epsilon) * key_gain).astype(bf16)
    new_values = raw[:, kv_width:].reshape(new_rows, local_kv, head_depth).astype(bf16)
    fresh_sum, fresh_peak, fresh_total = attend_block(
        grouped, new_keys, new_values, key_position[cached_rows:], limits, score_scale
    )
    peak = jnp.maximum(cached_peak, fresh_peak)
    cached_factor = jnp.exp(cached_peak - peak)
    fresh_factor = jnp.exp(fresh_peak - peak)
    total = cached_factor * cached_total + fresh_factor * fresh_total
    summed = cached_factor[..., None] * cached_sum + fresh_factor[..., None] * fresh_sum
    some = total > 0.0
    safe_total = jnp.where(some, total, 1.0)
    mean_value = (summed / safe_total[..., None]).astype(bf16)
    log_total = jnp.where(some, peak + jnp.log(safe_total), masked_score)

    mean_value = mean_value.reshape(seq_size, text_rows * local_heads, head_depth)
    log_total = log_total.reshape(seq_size, text_rows * local_heads)
    log_count = text_rows * local_heads
    log_rows = -(-log_count // head_depth)
    log_pieces = jnp.stack(split_three(log_total), axis=1)
    log_pieces = jnp.pad(log_pieces, ((0, 0), (0, 0), (0, log_rows * head_depth - log_count)))
    log_pieces = log_pieces.reshape(seq_size, 3 * log_rows, head_depth)
    message = jnp.concatenate((mean_value, log_pieces), axis=1)
    returned = [message[0]] + [
        shifted(message[by], "seq", seq_size - by) for by in range(1, seq_size)
    ]
    returned = jnp.stack(returned)
    means = returned[:, : text_rows * local_heads].astype(f32)
    logs = returned[:, text_rows * local_heads :].astype(f32)
    logs = jnp.sum(logs.reshape(seq_size, 3, -1), axis=1)[:, :log_count]
    top = jnp.max(logs, axis=0)
    share = jnp.exp(logs - top[None])
    merged = jnp.sum(share[..., None] * means, axis=0) / jnp.sum(share, axis=0)[:, None]
    attended = merged.astype(bf16).reshape(text_rows, local_heads * head_depth)

    every = jnp.stack(gathered(attended, "seq"))
    order = (seq_index - jnp.arange(seq_size)) % seq_size
    every = jnp.concatenate([block_at(every, order[i]) for i in range(seq_size)], axis=0)
    partial = jnp.dot(every, out_weight, preferred_element_type=f32)

    section_size = lax.axis_size("section")
    out_rows = partial.shape[0] // (section_size * head_size)
    partial = partial.reshape(section_size, head_size, out_rows, -1)
    partial = summed_rows(jnp.swapaxes(partial, 0, 1), "head", bf16)
    layer_output = summed_rows(partial, "section", bf16).astype(bf16)
    return (layer_output, new_keys, new_values)


def solution(mesh):
    placed = (
        P(("groups", "seq"), ("section", "head"), None),
        P(("groups", "seq"), ("section", "head"), None),
        P(("groups", "seq"), ("section", "head"), None),
        P(("groups", "seq"), None),
        P("seq", ("section", "head")),
        P("seq", ("section", "head")),
        P(),
        P(("section", "head"), "seq"),
        P("groups"),
        P(("groups", "seq")),
    )
    return jax.shard_map(
        on_device,
        mesh=mesh,
        in_specs=placed,
        out_specs=(
            P(("groups", "section", "head"), "seq"),
            P(("groups", "seq"), ("section", "head"), None),
            P(("groups", "seq"), ("section", "head"), None),
        ),
        check_vma=False,
    )
```

time: 144 us -> 84.3 us (0.59)
  waiting for transfers between devices: 84 us -> 11.9 us
  blocking collectives: 13.3 us -> 0 us
  starting transfers between devices: 15.2 us -> 24.1 us
  local copies, waits for them, and re-layouts: 5.37 us -> 14 us
  matrix products: 8.47 us -> 16.6 us
  between operations: 14.3 us -> 9.03 us
  other arithmetic: 2.99 us -> 7.97 us
    ppermute x17 -> x20, waiting for transfers between devices: 36.9 us -> 11.9 us  [shifted(): lax.ppermute(part, axis, [(i, (i + by) % peers) for i in range(peers)])]
    reduce_scatter x2 -> x0, waiting for transfers between devices: 24.3 us -> none  [the longest x1 17.3 us: on_device(): lax.psum_scatter(partial_terms.astype(jnp.bfloat16), ('section', 'head'),...]
    all_to_all x1 -> x0, waiting for transfers between devices: 22.7 us -> none  [on_device(): lax.all_to_all(new_features, 'seq', split_axis=1, concat_axis=0, tiled=True)]
    ppermute x17 -> x20, starting transfers between devices: 8.83 us -> 24.1 us  [shifted(): lax.ppermute(part, axis, [(i, (i + by) % peers) for i in range(peers)])]
    all_gather x1 -> x0, blocking collectives: 13.3 us -> none  [on_device(): lax.all_gather(attended, 'seq', axis=0, tiled=True)]
    dot_general x10 -> x9, matrix products: 8.47 us -> 16.6 us  [the longest x3 6.03 us: on_device(): jnp.dot(whole, stacked_weight, preferred_element_type=f32).astype(bf16)]
    all_to_all x1 -> x0, starting transfers between devices: 6.35 us -> none  [on_device(): lax.all_to_all(new_features, 'seq', split_axis=1, concat_axis=0, tiled=True)]
    unnamed x22 -> x19, local copies, waits for them, and re-layouts: 2.13 us -> 4.7 us
  transfers between devices with their start and end apart: 20 -> 20, of which waited for: 13 -> 7; matrix products, arithmetic and copies ran while one was open for 8% -> 29% of each run, Pallas kernels for 0% -> 0%
where the time goes in v1:
time: 84.3 us; the launch traced here: 83.6 us
  starting transfers between devices  24.1 us (29%)
  matrix products  16.6 us (20%)
  local copies, waits for them, and re-layouts  14 us (17%)
  waiting for transfers between devices  11.9 us (14%)
  between operations  9.03 us (11%)
  other arithmetic  7.97 us (9%)
    ppermute x20, starting transfers between devices, shifted(): lax.ppermute(part, axis, [(i, (i + by) % peers) for i in range(peers)])  24.1 us
    ppermute x20, waiting for transfers between devices, shifted(): lax.ppermute(part, axis, [(i, (i + by) % peers) for i in range(peers)])  11.9 us
    dot_general x3, matrix products, on_device(): jnp.dot(whole, stacked_weight, preferred_element_type=f32).astype(bf16)  6.03 us
    dot_general x1, matrix products, on_device(): partial = jnp.dot(every, out_weight, preferred_element_type=f32)  4.92 us
    unnamed x19, local copies, waits for them, and re-layouts  4.7 us
    dot_general x2, matrix products, attend_block(): jnp.einsum('rcgk,kcd->rcgd', weights.astype(jnp.bfloat16), value_block, p...  3.68 us
    dynamic_slice x1, local copies, waits for them, and re-layouts, block_at(): return lax.dynamic_index_in_dim(array, index, axis, keepdims=False)  2.28 us
    reshape x1, local copies, waits for them, and re-layouts, on_device(): feature_blocks = new_features.reshape(head_size, half_rows, seq_size, depth)  1.84 us
  transfers between devices with their start and end apart: 20, of which 7 were waited for; matrix products, arithmetic and copies ran while one was open for 29% of the time, Pallas kernels for 0%

profile of v1, /device:TPU:0, one launch (start us, length us, event | category | flops | bytes accessed | tf_op | source)
XLA Modules:
  0.0 83.6 jit_solution(17002433582091525641)
XLA Ops:
  0.6 0.9 %select_reduce_fusion.1 = s32[8]{0:T(128)S(1)} fusion(s32[64]{0:T(128)} %param.18, s32[8]{0:T(128)} %param.19), kind=kLoop, calls=%fused_computation.110 | loop fusion | flops 1528 | bytes 320 | tf_op jit(solution)/shard_map/reduce_sum | solution.py:87
  1.6 0.5 fusion.88
  2.1 0.8 pad_maximum_fusion.7
  2.9 5.1 %collective-permute-start.2 = (bf16[131,128]{1,0:T(8,128)(2,1)S(1)}, bf16[131,128]{1,0:T(8,128)(2,1)S(1)}, u32[]{:S(2)}, u32[]{:S(2)}) collective-permute-start(bf16[131,128]{1,0:T(8,128)(2,1)S(1)} %pad_maximum_fusion.7), channel_id=1, source_target_pairs={{0,12},{4,0},{8,4},{12,8},{1,13},{5,1},{9,5},{13,9},{2,14},{6,2},{... | collective-permute-start | bytes 100616 | tf_op jit(solution)/shard_map/ppermute | solution.py:12
  8.0 1.0 %collective-permute-start = (bf16[131,128]{1,0:T(8,128)(2,1)S(1)}, bf16[131,128]{1,0:T(8,128)(2,1)}, u32[]{:S(2)}, u32[]{:S(2)}) collective-permute-start(bf16[131,128]{1,0:T(8,128)(2,1)S(1)} %pad_maximum_fusion.7), channel_id=1, source_target_pairs={{0,4},{4,8},{8,12},{12,0},{1,5},{5,9},{9,13},{13,1},{2,6},{6,10},{... | collective-permute-start | bytes 100616 | tf_op jit(solution)/shard_map/ppermute | solution.py:12
  9.0 1.8 %reshape.530 = bf16[2,32,4,2048]{3,2,1,0:T(4,128)(2,1)S(1)} reshape(bf16[64,8192]{1,0:T(8,128)(2,1)} %param.13) | data formatting | bytes 2097152 | tf_op jit(solution)/shard_map/reshape | solution.py:99
  10.9 2.3 %constant_dynamic-slice_fusion.2 = (bf16[1,32,1,2048]{3,2,1,0:T(2,128)(2,1)}, bf16[1,32,1,2048]{3,2,1,0:T(2,128)(2,1)S(1)}, bf16[1,32,1,2048]{3,2,1,0:T(2,128)(2...) fusion(bf16[2,32,4,2048]{3,2,1,0:T(4,128)(2,1)S(1)} %reshape.530, s32[]{:T(128)S(6)} %select_n.260, ...), kind=kLoop, calls=%fused_computation.114 | loop fusion | bytes 1310748 | tf_op jit(solution)/shard_map/jit(dynamic_index_in_dim)/dynamic_slice | solution.py:16
  13.2 0.8 copy.199
  13.9 2.8 %collective-permute-start.9 = (bf16[32,2048]{1,0:T(8,128)(2,1)}, bf16[32,2048]{1,0:T(8,128)(2,1)}, u32[]{:S(2)}, u32[]{:S(2)}) collective-permute-start(bf16[32,2048]{1,0:T(8,128)(2,1)} %bitcast.154), channel_id=1, source_target_pairs={{0,12},{4,0},{8,4},{12,8},{1,13},{5,1},{9,5},{13,9},{2,14},{6,2},{... | collective-permute-start | bytes 393224 | tf_op jit(solution)/shard_map/ppermute | solution.py:12
  16.7 0.7 copy.200
  17.5 1.1 %collective-permute-start.6 = (bf16[32,2048]{1,0:T(8,128)(2,1)}, bf16[32,2048]{1,0:T(8,128)(2,1)}, u32[]{:S(2)}, u32[]{:S(2)}) collective-permute-start(bf16[32,2048]{1,0:T(8,128)(2,1)} %bitcast.155), channel_id=1, source_target_pairs={{0,8},{4,12},{8,0},{12,4},{1,9},{5,13},{9,1},{13,5},{2,10},{6,14},... | collective-permute-start | bytes 393224 | tf_op jit(solution)/shard_map/ppermute | solution.py:12
  18.6 1.3 %constant_dynamic-update-slice_fusion.1 = bf16[2048,512]{1,0:T(8,128)(2,1)S(1)} fusion(bf16[2048,256]{1,0:T(8,128)(2,1)} %param.14), kind=kLoop, calls=%fused_computation.109 | loop fusion | bytes 2097152
  20.0 1.3 %constant_dynamic-update-slice_fusion = bf16[2048,512]{1,0:T(8,128)(2,1)S(1)} fusion(bf16[2048,512]{1,0:T(8,128)(2,1)S(1)} %constant_dynamic-update-slice_fusion.1, bf16[2048,256]{1,0:T(8,128)(2,1)} %param.15), kind=kLoop, calls=%fused_computation.108 | loop fusion | bytes 2097152 | tf_op jit(solution)/shard_map/concatenate | solution.py:108
  21.4 0.5 fusion.22
  22.0 0.6 slice.101
  22.5 1.7 %copy.201 = bf16[1,32,1,2048]{3,1,2,0:T(8,128)(2,1)} copy(bf16[1,32,1,2048]{3,2,1,0:T(2,128)(2,1)} %get-tuple-element.13) | data formatting | bytes 262144
  24.3 0.7 slice_bitcast_fusion.8
  24.9 0.8 fusion.71
  25.9 0.8 slice_bitcast_fusion.5
  26.7 1.2 %fusion = (f32[32,2,8]{2,0,1:T(8,128)S(1)}, f32[2,32,8,1984]{3,2,1,0:T(8,128)S(1)}) fusion(pred[32,1984]{1,0:T(8,128)(4,1)S(1)} %broadcast_compare_fusion, bf16[1984,2,128,1]{2,1,0,3:T(2,128)(2,1)S(1)} %bitcast.158, bf16[32,2,8,128]{3,2,1,0:T(8,128)(2,1)S(1)} %bitcast.161), kind=kOutput, calls=%fused_computation.2 | convolution fusion | flops 263093760 | bytes 5275648 | tf_op jit(solution)/shard_map/rcgd,kcd->rcgk/dot_general | solution.py:44
  28.1 1.4 %fusion.3 = f32[32,2,8]{2,0,1:T(8,128)S(1)} fusion(f32[2,32,8,1984]{3,2,1,0:T(8,128)S(1)} %get-tuple-element.45, f32[32,2,8]{2,0,1:T(8,128)S(1)} %get-tuple-element.44, pred[32,1984]{1,0:T(8,128)(4,1)S(1)} %broadcast_compare_fusion), kind=kLoop, calls=%fused_computation.5 | loop fusion | flops 4062720 | bytes 4130816 | tf_op jit(solution)/shard_map/reduce_sum | solution.py:50
  29.5 0.6 collective-permute-start.7
  30.1 1.3 %collective-permute-done.3 = bf16[32,2048]{1,0:T(8,128)(2,1)} collective-permute-done((bf16[32,2048]{1,0:T(8,128)(2,1)}, bf16[32,2048]{1,0:T(8,128)(2,1)}, u32[]{:S(2)}, u32[]{:S(2)}) %collective-permute-start.3) | collective-permute-done | bytes 131104 | tf_op jit(solution)/shard_map/ppermute | solution.py:12
  31.3 2.0 %convolution_convert_fusion = bf16[64,512]{1,0:T(8,128)(2,1)} fusion(bf16[2048,512]{1,0:T(8,128)(2,1)S(1)} %constant_dynamic-update-slice_fusion, bf16[32,2048]{1,0:T(8,128)(2,1)S(1)} %collective-permute-done.10, bf16[32,2048]{1,0:T(8,128)(2,1)} %collective-permute-done.9), kind=kOutput, calls=%fused_computation.18 | convolution fusion | flops 134774784 | bytes 2424832 | tf_op jit(solution)/shard_map/dot_general | solution.py:119
  33.3 1.2 %collective-permute-start.11 = (bf16[64,512]{1,0:T(8,128)(2,1)}, bf16[64,512]{1,0:T(8,128)(2,1)}, u32[]{:S(2)}, u32[]{:S(2)}) collective-permute-start(bf16[64,512]{1,0:T(8,128)(2,1)} %convolution_convert_fusion), channel_id=1, source_target_pairs={{0,4},{4,8},{8,12},{12,0},{1,5},{5,9},{9,13},{13,1},{2,6},{6,10},{... | collective-permute-start | bytes 196616 | tf_op jit(solution)/shard_map/ppermute | solution.py:12
  34.5 2.0 %convolution_convert_fusion.1 = bf16[64,512]{1,0:T(8,128)(2,1)} fusion(bf16[2048,512]{1,0:T(8,128)(2,1)S(1)} %constant_dynamic-update-slice_fusion, bf16[32,2048]{1,0:T(8,128)(2,1)S(1)} %collective-permute-done.7, bf16[32,2048]{1,0:T(8,128)(2,1)} %collective-permute-done.6), kind=kOutput, calls=%fused_computation.19 | convolution fusion | flops 134774784 | bytes 2424832 | tf_op jit(solution)/shard_map/dot_general | solution.py:119
  36.5 2.0 %collective-permute-start.8 = (bf16[64,512]{1,0:T(8,128)(2,1)}, bf16[64,512]{1,0:T(8,128)(2,1)}, u32[]{:S(2)}, u32[]{:S(2)}) collective-permute-start(bf16[64,512]{1,0:T(8,128)(2,1)} %convolution_convert_fusion.1), channel_id=1, source_target_pairs={{0,8},{4,12},{8,0},{12,4},{1,9},{5,13},{9,1},{13,5},{2,10},{6,14},... | collective-permute-start | bytes 196616 | tf_op jit(solution)/shard_map/ppermute | solution.py:12
  38.6 2.0 %convolution_convert_fusion.2 = bf16[64,512]{1,0:T(8,128)(2,1)} fusion(bf16[2048,512]{1,0:T(8,128)(2,1)S(1)} %constant_dynamic-update-slice_fusion, bf16[32,2048]{1,0:T(8,128)(2,1)S(1)} %collective-permute-done.4, bf16[32,2048]{1,0:T(8,128)(2,1)} %collective-permute-done.3), kind=kOutput, calls=%fused_computation.20 | convolution fusion | flops 134774784 | bytes 2424832 | tf_op jit(solution)/shard_map/dot_general | solution.py:119
  40.5 0.6 collective-permute-start.5
  41.5 1.7 %collective-permute-done.8 = bf16[64,512]{1,0:T(8,128)(2,1)} collective-permute-done((bf16[64,512]{1,0:T(8,128)(2,1)}, bf16[64,512]{1,0:T(8,128)(2,1)}, u32[]{:S(2)}, u32[]{:S(2)}) %collective-permute-start.8) | collective-permute-done | bytes 65568 | tf_op jit(solution)/shard_map/ppermute | solution.py:12
  43.3 1.7 %collective-permute-done.5 = bf16[64,512]{1,0:T(8,128)(2,1)S(1)} collective-permute-done((bf16[64,512]{1,0:T(8,128)(2,1)}, bf16[64,512]{1,0:T(8,128)(2,1)S(1)}, u32[]{:S(2)}, u32[]{:S(2)}) %collective-permute-start.5) | collective-permute-done | bytes 65568 | tf_op jit(solution)/shard_map/ppermute | solution.py:12
  45.0 0.9 %convert_add_fusion = f32[64,512]{1,0:T(8,128)S(1)} fusion(bf16[64,512]{1,0:T(8,128)(2,1)} %collective-permute-done.11, bf16[64,512]{1,0:T(8,128)(2,1)} %collective-permute-done.8, f32[64,512]{1,0:T(8,128)S(1)} %fusion.22, bf16[64,512]{1,0:T(8,128)(2,1)S(1)} %collective-permute-done.5), kind=kLoop, calls=%fused_computation.68 | loop fusion | flops 196608 | bytes 458752 | tf_op jit(solution)/shard_map/add | solution.py:120
  47.6 3.5 %fusion.15 = f32[32,2,8,128]{3,2,0,1:T(8,128)S(1)} fusion(f32[2,32,8,1984]{3,2,1,0:T(8,128)} %copy-done.1, f32[32,2,8]{2,0,1:T(8,128)S(1)} %get-tuple-element.44, pred[32,1984]{1,0:T(8,128)(4,1)S(1)} %broadcast_compare_fusion, bf16[1984,2,128,1]{2,1,0,3:T(2,128)(2,1)} %bitcast.178, f32[32,2,8]{2,0,1:T(8,128)S(1)} %get-tuple-element.10), kind=kOutput, calls=%fused_computation.16 | convolution fusion | flops 264175616 | bytes 5408768 | tf_op jit(solution)/shard_map/rcgk,kcd->rcgd/dot_general | solution.py:51
  51.4 1.2 %collective-permute-start.14 = (bf16[131,128]{1,0:T(8,128)(2,1)S(1)}, bf16[131,128]{1,0:T(8,128)(2,1)S(1)}, u32[]{:S(2)}, u32[]{:S(2)}) collective-permute-start(bf16[131,128]{1,0:T(8,128)(2,1)S(1)} %get-tuple-element.21), channel_id=1, source_target_pairs={{0,4},{4,8},{8,12},{12,0},{1,5},{5,9},{9,13},{13,1},{2,6},{6,10},{... | collective-permute-start | bytes 100616 | tf_op jit(solution)/shard_map/ppermute | solution.py:12
  52.6 1.8 %collective-permute-start.13 = (bf16[131,128]{1,0:T(8,128)(2,1)S(1)}, bf16[131,128]{1,0:T(8,128)(2,1)S(1)}, u32[]{:S(2)}, u32[]{:S(2)}) collective-permute-start(bf16[131,128]{1,0:T(8,128)(2,1)S(1)} %get-tuple-element.22), channel_id=1, source_target_pairs={{0,8},{4,12},{8,0},{12,4},{1,9},{5,13},{9,1},{13,5},{2,10},{6,14},... | collective-permute-start | bytes 100616 | tf_op jit(solution)/shard_map/ppermute | solution.py:12
  54.4 0.8 collective-permute-start.12
  55.3 0.7 fusion.93
  64.3 1.8 %collective-permute-start.17 = (bf16[8,2048]{1,0:T(8,128)(2,1)S(1)}, bf16[8,2048]{1,0:T(8,128)(2,1)S(1)}, u32[]{:S(2)}, u32[]{:S(2)}) collective-permute-start(bf16[8,2048]{1,0:T(8,128)(2,1)S(1)} %fusion.52), channel_id=1, source_target_pairs={{0,12},{4,0},{8,4},{12,8},{1,13},{5,1},{9,5},{13,9},{2,14},{6,2},{... | collective-permute-start | bytes 98312 | tf_op jit(solution)/shard_map/ppermute | solution.py:12
  66.1 0.9 %collective-permute-start.16 = (bf16[8,2048]{1,0:T(8,128)(2,1)S(1)}, bf16[8,2048]{1,0:T(8,128)(2,1)S(1)}, u32[]{:S(2)}, u32[]{:S(2)}) collective-permute-start(bf16[8,2048]{1,0:T(8,128)(2,1)S(1)} %fusion.52), channel_id=1, source_target_pairs={{0,8},{4,12},{8,0},{12,4},{1,9},{5,13},{9,1},{13,5},{2,10},{6,14},... | collective-permute-start | bytes 98312 | tf_op jit(solution)/shard_map/ppermute | solution.py:12
  67.0 1.4 %collective-permute-start.15 = (bf16[8,2048]{1,0:T(8,128)(2,1)S(1)}, bf16[8,2048]{1,0:T(8,128)(2,1)S(1)}, u32[]{:S(2)}, u32[]{:S(2)}) collective-permute-start(bf16[8,2048]{1,0:T(8,128)(2,1)S(1)} %fusion.52), channel_id=1, source_target_pairs={{0,4},{4,8},{8,12},{12,0},{1,5},{5,9},{9,13},{13,1},{2,6},{6,10},{... | collective-permute-start | bytes 98312 | tf_op jit(solution)/shard_map/ppermute | solution.py:12
  68.5 2.5 %collective-permute-done.16 = bf16[8,2048]{1,0:T(8,128)(2,1)S(1)} collective-permute-done((bf16[8,2048]{1,0:T(8,128)(2,1)S(1)}, bf16[8,2048]{1,0:T(8,128)(2,1)S(1)}, u32[]{:S(2)}, u32[]{:S(2)}) %collective-permute-start.16) | collective-permute-done | bytes 32800 | tf_op jit(solution)/shard_map/ppermute | solution.py:12
  70.9 1.7 %collective-permute-done.15 = bf16[8,2048]{1,0:T(8,128)(2,1)S(1)} collective-permute-done((bf16[8,2048]{1,0:T(8,128)(2,1)S(1)}, bf16[8,2048]{1,0:T(8,128)(2,1)S(1)}, u32[]{:S(2)}, u32[]{:S(2)}) %collective-permute-start.15) | collective-permute-done | bytes 32800 | tf_op jit(solution)/shard_map/ppermute | solution.py:12
  72.7 4.9 %fusion.37 = f32[32,2048]{1,0:T(8,128)S(1)} fusion(bf16[2048,2048]{1,0:T(8,128)(2,1)} %param.17, bf16[8,2048]{1,0:T(8,128)(2,1)S(1)} %get-tuple-element.25, bf16[8,2048]{1,0:T(8,128)(2,1)S(1)} %get-tuple-element.26, bf16[8,2048]{1,0:T(8,128)(2,1)S(1)} %get-tuple-element.27, bf16[8,2048]{1,0:T(8,128)(2,1)S(1)} %get-tuple-element.24), kind=kOutput, calls=%fused_computation.50 | convolution fusion | flops 268959744 | bytes 8781824 | tf_op jit(solution)/shard_map/dot_general | solution.py:198
  77.8 1.2 %collective-permute-done.18 = bf16[2,8,2048]{2,1,0:T(8,128)(2,1)S(1)} collective-permute-done((bf16[2,8,2048]{2,1,0:T(8,128)(2,1)S(1)}, bf16[2,8,2048]{2,1,0:T(8,128)(2,1)S(1)}, u32[]{:S(2)}, u32[]{:S(2)}) %collective-permute-start.18) | collective-permute-done | bytes 65568 | tf_op jit(solution)/shard_map/ppermute | solution.py:12
  79.0 1.6 %collective-permute-start.19 = (bf16[8,2048]{1,0:T(8,128)(2,1)S(1)}, bf16[8,2048]{1,0:T(8,128)(2,1)S(1)}, u32[]{:S(2)}, u32[]{:S(2)}) collective-permute-start(bf16[8,2048]{1,0:T(8,128)(2,1)S(1)} %fusion.56), channel_id=1, source_target_pairs={{0,2},{2,0},{1,3},{3,1},{4,6},{6,4},{5,7},{7,5},{8,10},{10,8},{9,1... | collective-permute-start | bytes 98312 | tf_op jit(solution)/shard_map/ppermute | solution.py:12
  80.6 0.8 multiply_convert_fusion
  81.3 1.7 %collective-permute-done.19 = bf16[8,2048]{1,0:T(8,128)(2,1)S(1)} collective-permute-done((bf16[8,2048]{1,0:T(8,128)(2,1)S(1)}, bf16[8,2048]{1,0:T(8,128)(2,1)S(1)}, u32[]{:S(2)}, u32[]{:S(2)}) %collective-permute-start.19) | collective-permute-done | bytes 32800 | tf_op jit(solution)/shard_map/ppermute | solution.py:12
  83.0 0.6 fusion.51
  (89 shorter events, 3.4 us)
Async XLA Ops:
  0.6 26.1 %copy-start = (bf16[1984,2,128]{2,1,0:T(2,128)(2,1)S(1)}, bf16[1984,2,128]{2,1,0:T(2,128)(2,1)}, u32[]{:S(2)}) copy-start(bf16[1984,2,128]{2,1,0:T(2,128)(2,1)} %param.11) | copy-start | bytes 3047428
  2.9 21.3 %collective-permute-start.2 = (bf16[131,128]{1,0:T(8,128)(2,1)S(1)}, bf16[131,128]{1,0:T(8,128)(2,1)S(1)}, u32[]{:S(2)}, u32[]{:S(2)}) collective-permute-start(bf16[131,128]{1,0:T(8,128)(2,1)S(1)} %pad_maximum_fusion.7), channel_id=1, source_target_pairs={{0,12},{4,0},{8,4},{12,8},{1,13},{5,1},{9,5},{13,9},{2,14},{6,2},{... | collective-permute-start | bytes 100616 | tf_op jit(solution)/shard_map/ppermute | solution.py:12
  8.0 16.3 %collective-permute-start.1 = (bf16[131,128]{1,0:T(8,128)(2,1)S(1)}, bf16[131,128]{1,0:T(8,128)(2,1)S(1)}, u32[]{:S(2)}, u32[]{:S(2)}) collective-permute-start(bf16[131,128]{1,0:T(8,128)(2,1)S(1)} %pad_maximum_fusion.7), channel_id=1, source_target_pairs={{0,8},{4,12},{8,0},{12,4},{1,9},{5,13},{9,1},{13,5},{2,10},{6,14},... | collective-permute-start | bytes 100616 | tf_op jit(solution)/shard_map/ppermute | solution.py:12
  8.0 16.3 %collective-permute-start = (bf16[131,128]{1,0:T(8,128)(2,1)S(1)}, bf16[131,128]{1,0:T(8,128)(2,1)}, u32[]{:S(2)}, u32[]{:S(2)}) collective-permute-start(bf16[131,128]{1,0:T(8,128)(2,1)S(1)} %pad_maximum_fusion.7), channel_id=1, source_target_pairs={{0,4},{4,8},{8,12},{12,0},{1,5},{5,9},{9,13},{13,1},{2,6},{6,10},{... | collective-permute-start | bytes 100616 | tf_op jit(solution)/shard_map/ppermute | solution.py:12
  13.9 14.1 %collective-permute-start.9 = (bf16[32,2048]{1,0:T(8,128)(2,1)}, bf16[32,2048]{1,0:T(8,128)(2,1)}, u32[]{:S(2)}, u32[]{:S(2)}) collective-permute-start(bf16[32,2048]{1,0:T(8,128)(2,1)} %bitcast.154), channel_id=1, source_target_pairs={{0,12},{4,0},{8,4},{12,8},{1,13},{5,1},{9,5},{13,9},{2,14},{6,2},{... | collective-permute-start | bytes 393224 | tf_op jit(solution)/shard_map/ppermute | solution.py:12
  17.5 9.2 %copy-start.3 = (bf16[8,16,128]{2,1,0:T(8,128)(2,1)S(1)}, bf16[8,16,128]{2,1,0:T(8,128)(2,1)}, u32[]{:S(2)}) copy-start(bf16[8,16,128]{2,1,0:T(8,128)(2,1)} %param.10) | copy-start | bytes 98308
  17.5 12.0 %collective-permute-start.6 = (bf16[32,2048]{1,0:T(8,128)(2,1)}, bf16[32,2048]{1,0:T(8,128)(2,1)}, u32[]{:S(2)}, u32[]{:S(2)}) collective-permute-start(bf16[32,2048]{1,0:T(8,128)(2,1)} %bitcast.155), channel_id=1, source_target_pairs={{0,8},{4,12},{8,0},{12,4},{1,9},{5,13},{9,1},{13,5},{2,10},{6,14},... | collective-permute-start | bytes 393224 | tf_op jit(solution)/shard_map/ppermute | solution.py:12
  18.6 2.7 %copy-start.2 = (bf16[1,32,1,2048]{3,2,1,0:T(2,128)(2,1)S(1)}, bf16[1,32,1,2048]{3,2,1,0:T(2,128)(2,1)}, u32[]{:S(2)}) copy-start(bf16[1,32,1,2048]{3,2,1,0:T(2,128)(2,1)} %get-tuple-element.17) | copy-start | bytes 393220
  24.2 7.1 %collective-permute-start.3 = (bf16[32,2048]{1,0:T(8,128)(2,1)}, bf16[32,2048]{1,0:T(8,128)(2,1)}, u32[]{:S(2)}, u32[]{:S(2)}) collective-permute-start(bf16[32,2048]{1,0:T(8,128)(2,1)} %bitcast.156), channel_id=1, source_target_pairs={{0,4},{4,8},{8,12},{12,0},{1,5},{5,9},{9,13},{13,1},{2,6},{6,10},{... | collective-permute-start | bytes 393224 | tf_op jit(solution)/shard_map/ppermute | solution.py:12
  28.0 8.5 %copy-start.1 = (f32[2,32,8,1984]{3,2,1,0:T(8,128)}, f32[2,32,8,1984]{3,2,1,0:T(8,128)S(1)}, u32[]{:S(2)}) copy-start(f32[2,32,8,1984]{3,2,1,0:T(8,128)S(1)} %get-tuple-element.45) | copy-start | bytes 12189700
  28.0 3.3 %collective-permute-start.10 = (bf16[32,2048]{1,0:T(8,128)(2,1)}, bf16[32,2048]{1,0:T(8,128)(2,1)S(1)}, u32[]{:S(2)}, u32[]{:S(2)}) collective-permute-start(bf16[32,2048]{1,0:T(8,128)(2,1)} %collective-permute-done.9), channel_id=1, source_target_pairs={{0,1},{1,0},{2,3},{3,2},{4,5},{5,4},{6,7},{7,6},{8,9},{9,8},{10,11... | collective-permute-start | bytes 393224 | tf_op jit(solution)/shard_map/ppermute | solution.py:12
  29.5 11.7 %copy-start.6 = (f32[64]{0:T(128)S(1)}, f32[64]{0:T(128)}, u32[]{:S(2)}) copy-start(f32[64]{0:T(128)} %slice.101) | copy-start | bytes 772
  29.5 16.7 %copy-start.5 = (f32[128]{0:T(128)S(1)}, f32[128]{0:T(128)}, u32[]{:S(2)}) copy-start(f32[128]{0:T(128)} %param.16) | copy-start | bytes 1540
  29.5 5.0 %collective-permute-start.7 = (bf16[32,2048]{1,0:T(8,128)(2,1)}, bf16[32,2048]{1,0:T(8,128)(2,1)S(1)}, u32[]{:S(2)}, u32[]{:S(2)}) collective-permute-start(bf16[32,2048]{1,0:T(8,128)(2,1)} %collective-permute-done.6), channel_id=1, source_target_pairs={{0,1},{1,0},{2,3},{3,2},{4,5},{5,4},{6,7},{7,6},{8,9},{9,8},{10,11... | collective-permute-start | bytes 393224 | tf_op jit(solution)/shard_map/ppermute | solution.py:12
  31.3 7.2 %collective-permute-start.4 = (bf16[32,2048]{1,0:T(8,128)(2,1)}, bf16[32,2048]{1,0:T(8,128)(2,1)S(1)}, u32[]{:S(2)}, u32[]{:S(2)}) collective-permute-start(bf16[32,2048]{1,0:T(8,128)(2,1)} %collective-permute-done.3), channel_id=1, source_target_pairs={{0,1},{1,0},{2,3},{3,2},{4,5},{5,4},{6,7},{7,6},{8,9},{9,8},{10,11... | collective-permute-start | bytes 393224 | tf_op jit(solution)/shard_map/ppermute | solution.py:12
  33.3 8.2 %collective-permute-start.11 = (bf16[64,512]{1,0:T(8,128)(2,1)}, bf16[64,512]{1,0:T(8,128)(2,1)}, u32[]{:S(2)}, u32[]{:S(2)}) collective-permute-start(bf16[64,512]{1,0:T(8,128)(2,1)} %convolution_convert_fusion), channel_id=1, source_target_pairs={{0,4},{4,8},{8,12},{12,0},{1,5},{5,9},{9,13},{13,1},{2,6},{6,10},{... | collective-permute-start | bytes 196616 | tf_op jit(solution)/shard_map/ppermute | solution.py:12
  36.5 6.8 %collective-permute-start.8 = (bf16[64,512]{1,0:T(8,128)(2,1)}, bf16[64,512]{1,0:T(8,128)(2,1)}, u32[]{:S(2)}, u32[]{:S(2)}) collective-permute-start(bf16[64,512]{1,0:T(8,128)(2,1)} %convolution_convert_fusion.1), channel_id=1, source_target_pairs={{0,8},{4,12},{8,0},{12,4},{1,9},{5,13},{9,1},{13,5},{2,10},{6,14},... | collective-permute-start | bytes 196616 | tf_op jit(solution)/shard_map/ppermute | solution.py:12
  40.5 4.5 %collective-permute-start.5 = (bf16[64,512]{1,0:T(8,128)(2,1)}, bf16[64,512]{1,0:T(8,128)(2,1)S(1)}, u32[]{:S(2)}, u32[]{:S(2)}) collective-permute-start(bf16[64,512]{1,0:T(8,128)(2,1)} %convolution_convert_fusion.2), channel_id=1, source_target_pairs={{0,12},{4,0},{8,4},{12,8},{1,13},{5,1},{9,5},{13,9},{2,14},{6,2},{... | collective-permute-start | bytes 196616 | tf_op jit(solution)/shard_map/ppermute | solution.py:12
  47.6 3.7 %copy-start.4 = (bf16[64,2,128]{2,1,0:T(2,128)(2,1)}, bf16[64,2,128]{2,1,0:T(2,128)(2,1)S(1)}, u32[]{:S(2)}) copy-start(bf16[64,2,128]{2,1,0:T(2,128)(2,1)S(1)} %convert_element_type.130) | copy-start | bytes 98308
  51.4 12.3 %collective-permute-start.14 = (bf16[131,128]{1,0:T(8,128)(2,1)S(1)}, bf16[131,128]{1,0:T(8,128)(2,1)S(1)}, u32[]{:S(2)}, u32[]{:S(2)}) collective-permute-start(bf16[131,128]{1,0:T(8,128)(2,1)S(1)} %get-tuple-element.21), channel_id=1, source_target_pairs={{0,4},{4,8},{8,12},{12,0},{1,5},{5,9},{9,13},{13,1},{2,6},{6,10},{... | collective-permute-start | bytes 100616 | tf_op jit(solution)/shard_map/ppermute | solution.py:12
  52.6 11.1 %collective-permute-start.13 = (bf16[131,128]{1,0:T(8,128)(2,1)S(1)}, bf16[131,128]{1,0:T(8,128)(2,1)S(1)}, u32[]{:S(2)}, u32[]{:S(2)}) collective-permute-start(bf16[131,128]{1,0:T(8,128)(2,1)S(1)} %get-tuple-element.22), channel_id=1, source_target_pairs={{0,8},{4,12},{8,0},{12,4},{1,9},{5,13},{9,1},{13,5},{2,10},{6,14},... | collective-permute-start | bytes 100616 | tf_op jit(solution)/shard_map/ppermute | solution.py:12
  54.4 9.3 %collective-permute-start.12 = (bf16[131,128]{1,0:T(8,128)(2,1)S(1)}, bf16[131,128]{1,0:T(8,128)(2,1)S(1)}, u32[]{:S(2)}, u32[]{:S(2)}) collective-permute-start(bf16[131,128]{1,0:T(8,128)(2,1)S(1)} %get-tuple-element.23), channel_id=1, source_target_pairs={{0,12},{4,0},{8,4},{12,8},{1,13},{5,1},{9,5},{13,9},{2,14},{6,2},{... | collective-permute-start | bytes 100616 | tf_op jit(solution)/shard_map/ppermute | solution.py:12
  64.3 4.2 %collective-permute-start.17 = (bf16[8,2048]{1,0:T(8,128)(2,1)S(1)}, bf16[8,2048]{1,0:T(8,128)(2,1)S(1)}, u32[]{:S(2)}, u32[]{:S(2)}) collective-permute-start(bf16[8,2048]{1,0:T(8,128)(2,1)S(1)} %fusion.52), channel_id=1, source_target_pairs={{0,12},{4,0},{8,4},{12,8},{1,13},{5,1},{9,5},{13,9},{2,14},{6,2},{... | collective-permute-start | bytes 98312 | tf_op jit(solution)/shard_map/ppermute | solution.py:12
  66.1 4.9 %collective-permute-start.16 = (bf16[8,2048]{1,0:T(8,128)(2,1)S(1)}, bf16[8,2048]{1,0:T(8,128)(2,1)S(1)}, u32[]{:S(2)}, u32[]{:S(2)}) collective-permute-start(bf16[8,2048]{1,0:T(8,128)(2,1)S(1)} %fusion.52), channel_id=1, source_target_pairs={{0,8},{4,12},{8,0},{12,4},{1,9},{5,13},{9,1},{13,5},{2,10},{6,14},... | collective-permute-start | bytes 98312 | tf_op jit(solution)/shard_map/ppermute | solution.py:12
  67.0 5.7 %collective-permute-start.15 = (bf16[8,2048]{1,0:T(8,128)(2,1)S(1)}, bf16[8,2048]{1,0:T(8,128)(2,1)S(1)}, u32[]{:S(2)}, u32[]{:S(2)}) collective-permute-start(bf16[8,2048]{1,0:T(8,128)(2,1)S(1)} %fusion.52), channel_id=1, source_target_pairs={{0,4},{4,8},{8,12},{12,0},{1,5},{5,9},{9,13},{13,1},{2,6},{6,10},{... | collective-permute-start | bytes 98312 | tf_op jit(solution)/shard_map/ppermute | solution.py:12
  77.7 1.3 %collective-permute-start.18 = (bf16[2,8,2048]{2,1,0:T(8,128)(2,1)S(1)}, bf16[2,8,2048]{2,1,0:T(8,128)(2,1)S(1)}, u32[]{:S(2)}, u32[]{:S(2)}) collective-permute-start(bf16[2,8,2048]{2,1,0:T(8,128)(2,1)S(1)} %fusion.48), channel_id=1, source_target_pairs={{0,1},{1,0},{2,3},{3,2},{4,5},{5,4},{6,7},{7,6},{8,9},{9,8},{10,11... | collective-permute-start | bytes 196616 | tf_op jit(solution)/shard_map/ppermute | solution.py:12
  79.0 4.0 %collective-permute-start.19 = (bf16[8,2048]{1,0:T(8,128)(2,1)S(1)}, bf16[8,2048]{1,0:T(8,128)(2,1)S(1)}, u32[]{:S(2)}, u32[]{:S(2)}) collective-permute-start(bf16[8,2048]{1,0:T(8,128)(2,1)S(1)} %fusion.56), channel_id=1, source_target_pairs={{0,2},{2,0},{1,3},{3,1},{4,6},{6,4},{5,7},{7,5},{8,10},{10,8},{9,1... | collective-permute-start | bytes 98312 | tf_op jit(solution)/shard_map/ppermute | solution.py:12

commit v2 on v0

v2 whole, which is shorter than its diff:
```python
import functools

import jax
import jax.numpy as jnp
from jax import lax
from jax.experimental import pallas as pl
from jax.experimental.pallas import tpu as pltpu
from jax.sharding import PartitionSpec as P

masked_score = -1e30
norm_epsilon = 1e-05
bf16 = jnp.bfloat16
f32 = jnp.float32


def shifted(part, axis, by):
    peers = lax.axis_size(axis)
    return lax.ppermute(part, axis, [(i, (i + by) % peers) for i in range(peers)])


def block_at(array, index, axis=0):
    return lax.dynamic_index_in_dim(array, index, axis, keepdims=False)


def summed_rows(partial, axis):
    peers = lax.axis_size(axis)
    me = lax.axis_index(axis)
    total = block_at(partial, me)
    for by in range(1, peers):
        piece = block_at(partial, (me + by) % peers).astype(bf16)
        total = total + shifted(piece, axis, by).astype(f32)
    return total


vmem = pl.BlockSpec(memory_space=pltpu.VMEM)
smem = pl.BlockSpec(memory_space=pltpu.SMEM)


def call(body, outs, name, flops, moved, n_scalar, n_in, scratch=(), limit=None):
    return pl.pallas_call(
        body,
        out_shape=outs,
        in_specs=[smem] * n_scalar + [vmem] * n_in,
        out_specs=jax.tree.map(lambda _: vmem, outs),
        scratch_shapes=list(scratch),
        name=name,
        cost_estimate=pl.CostEstimate(flops=flops, bytes_accessed=moved, transcendentals=0),
        compiler_params=pltpu.CompilerParams(vmem_limit_bytes=limit or (16 << 20)),
    )


def project_body(halves, *refs):
    row_refs, (key_ref, value_ref, out_ref) = refs[:halves], refs[halves:]
    rows = jnp.concatenate([ref[...] for ref in row_refs], axis=0)
    width = key_ref.shape[1]
    out_ref[:, :width] = jnp.dot(rows, key_ref[...], preferred_element_type=f32).astype(out_ref.dtype)
    out_ref[:, width:] = jnp.dot(rows, value_ref[...], preferred_element_type=f32).astype(out_ref.dtype)


def row_limits(message_refs, unit_rows, query_rows):
    columns = []
    for ref in message_refs:
        digits = ref[query_rows:, :].astype(f32)
        limit = digits[:unit_rows, 0:1] + 256.0 * digits[:unit_rows, 1:2] + 65536.0 * digits[:unit_rows, 2:3]
        columns.append(limit)
    return columns


def cached_body(blocks, text_rows, kv, scale, *refs):
    base_ref = refs[0]
    message_refs = refs[1 : 1 + blocks]
    key_ref, value_ref, sum_ref, peak_ref, total_ref = refs[1 + blocks :]
    depth = message_refs[0].shape[1]
    query_rows = message_refs[0].shape[0] - 16
    unit = query_rows // kv
    group = unit // text_rows
    keys = key_ref.shape[0]
    base = base_ref[0]
    step = min(blocks, 4)
    position = lax.broadcasted_iota(jnp.int32, (step * unit, keys), 1) + base
    for start in range(0, blocks, step):
        some = message_refs[start : start + step]
        limit = jnp.concatenate(
            [jnp.concatenate([c] * group, axis=0) for c in row_limits(some, text_rows, query_rows)],
            axis=0,
        )
        visible = position < limit.astype(jnp.int32)
        for c in range(kv):
            query = jnp.concatenate([ref[c * unit : (c + 1) * unit, :] for ref in some], axis=0)
            lanes = slice(c * depth, (c + 1) * depth)
            scores = lax.dot_general(
                query, key_ref[:, lanes], (((1,), (1,)), ((), ())), preferred_element_type=f32
            ) * scale
            scores = jnp.where(visible, scores, masked_score)
            peak = jnp.max(scores, axis=1, keepdims=True)
            weights = jnp.where(visible, jnp.exp(scores - peak), 0.0)
            total = jnp.sum(weights, axis=1, keepdims=True)
            summed = jnp.dot(weights.astype(bf16), value_ref[:, lanes], preferred_element_type=f32)
            rows = slice(start * unit, (start + step) * unit)
            sum_ref[c, rows, :] = summed
            peak_ref[c, rows, :] = jnp.broadcast_to(peak, summed.shape)
            total_ref[c, rows, :] = jnp.broadcast_to(total, summed.shape)


def fresh_body(blocks, text_rows, kv, halves, scale, *refs):
    base_ref, half_ref = refs[:2]
    message_refs = refs[2 : 2 + blocks]
    own_ref = refs[2 + blocks]
    term_refs = refs[3 + blocks : 2 + 2 * blocks]
    gain_ref, sum_ref, peak_ref, total_ref, key_out, value_out = refs[2 + 2 * blocks : 8 + 2 * blocks]
    out_refs = refs[8 + 2 * blocks :]
    depth = message_refs[0].shape[1]
    query_rows = message_refs[0].shape[0] - 16
    unit = query_rows // kv
    group = unit // text_rows
    width = kv * depth
    raw = term_refs[0][...].astype(f32)
    for ref in term_refs[1:]:
        raw = raw + ref[...].astype(f32)
    count = raw.shape[0] // halves
    my_half = half_ref[0]
    turned = raw
    for turn in range(1, halves):
        other = jnp.concatenate((raw[-turn * count :], raw[: -turn * count]), axis=0)
        turned = jnp.where(my_half == turn, other, turned)
    raw = turned + own_ref[...]
    keys = raw.shape[0]
    value_rows = raw[:, width:].astype(bf16)
    value_out[...] = value_rows
    position = lax.broadcasted_iota(jnp.int32, (unit, keys), 1) + base_ref[0]
    limits = [
        jnp.concatenate([c] * group, axis=0).astype(jnp.int32)
        for c in row_limits(message_refs, text_rows, query_rows)
    ]
    diagonal = lax.broadcasted_iota(jnp.int32, (unit, unit), 0) == lax.broadcasted_iota(
        jnp.int32, (unit, unit), 1
    )
    key_rows = []
    for c in range(kv):
        lanes = slice(c * depth, (c + 1) * depth)
        part = raw[:, lanes]
        mean_square = jnp.mean(part * part, axis=1, keepdims=True)
        normed = (part * lax.rsqrt(mean_square + norm_epsilon) * gain_ref[...]).astype(bf16)
        key_out[:, lanes] = normed
        key_rows.append(normed)
    for at in range(blocks):
        visible = position < limits[at]
        logs = []
        for c in range(kv):
            lanes = slice(c * depth, (c + 1) * depth)
            query = message_refs[at][c * unit : (c + 1) * unit, :]
            scores = lax.dot_general(
                query, key_rows[c], (((1,), (1,)), ((), ())), preferred_element_type=f32
            ) * scale
            scores = jnp.where(visible, scores, masked_score)
            rows = slice(at * unit, (at + 1) * unit)
            old_peak = peak_ref[c, rows, :]
            peak = jnp.maximum(jnp.max(scores, axis=1, keepdims=True), old_peak)
            weights = jnp.where(visible, jnp.exp(scores - peak[:, :1]), 0.0)
            factor = jnp.exp(old_peak - peak)
            total = factor * total_ref[c, rows, :] + jnp.sum(weights, axis=1, keepdims=True)
            summed = factor * sum_ref[c, rows, :] + jnp.dot(
                weights.astype(bf16), value_rows[:, lanes], preferred_element_type=f32
            )
            some = total > 0.0
            safe = jnp.where(some, total, 1.0)
            out_refs[at][c * unit : (c + 1) * unit, :] = (summed / safe).astype(bf16)
            log = jnp.where(some, peak + jnp.log(safe), masked_score)
            logs.append(jnp.sum(jnp.where(diagonal, log[:, :1], 0.0), axis=0, keepdims=True))
        log = jnp.concatenate(logs, axis=1)
        if log.shape[1] < depth:
            log = jnp.concatenate((log, jnp.zeros((1, depth - log.shape[1]), f32)), axis=1)
        high = log.astype(bf16).astype(f32)
        middle = (log - high).astype(bf16).astype(f32)
        low = log - high - middle
        pieces = jnp.concatenate((high, middle, low, jnp.zeros((13, depth), f32)), axis=0)
        out_refs[at][query_rows:, :] = pieces.astype(bf16)


def merge_body(blocks, text_rows, *refs):
    message_refs, out_ref = refs[:blocks], refs[blocks]
    depth = message_refs[0].shape[1]
    query_rows = message_refs[0].shape[0] - 16
    logs = []
    diagonal = lax.broadcasted_iota(jnp.int32, (depth, depth), 0) == lax.broadcasted_iota(
        jnp.int32, (depth, depth), 1
    )
    for ref in message_refs:
        pieces = ref[query_rows:, :].astype(f32)
        logs.append(pieces[0:1] + pieces[1:2] + pieces[2:3])
    top = logs[0]
    for log in logs[1:]:
        top = jnp.maximum(top, log)
    shares = [jnp.exp(log - top) for log in logs]
    whole = shares[0]
    for share in shares[1:]:
        whole = whole + share
    merged = None
    for share, ref in zip(shares, message_refs):
        column = jnp.sum(jnp.where(diagonal, share / whole, 0.0), axis=1, keepdims=True)
        term = column[:query_rows] * ref[:query_rows, :].astype(f32)
        merged = term if merged is None else merged + term
    for head in range(query_rows // text_rows):
        out_ref[:, head * depth : (head + 1) * depth] = merged[
            head * text_rows : (head + 1) * text_rows
        ].astype(bf16)


def output_body(blocks, *refs):
    index_ref = refs[0]
    row_refs = refs[1 : 1 + blocks]
    weight_ref, out_ref, rows_ref = refs[1 + blocks :]
    count = row_refs[0].shape[0]
    for by, ref in enumerate(row_refs):
        at = lax.rem(index_ref[0] + (blocks - by), blocks)
        rows_ref[pl.ds(pl.multiple_of(at * count, count), count), :] = ref[...].astype(f32)
    rows = rows_ref[...].astype(bf16)
    out_ref[...] = jnp.dot(rows, weight_ref[...], preferred_element_type=f32)


def on_device(
    queries,
    key_cache,
    value_cache,
    new_features,
    key_weight,
    value_weight,
    key_gain,
    out_weight,
    frame_length,
    text_frame,
):
    cached_rows, local_kv, head_depth = key_cache.shape
    kv_width = key_weight.shape[1]
    depth = key_weight.shape[0]
    new_rows = new_features.shape[0]
    text_rows, local_heads, _ = queries.shape
    group = local_heads // local_kv
    query_rows = text_rows * local_heads
    seq_size = lax.axis_size("seq")
    head_size = lax.axis_size("head")
    section_size = lax.axis_size("section")
    seq_index = lax.axis_index("seq")
    head_index = lax.axis_index("head")
    half_rows = new_rows // head_size
    sds = jax.ShapeDtypeStruct

    arrived = []
    for by in range(1, seq_size):
        at = (seq_index + by) % seq_size
        piece = lax.dynamic_slice(
            new_features, (head_index * half_rows, at * depth), (half_rows, depth)
        )
        arrived.append(shifted(piece, "seq", by))
    own_rows = lax.dynamic_slice(new_features, (0, seq_index * depth), (new_rows, depth))

    frame_index = jnp.arange(frame_length.shape[0], dtype=jnp.int32)
    row_limit = jnp.sum(
        jnp.where(frame_index[None, :] <= text_frame[:, None], frame_length[None, :], 0), axis=1
    )
    digits = jnp.stack([row_limit % 256, (row_limit // 256) % 256, row_limit // 65536], axis=1)
    digits = jnp.pad(digits.astype(bf16), ((0, 16 - text_rows), (0, head_depth - 3)))
    grouped = queries.reshape(text_rows, local_kv, group, head_depth)
    grouped = jnp.transpose(grouped, (1, 2, 0, 3)).reshape(query_rows, head_depth)
    message = jnp.concatenate((grouped, digits), axis=0)
    messages = [message] + [shifted(message, "seq", by) for by in range(1, seq_size)]

    weight_bytes = 2 * depth * 2 * kv_width
    flops = 4 * new_rows * depth * kv_width

    def project(rows, dtype):
        return call(
            functools.partial(project_body, len(rows)),
            sds((new_rows, 2 * kv_width), dtype),
            "project",
            flops,
            weight_bytes,
            0,
            len(rows) + 2,
        )(*rows, key_weight, value_weight)

    own_term = project([own_rows], f32)
    terms = []
    for by, half in enumerate(arrived):
        halves = [half] + [shifted(half, "head", head_size - turn) for turn in range(1, head_size)]
        terms.append(shifted(project(halves, bf16), "seq", seq_size - (by + 1)))

    score_scale = head_depth ** (-0.5)
    base = (seq_index * (cached_rows + new_rows)).astype(jnp.int32).reshape(1)
    every_row = seq_size * query_rows // local_kv
    stats = sds((local_kv, every_row, head_depth), f32)
    attend_flops = 4 * seq_size * query_rows * head_depth * cached_rows
    cached = call(
        functools.partial(cached_body, seq_size, text_rows, local_kv, score_scale),
        (stats, stats, stats),
        "cached",
        attend_flops,
        4 * cached_rows * kv_width,
        1,
        seq_size + 2,
        limit=40 << 20,
    )(
        base,
        *messages,
        key_cache.reshape(cached_rows, kv_width),
        value_cache.reshape(cached_rows, kv_width),
    )
    fresh = call(
        functools.partial(fresh_body, seq_size, text_rows, local_kv, head_size, score_scale),
        (sds((new_rows, kv_width), bf16),) * 2 + (sds((query_rows + 16, head_depth), bf16),) * seq_size,
        "fresh",
        attend_flops * new_rows // cached_rows,
        8 * every_row * kv_width,
        2,
        2 * seq_size + 4,
    )(
        base + cached_rows,
        head_index.astype(jnp.int32).reshape(1),
        *messages,
        own_term,
        *terms,
        key_gain.reshape(1, head_depth),
        *cached,
    )
    new_keys, new_values = (part.reshape(new_rows, local_kv, head_depth) for part in fresh[:2])
    returned = [fresh[2]] + [
        shifted(fresh[2 + by], "seq", seq_size - by) for by in range(1, seq_size)
    ]
    attended = call(
        functools.partial(merge_body, seq_size, text_rows),
        sds((text_rows, local_heads * head_depth), bf16),
        "merge",
        seq_size * query_rows * head_depth,
        2 * seq_size * query_rows * head_depth,
        0,
        seq_size,
    )(*returned)

    every = [attended] + [shifted(attended, "seq", by) for by in range(1, seq_size)]
    all_rows = seq_size * text_rows
    partial = call(
        functools.partial(output_body, seq_size),
        sds((all_rows, out_weight.shape[1]), f32),
        "output",
        2 * all_rows * out_weight.size,
        2 * out_weight.size,
        1,
        seq_size + 1,
        scratch=[pltpu.VMEM((all_rows, out_weight.shape[0]), f32)],
        limit=24 << 20,
    )(seq_index.astype(jnp.int32).reshape(1), *every, out_weight)

    out_rows = all_rows // (section_size * head_size)
    partial = partial.reshape(section_size, head_size, out_rows, -1)
    partial = summed_rows(jnp.swapaxes(partial, 0, 1), "head")
    layer_output = summed_rows(partial, "section").astype(bf16)
    return (layer_output, new_keys, new_values)


def solution(mesh):
    placed = (
        P(("groups", "seq"), ("section", "head"), None),
        P(("groups", "seq"), ("section", "head"), None),
        P(("groups", "seq"), ("section", "head"), None),
        P(("groups", "seq"), None),
        P("seq", ("section", "head")),
        P("seq", ("section", "head")),
        P(),
        P(("section", "head"), "seq"),
        P("groups"),
        P(("groups", "seq")),
    )
    return jax.shard_map(
        on_device,
        mesh=mesh,
        in_specs=placed,
        out_specs=(
            P(("groups", "section", "head"), "seq"),
            P(("groups", "seq"), ("section", "head"), None),
            P(("groups", "seq"), ("section", "head"), None),
        ),
        check_vma=False,
    )
```

time: 144 us -> 67 us (0.47)
  waiting for transfers between devices: 84 us -> 16.9 us
  between operations: 14.3 us -> 0.94 us
  blocking collectives: 13.3 us -> 0 us
  Pallas kernels: 0 us -> 11.5 us
  starting transfers between devices: 15.2 us -> 23.7 us
  matrix products: 8.47 us -> 0 us
  local copies, waits for them, and re-layouts: 5.37 us -> 11.9 us
    reduce_scatter x2 -> x0, waiting for transfers between devices: 24.3 us -> none  [the longest x1 17.3 us: on_device(): lax.psum_scatter(partial_terms.astype(jnp.bfloat16), ('section', 'head'),...]
    all_to_all x1 -> x0, waiting for transfers between devices: 22.7 us -> none  [on_device(): lax.all_to_all(new_features, 'seq', split_axis=1, concat_axis=0, tiled=True)]
    ppermute x17 -> x20, waiting for transfers between devices: 36.9 us -> 16.9 us  [shifted(): lax.ppermute(part, axis, [(i, (i + by) % peers) for i in range(peers)])]
    ppermute x17 -> x20, starting transfers between devices: 8.83 us -> 23.7 us  [shifted(): lax.ppermute(part, axis, [(i, (i + by) % peers) for i in range(peers)])]
    all_gather x1 -> x0, blocking collectives: 13.3 us -> none  [on_device(): lax.all_gather(attended, 'seq', axis=0, tiled=True)]
    pallas_call x0 -> x8, Pallas kernels: none -> 11.5 us  [the longest x4 4.7 us: project(): call(functools.partial(project_body, len(rows)), sds((new_rows, 2 * kv_wi...]
    dot_general x10 -> x0, matrix products: 8.47 us -> none  [the longest x1 2.38 us: on_device(): jnp.dot(spread, stacked_weight, preferred_element_type=jnp.float32)]
    all_to_all x1 -> x0, starting transfers between devices: 6.35 us -> none  [on_device(): lax.all_to_all(new_features, 'seq', split_axis=1, concat_axis=0, tiled=True)]
  transfers between devices with their start and end apart: 20 -> 20, of which waited for: 13 -> 8; matrix products, arithmetic and copies ran while one was open for 8% -> 9% of each run, Pallas kernels for 0% -> 10%
where the time goes in v2:
time: 67 us; the launch traced here: 66.6 us
  starting transfers between devices  23.7 us (35%)
  waiting for transfers between devices  16.9 us (25%)
  local copies, waits for them, and re-layouts  11.9 us (18%)
  Pallas kernels  11.5 us (17%)
  other arithmetic  1.6 us (2%)
  between operations  0.94 us (1%)
    ppermute x20, starting transfers between devices, shifted(): lax.ppermute(part, axis, [(i, (i + by) % peers) for i in range(peers)])  23.7 us
    ppermute x20, waiting for transfers between devices, shifted(): lax.ppermute(part, axis, [(i, (i + by) % peers) for i in range(peers)])  16.9 us
    unnamed x10, local copies, waits for them, and re-layouts  5.84 us
    pallas_call x4, Pallas kernels, project(): call(functools.partial(project_body, len(rows)), sds((new_rows, 2 * kv_wi...  4.7 us
    pallas_call x1, Pallas kernels, on_device(): call(functools.partial(fresh_body, seq_size, text_rows, local_kv, head_si...  2.84 us
    pallas_call x1, Pallas kernels, on_device(): call(functools.partial(cached_body, seq_size, text_rows, local_kv, score_...  2.22 us
    reshape x1, local copies, waits for them, and re-layouts, on_device(): value_cache.reshape(cached_rows, kv_width)  1.84 us
    pallas_call x1, Pallas kernels, on_device(): call(functools.partial(output_body, seq_size), sds((all_rows, out_weight....  1.53 us
  transfers between devices with their start and end apart: 20, of which 8 were waited for; matrix products, arithmetic and copies ran while one was open for 9% of the time, Pallas kernels for 10%

profile of v2, /device:TPU:0, one launch (start us, length us, event | category | flops | bytes accessed | tf_op | source)
XLA Modules:
  0.0 66.6 jit_solution(7851285184992062034)
XLA Ops:
  0.6 0.0 copy-start.1
  0.7 1.1 %fusion.19 = (bf16[32,2048]{1,0:T(8,128)(2,1)S(1)}, bf16[32,2048]{1,0:T(8,128)(2,1)S(1)}, bf16[32,2048]{1,0:T(8,128)(2,1)S(1)}) fusion(bf16[64,8192]{1,0:T(8,128)(2,1)} %param.13, s32[]{:T(128)S(6)} %select_n.110, s32[]{:T(128)S(6)} %select_n.116, s32[]{:T(128)S(6)} %select_n.112, s32[]{:T(128)S(6)} %select_n.114), kind=kLoop, calls=%fused_computation.43 | loop fusion | bytes 786448 | tf_op jit(solution)/shard_map/dynamic_slice | solution.py:251
  1.8 0.0 copy-start.4
  1.8 5.1 %collective-permute-start.9 = (bf16[32,2048]{1,0:T(8,128)(2,1)S(1)}, bf16[32,2048]{1,0:T(8,128)(2,1)}, u32[]{:S(2)}, u32[]{:S(2)}) collective-permute-start(bf16[32,2048]{1,0:T(8,128)(2,1)S(1)} %get-tuple-element.21), channel_id=1, source_target_pairs={{0,12},{4,0},{8,4},{12,8},{1,13},{5,1},{9,5},{13,9},{2,14},{6,2},{... | collective-permute-start | bytes 393224 | tf_op jit(solution)/shard_map/ppermute | solution.py:18
  7.0 1.0 %collective-permute-start.3 = (bf16[32,2048]{1,0:T(8,128)(2,1)S(1)}, bf16[32,2048]{1,0:T(8,128)(2,1)S(1)}, u32[]{:S(2)}, u32[]{:S(2)}) collective-permute-start(bf16[32,2048]{1,0:T(8,128)(2,1)S(1)} %get-tuple-element.22), channel_id=1, source_target_pairs={{0,4},{4,8},{8,12},{12,0},{1,5},{5,9},{9,13},{13,1},{2,6},{6,10},{... | collective-permute-start | bytes 393224 | tf_op jit(solution)/shard_map/ppermute | solution.py:18
  8.0 0.9 %select_reduce_fusion = s32[8]{0:T(128)S(1)} fusion(s32[64]{0:T(128)} %param.18, s32[8]{0:T(128)} %param.19), kind=kLoop, calls=%fused_computation.38 | loop fusion | flops 1528 | bytes 320 | tf_op jit(solution)/shard_map/reduce_sum | solution.py:258
  8.8 0.1 copy.20
  9.0 0.1 fusion.11
  9.0 0.8 %copy.19 = bf16[8,2,8,128]{3,0,2,1:T(8,128)(2,1)S(1)} copy(bf16[8,2,8,128]{3,2,1,0:T(8,128)(2,1)} %bitcast.36) | data formatting | bytes 65536 | tf_op jit(solution)/shard_map/reshape | solution.py:263
  9.8 2.5 %collective-permute-start = (bf16[144,128]{1,0:T(8,128)(2,1)S(1)}, bf16[144,128]{1,0:T(8,128)(2,1)S(1)}, u32[]{:S(2)}, u32[]{:S(2)}) collective-permute-start(bf16[144,128]{1,0:T(8,128)(2,1)S(1)} %pad_maximum_fusion.refs_1_.refs_2_), channel_id=1, source_target_pairs={{0,4},{4,8},{8,12},{12,0},{1,5},{5,9},{9,13},{13,1},{2,6},{6,10},{... | collective-permute-start | bytes 110600 | tf_op jit(solution)/shard_map/ppermute | solution.py:18
  12.3 0.9 %collective-permute-start.1 = (bf16[144,128]{1,0:T(8,128)(2,1)S(1)}, bf16[144,128]{1,0:T(8,128)(2,1)S(1)}, u32[]{:S(2)}, u32[]{:S(2)}) collective-permute-start(bf16[144,128]{1,0:T(8,128)(2,1)S(1)} %pad_maximum_fusion.refs_1_.refs_2_), channel_id=1, source_target_pairs={{0,8},{4,12},{8,0},{12,4},{1,9},{5,13},{9,1},{13,5},{2,10},{6,14},... | collective-permute-start | bytes 110600 | tf_op jit(solution)/shard_map/ppermute | solution.py:18
  13.3 6.9 %collective-permute-done.6.refs_0_ = bf16[32,2048]{1,0:T(8,128)(2,1)S(1)} collective-permute-done((bf16[32,2048]{1,0:T(8,128)(2,1)S(1)}, bf16[32,2048]{1,0:T(8,128)(2,1)S(1)}, u32[]{:S(2)}, u32[]{:S(2)}) %collective-permute-start.6) | collective-permute-done | bytes 131104 | tf_op jit(solution)/shard_map/ppermute | solution.py:18
  20.2 0.5 collective-permute-start.4
  20.7 1.8 %copy_bitcast_fusion = (bf16[1984,256]{1,0:T(8,128)(2,1)S(1)}, bf16[1984,256]{1,0:T(8,128)(2,1)S(1)}) fusion(bf16[248,8,2,128]{3,2,1,0:T(2,128)(2,1)} %bitcast.33, bf16[248,8,2,128]{3,2,1,0:T(2,128)(2,1)} %bitcast.34), kind=kLoop, calls=%fused_computation | loop fusion | bytes 4063232 | tf_op jit(solution)/shard_map/reshape | solution.py:306
  22.5 0.1 collective-permute-start.2
  22.6 1.2 %copy-done = bf16[2048,256]{1,0:T(8,128)(2,1)S(1)} copy-done((bf16[2048,256]{1,0:T(8,128)(2,1)S(1)}, bf16[2048,256]{1,0:T(8,128)(2,1)}, u32[]{:S(2)}) %copy-start) | copy-done | bytes 1048600
  23.8 1.2 %copy-done.2 = bf16[2048,256]{1,0:T(8,128)(2,1)S(1)} copy-done((bf16[2048,256]{1,0:T(8,128)(2,1)S(1)}, bf16[2048,256]{1,0:T(8,128)(2,1)}, u32[]{:S(2)}) %copy-start.2) | copy-done | bytes 1048600
  25.1 1.5 %project.7 = bf16[64,512]{1,0:T(8,128)(2,1)S(1)} custom-call(bf16[32,2048]{1,0:T(8,128)(2,1)} %collective-permute-done.9.refs_0_, bf16[32,2048]{1,0:T(8,128)(2,1)} %collective-permute-done.10.refs_1_, bf16[2048,256]{1,0:T(8,128)(2,1)S(1)} %copy-done, bf16[2048,256]{1,0:T(8,128)(2,1)S(1)} %copy-done.2), custom_call_target="tpu_custom_call" | custom-call | flops 134217728 | bytes 2097152 | tf_op jit(solution)/shard_map/project/pallas_call | solution.py:272
  26.5 2.1 %collective-permute-start.11 = (bf16[64,512]{1,0:T(8,128)(2,1)S(1)}, bf16[64,512]{1,0:T(8,128)(2,1)S(1)}, u32[]{:S(2)}, u32[]{:S(2)}) collective-permute-start(bf16[64,512]{1,0:T(8,128)(2,1)S(1)} %project.7), channel_id=1, source_target_pairs={{0,4},{4,8},{8,12},{12,0},{1,5},{5,9},{9,13},{13,1},{2,6},{6,10},{... | collective-permute-start | bytes 196616 | tf_op jit(solution)/shard_map/ppermute | solution.py:18
  28.6 1.4 %project.6 = bf16[64,512]{1,0:T(8,128)(2,1)S(1)} custom-call(bf16[32,2048]{1,0:T(8,128)(2,1)S(1)} %collective-permute-done.6.refs_0_, bf16[32,2048]{1,0:T(8,128)(2,1)} %collective-permute-done.7.refs_1_, bf16[2048,256]{1,0:T(8,128)(2,1)S(1)} %copy-done, bf16[2048,256]{1,0:T(8,128)(2,1)S(1)} %copy-done.2), custom_call_target="tpu_custom_call" | custom-call | flops 134217728 | bytes 2097152 | tf_op jit(solution)/shard_map/project/pallas_call | solution.py:272
  30.0 1.8 %collective-permute-start.8 = (bf16[64,512]{1,0:T(8,128)(2,1)S(1)}, bf16[64,512]{1,0:T(8,128)(2,1)S(1)}, u32[]{:S(2)}, u32[]{:S(2)}) collective-permute-start(bf16[64,512]{1,0:T(8,128)(2,1)S(1)} %project.6), channel_id=1, source_target_pairs={{0,8},{4,12},{8,0},{12,4},{1,9},{5,13},{9,1},{13,5},{2,10},{6,14},... | collective-permute-start | bytes 196616 | tf_op jit(solution)/shard_map/ppermute | solution.py:18
  31.8 1.4 %project.5 = bf16[64,512]{1,0:T(8,128)(2,1)S(1)} custom-call(bf16[32,2048]{1,0:T(8,128)(2,1)S(1)} %collective-permute-done.3.refs_0_, bf16[32,2048]{1,0:T(8,128)(2,1)} %collective-permute-done.4.refs_1_, bf16[2048,256]{1,0:T(8,128)(2,1)S(1)} %copy-done, bf16[2048,256]{1,0:T(8,128)(2,1)S(1)} %copy-done.2), custom_call_target="tpu_custom_call" | custom-call | flops 134217728 | bytes 2097152 | tf_op jit(solution)/shard_map/project/pallas_call | solution.py:272
  33.2 1.0 %collective-permute-start.5 = (bf16[64,512]{1,0:T(8,128)(2,1)S(1)}, bf16[64,512]{1,0:T(8,128)(2,1)S(1)}, u32[]{:S(2)}, u32[]{:S(2)}) collective-permute-start(bf16[64,512]{1,0:T(8,128)(2,1)S(1)} %project.5), channel_id=1, source_target_pairs={{0,12},{4,0},{8,4},{12,8},{1,13},{5,1},{9,5},{13,9},{2,14},{6,2},{... | collective-permute-start | bytes 196616 | tf_op jit(solution)/shard_map/ppermute | solution.py:18
  34.2 1.0 %constant_dynamic-slice_fusion.refs_0_ = bf16[64,2048]{1,0:T(8,128)(2,1)S(1)} fusion(bf16[64,8192]{1,0:T(8,128)(2,1)} %param.13, s32[]{:T(128)S(6)} %select_n.109), kind=kLoop, calls=%fused_computation.42 | loop fusion | bytes 524292 | tf_op jit(solution)/shard_map/dynamic_slice | solution.py:255
  35.1 0.5 project.4.refs_6_
  35.6 2.2 %cached.1 = (f32[2,256,128]{2,1,0:T(8,128)S(1)}, f32[2,256,128]{2,1,0:T(8,128)S(1)}, f32[2,256,128]{2,1,0:T(8,128)S(1)}) custom-call(s32[1]{0:T(128)} %bitcast.1.refs_0_, bf16[144,128]{1,0:T(8,128)(2,1)S(1)} %pad_maximum_fusion.refs_1_.refs_2_, bf16[144,128]{1,0:T(8,128)(2,1)S(1)} %collective-permute-done.refs_2_.refs_3_, ...), custom_call_target="tpu_custom_call" | custom-call | flops 520093696 | bytes 2031616 | tf_op jit(solution)/shard_map/cached/pallas_call | solution.py:293
  37.9 2.8 %fresh.1 = (bf16[64,256]{1,0:T(8,128)(2,1)S(1)}, bf16[64,256]{1,0:T(8,128)(2,1)S(1)}, bf16[144,128]{1,0:T(8,128)(2,1)S(1)}, bf16[144,128]{1,0:T(8,128)(2,1)S(1)}...) custom-call(s32[1]{0:T(128)S(6)} %add.113.refs_0_, s32[1]{0:T(128)} %bitcast.2.refs_1_, ...), custom_call_target="tpu_custom_call" | custom-call | flops 16777216 | bytes 524288 | tf_op jit(solution)/shard_map/fresh/pallas_call | solution.py:308
  40.8 2.4 %collective-permute-start.12 = (bf16[144,128]{1,0:T(8,128)(2,1)S(1)}, bf16[144,128]{1,0:T(8,128)(2,1)S(1)}, u32[]{:S(2)}, u32[]{:S(2)}) collective-permute-start(bf16[144,128]{1,0:T(8,128)(2,1)S(1)} %get-tuple-element.16), channel_id=1, source_target_pairs={{0,12},{4,0},{8,4},{12,8},{1,13},{5,1},{9,5},{13,9},{2,14},{6,2},{... | collective-permute-start | bytes 110600 | tf_op jit(solution)/shard_map/ppermute | solution.py:18
  43.1 0.3 collective-permute-start.13
  43.4 0.7 collective-permute-start.14
  44.0 0.7 %collective-permute-done.12.refs_1_ = bf16[144,128]{1,0:T(8,128)(2,1)S(1)} collective-permute-done((bf16[144,128]{1,0:T(8,128)(2,1)S(1)}, bf16[144,128]{1,0:T(8,128)(2,1)S(1)}, u32[]{:S(2)}, u32[]{:S(2)}) %collective-permute-start.12) | collective-permute-done | bytes 36896 | tf_op jit(solution)/shard_map/ppermute | solution.py:18
  44.8 3.2 %collective-permute-done.13.refs_2_ = bf16[144,128]{1,0:T(8,128)(2,1)S(1)} collective-permute-done((bf16[144,128]{1,0:T(8,128)(2,1)S(1)}, bf16[144,128]{1,0:T(8,128)(2,1)S(1)}, u32[]{:S(2)}, u32[]{:S(2)}) %collective-permute-start.13) | collective-permute-done | bytes 36896 | tf_op jit(solution)/shard_map/ppermute | solution.py:18
  48.0 1.2 %collective-permute-done.14.refs_3_ = bf16[144,128]{1,0:T(8,128)(2,1)S(1)} collective-permute-done((bf16[144,128]{1,0:T(8,128)(2,1)S(1)}, bf16[144,128]{1,0:T(8,128)(2,1)S(1)}, u32[]{:S(2)}, u32[]{:S(2)}) %collective-permute-start.14) | collective-permute-done | bytes 36896 | tf_op jit(solution)/shard_map/ppermute | solution.py:18
  49.1 0.2 merge.1.refs_1_
  49.3 0.1 collective-permute-start.15
  49.4 0.9 %collective-permute-start.16 = (bf16[8,2048]{1,0:T(8,128)(2,1)S(1)}, bf16[8,2048]{1,0:T(8,128)(2,1)S(1)}, u32[]{:S(2)}, u32[]{:S(2)}) collective-permute-start(bf16[8,2048]{1,0:T(8,128)(2,1)S(1)} %merge.1.refs_1_), channel_id=1, source_target_pairs={{0,8},{4,12},{8,0},{12,4},{1,9},{5,13},{9,1},{13,5},{2,10},{6,14},... | collective-permute-start | bytes 98312 | tf_op jit(solution)/shard_map/ppermute | solution.py:18
  50.3 2.9 %collective-permute-start.17 = (bf16[8,2048]{1,0:T(8,128)(2,1)S(1)}, bf16[8,2048]{1,0:T(8,128)(2,1)S(1)}, u32[]{:S(2)}, u32[]{:S(2)}) collective-permute-start(bf16[8,2048]{1,0:T(8,128)(2,1)S(1)} %merge.1.refs_1_), channel_id=1, source_target_pairs={{0,12},{4,0},{8,4},{12,8},{1,13},{5,1},{9,5},{13,9},{2,14},{6,2},{... | collective-permute-start | bytes 98312 | tf_op jit(solution)/shard_map/ppermute | solution.py:18
  53.2 1.9 %collective-permute-done.15.refs_2_ = bf16[8,2048]{1,0:T(8,128)(2,1)S(1)} collective-permute-done((bf16[8,2048]{1,0:T(8,128)(2,1)S(1)}, bf16[8,2048]{1,0:T(8,128)(2,1)S(1)}, u32[]{:S(2)}, u32[]{:S(2)}) %collective-permute-start.15) | collective-permute-done | bytes 32800 | tf_op jit(solution)/shard_map/ppermute | solution.py:18
  55.1 0.6 collective-permute-done.17.refs_4_
  55.6 3.4 %copy-done.3 = bf16[2048,2048]{1,0:T(8,128)(2,1)S(1)} copy-done((bf16[2048,2048]{1,0:T(8,128)(2,1)S(1)}, bf16[2048,2048]{1,0:T(8,128)(2,1)}, u32[]{:S(2)}) %copy-start.3) | copy-done | bytes 8388632
  59.0 1.5 %output.1 = f32[32,2048]{1,0:T(8,128)S(1)} custom-call(s32[1]{0:T(128)} %bitcast.refs_0_, bf16[8,2048]{1,0:T(8,128)(2,1)S(1)} %merge.1.refs_1_, bf16[8,2048]{1,0:T(8,128)(2,1)S(1)} %collective-permute-done.15.refs_2_, bf16[8,2048]{1,0:T(8,128)(2,1)S(1)} %collective-permute-done.16.refs_3_, bf16[8,2048]{1,0:T(8,128)(2,1)S(1)} %collective-permute-done.17.refs_4_, ...), custom_call_target="tpu_custom_call" | custom-call | flops 268435456 | bytes 8388608 | tf_op jit(solution)/shard_map/output/pallas_call | solution.py:341
  60.6 0.1 collective-permute-start.18
  60.7 1.2 %collective-permute-done.18 = bf16[2,8,2048]{2,1,0:T(8,128)(2,1)S(1)} collective-permute-done((bf16[2,8,2048]{2,1,0:T(8,128)(2,1)S(1)}, bf16[2,8,2048]{2,1,0:T(8,128)(2,1)S(1)}, u32[]{:S(2)}, u32[]{:S(2)}) %collective-permute-start.18) | collective-permute-done | bytes 65568 | tf_op jit(solution)/shard_map/ppermute | solution.py:18
  61.9 1.6 %collective-permute-start.19 = (bf16[8,2048]{1,0:T(8,128)(2,1)S(1)}, bf16[8,2048]{1,0:T(8,128)(2,1)S(1)}, u32[]{:S(2)}, u32[]{:S(2)}) collective-permute-start(bf16[8,2048]{1,0:T(8,128)(2,1)S(1)} %fusion.2), channel_id=1, source_target_pairs={{0,2},{2,0},{1,3},{3,1},{4,6},{6,4},{5,7},{7,5},{8,10},{10,8},{9,1... | collective-permute-start | bytes 98312 | tf_op jit(solution)/shard_map/ppermute | solution.py:18
  63.5 0.6 reshape.195
  64.1 0.6 reshape.196
  64.8 1.2 %collective-permute-done.19 = bf16[8,2048]{1,0:T(8,128)(2,1)S(1)} collective-permute-done((bf16[8,2048]{1,0:T(8,128)(2,1)S(1)}, bf16[8,2048]{1,0:T(8,128)(2,1)S(1)}, u32[]{:S(2)}, u32[]{:S(2)}) %collective-permute-start.19) | collective-permute-done | bytes 32800 | tf_op jit(solution)/shard_map/ppermute | solution.py:18
  65.9 0.6 fusion.1
  (25 shorter events, 0.1 us)
Async XLA Ops:
  0.6 34.5 %copy-start.1 = (bf16[2048,256]{1,0:T(8,128)(2,1)S(1)}, bf16[2048,256]{1,0:T(8,128)(2,1)}, u32[]{:S(2)}) copy-start(bf16[2048,256]{1,0:T(8,128)(2,1)} %refs_2_.7) | copy-start | bytes 3145732
  1.8 36.1 %copy-start.4 = (f32[128]{0:T(128)S(1)}, f32[128]{0:T(128)}, u32[]{:S(2)}) copy-start(f32[128]{0:T(128)} %param.16) | copy-start | bytes 1540
  1.8 11.4 %collective-permute-start.9 = (bf16[32,2048]{1,0:T(8,128)(2,1)S(1)}, bf16[32,2048]{1,0:T(8,128)(2,1)}, u32[]{:S(2)}, u32[]{:S(2)}) collective-permute-start(bf16[32,2048]{1,0:T(8,128)(2,1)S(1)} %get-tuple-element.21), channel_id=1, source_target_pairs={{0,12},{4,0},{8,4},{12,8},{1,13},{5,1},{9,5},{13,9},{2,14},{6,2},{... | collective-permute-start | bytes 393224 | tf_op jit(solution)/shard_map/ppermute | solution.py:18
  7.0 13.2 %collective-permute-start.6 = (bf16[32,2048]{1,0:T(8,128)(2,1)S(1)}, bf16[32,2048]{1,0:T(8,128)(2,1)S(1)}, u32[]{:S(2)}, u32[]{:S(2)}) collective-permute-start(bf16[32,2048]{1,0:T(8,128)(2,1)S(1)} %get-tuple-element.23), channel_id=1, source_target_pairs={{0,8},{4,12},{8,0},{12,4},{1,9},{5,13},{9,1},{13,5},{2,10},{6,14},... | collective-permute-start | bytes 393224 | tf_op jit(solution)/shard_map/ppermute | solution.py:18
  7.0 13.2 %collective-permute-start.3 = (bf16[32,2048]{1,0:T(8,128)(2,1)S(1)}, bf16[32,2048]{1,0:T(8,128)(2,1)S(1)}, u32[]{:S(2)}, u32[]{:S(2)}) collective-permute-start(bf16[32,2048]{1,0:T(8,128)(2,1)S(1)} %get-tuple-element.22), channel_id=1, source_target_pairs={{0,4},{4,8},{8,12},{12,0},{1,5},{5,9},{9,13},{13,1},{2,6},{6,10},{... | collective-permute-start | bytes 393224 | tf_op jit(solution)/shard_map/ppermute | solution.py:18
  9.8 23.4 %collective-permute-start = (bf16[144,128]{1,0:T(8,128)(2,1)S(1)}, bf16[144,128]{1,0:T(8,128)(2,1)S(1)}, u32[]{:S(2)}, u32[]{:S(2)}) collective-permute-start(bf16[144,128]{1,0:T(8,128)(2,1)S(1)} %pad_maximum_fusion.refs_1_.refs_2_), channel_id=1, source_target_pairs={{0,4},{4,8},{8,12},{12,0},{1,5},{5,9},{9,13},{13,1},{2,6},{6,10},{... | collective-permute-start | bytes 110600 | tf_op jit(solution)/shard_map/ppermute | solution.py:18
  12.3 23.3 %collective-permute-start.1 = (bf16[144,128]{1,0:T(8,128)(2,1)S(1)}, bf16[144,128]{1,0:T(8,128)(2,1)S(1)}, u32[]{:S(2)}, u32[]{:S(2)}) collective-permute-start(bf16[144,128]{1,0:T(8,128)(2,1)S(1)} %pad_maximum_fusion.refs_1_.refs_2_), channel_id=1, source_target_pairs={{0,8},{4,12},{8,0},{12,4},{1,9},{5,13},{9,1},{13,5},{2,10},{6,14},... | collective-permute-start | bytes 110600 | tf_op jit(solution)/shard_map/ppermute | solution.py:18
  13.3 9.3 %collective-permute-start.10 = (bf16[32,2048]{1,0:T(8,128)(2,1)}, bf16[32,2048]{1,0:T(8,128)(2,1)}, u32[]{:S(2)}, u32[]{:S(2)}) collective-permute-start(bf16[32,2048]{1,0:T(8,128)(2,1)} %collective-permute-done.9.refs_0_), channel_id=1, source_target_pairs={{0,1},{1,0},{2,3},{3,2},{4,5},{5,4},{6,7},{7,6},{8,9},{9,8},{10,11... | collective-permute-start | bytes 393224 | tf_op jit(solution)/shard_map/ppermute | solution.py:18
  20.2 6.4 %collective-permute-start.7 = (bf16[32,2048]{1,0:T(8,128)(2,1)S(1)}, bf16[32,2048]{1,0:T(8,128)(2,1)}, u32[]{:S(2)}, u32[]{:S(2)}) collective-permute-start(bf16[32,2048]{1,0:T(8,128)(2,1)S(1)} %collective-permute-done.6.refs_0_), channel_id=1, source_target_pairs={{0,1},{1,0},{2,3},{3,2},{4,5},{5,4},{6,7},{7,6},{8,9},{9,8},{10,11... | collective-permute-start | bytes 393224 | tf_op jit(solution)/shard_map/ppermute | solution.py:18
  20.2 9.8 %collective-permute-start.4 = (bf16[32,2048]{1,0:T(8,128)(2,1)S(1)}, bf16[32,2048]{1,0:T(8,128)(2,1)}, u32[]{:S(2)}, u32[]{:S(2)}) collective-permute-start(bf16[32,2048]{1,0:T(8,128)(2,1)S(1)} %collective-permute-done.3.refs_0_), channel_id=1, source_target_pairs={{0,1},{1,0},{2,3},{3,2},{4,5},{5,4},{6,7},{7,6},{8,9},{9,8},{10,11... | collective-permute-start | bytes 393224 | tf_op jit(solution)/shard_map/ppermute | solution.py:18
  22.5 13.1 %collective-permute-start.2 = (bf16[144,128]{1,0:T(8,128)(2,1)S(1)}, bf16[144,128]{1,0:T(8,128)(2,1)S(1)}, u32[]{:S(2)}, u32[]{:S(2)}) collective-permute-start(bf16[144,128]{1,0:T(8,128)(2,1)S(1)} %pad_maximum_fusion.refs_1_.refs_2_), channel_id=1, source_target_pairs={{0,12},{4,0},{8,4},{12,8},{1,13},{5,1},{9,5},{13,9},{2,14},{6,2},{... | collective-permute-start | bytes 110600 | tf_op jit(solution)/shard_map/ppermute | solution.py:18
  22.6 1.2 %copy-start = (bf16[2048,256]{1,0:T(8,128)(2,1)S(1)}, bf16[2048,256]{1,0:T(8,128)(2,1)}, u32[]{:S(2)}) copy-start(bf16[2048,256]{1,0:T(8,128)(2,1)} %refs_2_.7) | copy-start | bytes 3145732
  23.8 1.2 %copy-start.2 = (bf16[2048,256]{1,0:T(8,128)(2,1)S(1)}, bf16[2048,256]{1,0:T(8,128)(2,1)}, u32[]{:S(2)}) copy-start(bf16[2048,256]{1,0:T(8,128)(2,1)} %refs_3_.5) | copy-start | bytes 3145732
  26.5 11.3 %collective-permute-start.11 = (bf16[64,512]{1,0:T(8,128)(2,1)S(1)}, bf16[64,512]{1,0:T(8,128)(2,1)S(1)}, u32[]{:S(2)}, u32[]{:S(2)}) collective-permute-start(bf16[64,512]{1,0:T(8,128)(2,1)S(1)} %project.7), channel_id=1, source_target_pairs={{0,4},{4,8},{8,12},{12,0},{1,5},{5,9},{9,13},{13,1},{2,6},{6,10},{... | collective-permute-start | bytes 196616 | tf_op jit(solution)/shard_map/ppermute | solution.py:18
  30.0 7.9 %collective-permute-start.8 = (bf16[64,512]{1,0:T(8,128)(2,1)S(1)}, bf16[64,512]{1,0:T(8,128)(2,1)S(1)}, u32[]{:S(2)}, u32[]{:S(2)}) collective-permute-start(bf16[64,512]{1,0:T(8,128)(2,1)S(1)} %project.6), channel_id=1, source_target_pairs={{0,8},{4,12},{8,0},{12,4},{1,9},{5,13},{9,1},{13,5},{2,10},{6,14},... | collective-permute-start | bytes 196616 | tf_op jit(solution)/shard_map/ppermute | solution.py:18
  33.2 4.7 %collective-permute-start.5 = (bf16[64,512]{1,0:T(8,128)(2,1)S(1)}, bf16[64,512]{1,0:T(8,128)(2,1)S(1)}, u32[]{:S(2)}, u32[]{:S(2)}) collective-permute-start(bf16[64,512]{1,0:T(8,128)(2,1)S(1)} %project.5), channel_id=1, source_target_pairs={{0,12},{4,0},{8,4},{12,8},{1,13},{5,1},{9,5},{13,9},{2,14},{6,2},{... | collective-permute-start | bytes 196616 | tf_op jit(solution)/shard_map/ppermute | solution.py:18
  40.8 4.0 %collective-permute-start.12 = (bf16[144,128]{1,0:T(8,128)(2,1)S(1)}, bf16[144,128]{1,0:T(8,128)(2,1)S(1)}, u32[]{:S(2)}, u32[]{:S(2)}) collective-permute-start(bf16[144,128]{1,0:T(8,128)(2,1)S(1)} %get-tuple-element.16), channel_id=1, source_target_pairs={{0,12},{4,0},{8,4},{12,8},{1,13},{5,1},{9,5},{13,9},{2,14},{6,2},{... | collective-permute-start | bytes 110600 | tf_op jit(solution)/shard_map/ppermute | solution.py:18
  43.1 4.9 %collective-permute-start.13 = (bf16[144,128]{1,0:T(8,128)(2,1)S(1)}, bf16[144,128]{1,0:T(8,128)(2,1)S(1)}, u32[]{:S(2)}, u32[]{:S(2)}) collective-permute-start(bf16[144,128]{1,0:T(8,128)(2,1)S(1)} %get-tuple-element.17), channel_id=1, source_target_pairs={{0,8},{4,12},{8,0},{12,4},{1,9},{5,13},{9,1},{13,5},{2,10},{6,14},... | collective-permute-start | bytes 110600 | tf_op jit(solution)/shard_map/ppermute | solution.py:18
  43.4 5.8 %collective-permute-start.14 = (bf16[144,128]{1,0:T(8,128)(2,1)S(1)}, bf16[144,128]{1,0:T(8,128)(2,1)S(1)}, u32[]{:S(2)}, u32[]{:S(2)}) collective-permute-start(bf16[144,128]{1,0:T(8,128)(2,1)S(1)} %get-tuple-element.18), channel_id=1, source_target_pairs={{0,4},{4,8},{8,12},{12,0},{1,5},{5,9},{9,13},{13,1},{2,6},{6,10},{... | collective-permute-start | bytes 110600 | tf_op jit(solution)/shard_map/ppermute | solution.py:18
  49.3 5.8 %collective-permute-start.15 = (bf16[8,2048]{1,0:T(8,128)(2,1)S(1)}, bf16[8,2048]{1,0:T(8,128)(2,1)S(1)}, u32[]{:S(2)}, u32[]{:S(2)}) collective-permute-start(bf16[8,2048]{1,0:T(8,128)(2,1)S(1)} %merge.1.refs_1_), channel_id=1, source_target_pairs={{0,4},{4,8},{8,12},{12,0},{1,5},{5,9},{9,13},{13,1},{2,6},{6,10},{... | collective-permute-start | bytes 98312 | tf_op jit(solution)/shard_map/ppermute | solution.py:18
  49.4 5.7 %collective-permute-start.16 = (bf16[8,2048]{1,0:T(8,128)(2,1)S(1)}, bf16[8,2048]{1,0:T(8,128)(2,1)S(1)}, u32[]{:S(2)}, u32[]{:S(2)}) collective-permute-start(bf16[8,2048]{1,0:T(8,128)(2,1)S(1)} %merge.1.refs_1_), channel_id=1, source_target_pairs={{0,8},{4,12},{8,0},{12,4},{1,9},{5,13},{9,1},{13,5},{2,10},{6,14},... | collective-permute-start | bytes 98312 | tf_op jit(solution)/shard_map/ppermute | solution.py:18
  50.3 5.3 %collective-permute-start.17 = (bf16[8,2048]{1,0:T(8,128)(2,1)S(1)}, bf16[8,2048]{1,0:T(8,128)(2,1)S(1)}, u32[]{:S(2)}, u32[]{:S(2)}) collective-permute-start(bf16[8,2048]{1,0:T(8,128)(2,1)S(1)} %merge.1.refs_1_), channel_id=1, source_target_pairs={{0,12},{4,0},{8,4},{12,8},{1,13},{5,1},{9,5},{13,9},{2,14},{6,2},{... | collective-permute-start | bytes 98312 | tf_op jit(solution)/shard_map/ppermute | solution.py:18
  55.6 3.4 %copy-start.3 = (bf16[2048,2048]{1,0:T(8,128)(2,1)S(1)}, bf16[2048,2048]{1,0:T(8,128)(2,1)}, u32[]{:S(2)}) copy-start(bf16[2048,2048]{1,0:T(8,128)(2,1)} %refs_5_.1) | copy-start | bytes 25165828
  60.6 1.3 %collective-permute-start.18 = (bf16[2,8,2048]{2,1,0:T(8,128)(2,1)S(1)}, bf16[2,8,2048]{2,1,0:T(8,128)(2,1)S(1)}, u32[]{:S(2)}, u32[]{:S(2)}) collective-permute-start(bf16[2,8,2048]{2,1,0:T(8,128)(2,1)S(1)} %fusion), channel_id=1, source_target_pairs={{0,1},{1,0},{2,3},{3,2},{4,5},{5,4},{6,7},{7,6},{8,9},{9,8},{10,11... | collective-permute-start | bytes 196616 | tf_op jit(solution)/shard_map/ppermute | solution.py:18
  61.9 4.0 %collective-permute-start.19 = (bf16[8,2048]{1,0:T(8,128)(2,1)S(1)}, bf16[8,2048]{1,0:T(8,128)(2,1)S(1)}, u32[]{:S(2)}, u32[]{:S(2)}) collective-permute-start(bf16[8,2048]{1,0:T(8,128)(2,1)S(1)} %fusion.2), channel_id=1, source_target_pairs={{0,2},{2,0},{1,3},{3,1},{4,6},{6,4},{5,7},{7,5},{8,10},{10,8},{9,1... | collective-permute-start | bytes 98312 | tf_op jit(solution)/shard_map/ppermute | solution.py:18

commit v3 on v0

v3 whole, which is shorter than its diff:
```python
import functools

import jax
import jax.numpy as jnp
from jax import lax
from jax.experimental import pallas as pl
from jax.experimental.pallas import tpu as pltpu
from jax.sharding import PartitionSpec as P


masked_score = -1e30
norm_epsilon = 1e-05
bf16 = jnp.bfloat16
f32 = jnp.float32


def shifted(part, axis, by):
    peers = lax.axis_size(axis)
    return lax.ppermute(part, axis, [(i, (i + by) % peers) for i in range(peers)])


def block_at(array, index, axis=0):
    return lax.dynamic_index_in_dim(array, index, axis, keepdims=False)


def summed_rows(partial, axis):
    peers = lax.axis_size(axis)
    me = lax.axis_index(axis)
    total = block_at(partial, me)
    for by in range(1, peers):
        piece = block_at(partial, (me + by) % peers).astype(bf16)
        total = total + shifted(piece, axis, by).astype(f32)
    return total


vmem = pl.BlockSpec(memory_space=pltpu.VMEM)
hbm = pl.BlockSpec(memory_space=pltpu.HBM)


def call(body, outs, flops, moved, n_in, scratch=(), limit=None):
    return pl.pallas_call(
        body,
        out_shape=outs,
        in_specs=[vmem] * n_in,
        out_specs=jax.tree.map(lambda _: vmem, outs),
        scratch_shapes=list(scratch),
        cost_estimate=pl.CostEstimate(flops=flops, bytes_accessed=moved, transcendentals=0),
        compiler_params=pltpu.CompilerParams(vmem_limit_bytes=limit or (16 << 20)),
    )


def project_body(halves, blocks, *refs):
    row_refs, (key_ref, value_ref) = refs[:halves], refs[halves : halves + 2]
    extra_refs, out_ref = refs[halves + 2 : -1], refs[-1]
    rows = jnp.concatenate([ref[...] for ref in row_refs], axis=0)
    count = rows.shape[0]
    depth = out_ref.shape[1]
    kv = blocks // 2
    for i, ref in enumerate((key_ref, value_ref)):
        part = jnp.dot(rows, ref[...], preferred_element_type=f32).astype(out_ref.dtype)
        for c in range(kv):
            at = (i * kv + c) * count
            out_ref[at : at + count, :] = part[:, c * depth : (c + 1) * depth]
    for ref in extra_refs:
        out_ref[blocks * count :, :] = ref[...]


def prepare_body(pieces, *refs):
    feature_ref, query_ref, length_ref, frame_ref = refs[:4]
    piece_refs, message_ref = refs[4 : 4 + pieces], refs[4 + pieces]
    query_in, length_in, frame_in, query_wide, sems = refs[5 + pieces :]
    half_rows, depth = piece_refs[0].shape
    seq_size = pieces + 1
    rows = pl.ds(pl.multiple_of(lax.axis_index("head") * half_rows, half_rows), half_rows)
    copies = []
    for i, (source, target) in enumerate(
        ((query_ref, query_in), (length_ref, length_in), (frame_ref, frame_in))
    ):
        copies.append(pltpu.make_async_copy(source, target, sems.at[i]))
    for by, target in enumerate(piece_refs):
        at = lax.rem(lax.axis_index("seq") + (by + 1), seq_size)
        source = feature_ref.at[rows, pl.ds(pl.multiple_of(at * depth, depth), depth)]
        copies.append(pltpu.make_async_copy(source, target, sems.at[3 + by]))
    for copy in copies:
        copy.start()
    for copy in copies[:3]:
        copy.wait()
    text_rows = frame_in.shape[1]
    query_rows = query_in.shape[0]
    heads = query_rows // text_rows
    frames = length_in.shape[1]
    column = as_column(frame_in[...].astype(f32), diagonal(text_rows)).astype(jnp.int32)
    index = lax.broadcasted_iota(jnp.int32, (text_rows, frames), 1)
    seen = jnp.where(index <= column, length_in[...].astype(f32), 0.0)
    limit = jnp.sum(seen, axis=1, keepdims=True).astype(jnp.int32)
    lane = lax.broadcasted_iota(jnp.int32, (text_rows, query_in.shape[1]), 1)
    digits = jnp.where(lane == 0, limit & 255, 0)
    digits = jnp.where(lane == 1, (limit >> 8) & 255, digits)
    digits = jnp.where(lane == 2, limit >> 16, digits).astype(f32)
    blank = jnp.zeros((16 - text_rows, digits.shape[1]), f32)
    message_ref[query_rows:, :] = jnp.concatenate((digits, blank), axis=0).astype(bf16)
    query_wide[...] = query_in[...].astype(f32)
    for head in range(0, heads, 2):
        pair = [query_wide[pl.ds(head + i, text_rows, stride=heads), :] for i in range(2)]
        message_ref[head * text_rows : (head + 2) * text_rows, :] = jnp.concatenate(
            pair, axis=0
        ).astype(bf16)
    for copy in copies[3:]:
        copy.wait()


def own_body(blocks, *refs):
    feature_ref, *sources = refs[:4]
    *targets, term_ref, rows_ref, sems = refs[4:]
    depth = rows_ref.shape[1]
    columns = pl.ds(pl.multiple_of(lax.axis_index("seq") * depth, depth), depth)
    copies = [pltpu.make_async_copy(feature_ref.at[:, columns], rows_ref, sems.at[0])]
    for i in range(3):
        copies.append(pltpu.make_async_copy(sources[i], targets[i], sems.at[1 + i]))
    for copy in copies:
        copy.start()
    for copy in copies[:3]:
        copy.wait()
    project_body(1, blocks, rows_ref, targets[0], targets[1], term_ref)
    copies[3].wait()


def row_limits(message_refs, text_rows, query_rows, group):
    columns = []
    for ref in message_refs:
        digits = ref[query_rows:, :].astype(f32)[:text_rows]
        limit = digits[:, 0:1] + 256.0 * digits[:, 1:2] + 65536.0 * digits[:, 2:3]
        columns.extend([limit] * group)
    return jnp.concatenate(columns, axis=0).astype(jnp.int32)


def diagonal(size):
    shape = (size, size)
    return lax.broadcasted_iota(jnp.int32, shape, 0) == lax.broadcasted_iota(jnp.int32, shape, 1)


def store_logs(out_ref, start, query_rows, log):
    depth = out_ref.shape[1]
    if log.shape[1] < depth:
        log = jnp.concatenate((log, jnp.zeros((1, depth - log.shape[1]), f32)), axis=1)
    high = log.astype(bf16).astype(f32)
    middle = (log - high).astype(bf16).astype(f32)
    low = log - high - middle
    pieces = jnp.concatenate((high, middle, low, jnp.zeros((13, depth), f32)), axis=0)
    out_ref[start + query_rows :, :] = pieces.astype(bf16)


def read_logs(message, query_rows):
    pieces = message[query_rows:].astype(f32)
    return (pieces[0:1] + pieces[1:2] + pieces[2:3])[:, :query_rows]


def as_column(row, on_diagonal):
    return jnp.sum(jnp.where(on_diagonal, row, 0.0), axis=1, keepdims=True)


def cached_body(blocks, text_rows, kv, scale, block_keys, *refs):
    message_refs = refs[:blocks]
    key_ref, value_ref = refs[blocks : 2 + blocks]
    out_refs = refs[2 + blocks :]
    depth = message_refs[0].shape[1]
    query_rows = message_refs[0].shape[0] - 16
    unit = query_rows // kv
    group = unit // text_rows
    keys = key_ref.shape[0]
    step = min(blocks, 4)
    position = lax.broadcasted_iota(jnp.int32, (step * unit, keys), 1) + lax.axis_index("seq") * block_keys
    on_diagonal = diagonal(unit)
    for start in range(0, blocks, step):
        some = message_refs[start : start + step]
        visible = position < row_limits(some, text_rows, query_rows, group)
        logs = [[] for _ in some]
        for c in range(kv):
            query = jnp.concatenate([ref[c * unit : (c + 1) * unit, :] for ref in some], axis=0)
            lanes = slice(c * depth, (c + 1) * depth)
            scores = lax.dot_general(
                query, key_ref[:, lanes], (((1,), (1,)), ((), ())), preferred_element_type=f32
            ) * scale
            scores = jnp.where(visible, scores, masked_score)
            peak = jnp.max(scores, axis=1, keepdims=True)
            weights = jnp.where(visible, jnp.exp(scores - peak), 0.0)
            total = jnp.sum(weights, axis=1, keepdims=True)
            summed = jnp.dot(weights.astype(bf16), value_ref[:, lanes], preferred_element_type=f32)
            some_seen = total > 0.0
            safe = jnp.where(some_seen, total, 1.0)
            mean = (summed / safe).astype(bf16)
            log = jnp.where(some_seen, peak + jnp.log(safe), masked_score)
            for i in range(len(some)):
                rows = slice(i * unit, (i + 1) * unit)
                out_refs[start + i][c * unit : (c + 1) * unit, :] = mean[rows]
                logs[i].append(
                    jnp.sum(jnp.where(on_diagonal, log[rows], 0.0), axis=0, keepdims=True)
                )
        for i in range(len(some)):
            store_logs(out_refs[start + i], 0, query_rows, jnp.concatenate(logs[i], axis=1))


def owner_body(kv, halves, own_ref, gain_ref, mine_ref, *refs):
    term_refs, out_ref = refs[:-1], refs[-1]
    fresh_rows = own_ref.shape[0]
    count = fresh_rows // (2 * kv)
    query_rows = mine_ref.shape[0] - 16
    half = count // halves
    for c in range(2 * kv):
        at = slice(c * count, (c + 1) * count)
        raw = functools.reduce(jnp.add, [ref[at, :].astype(f32) for ref in term_refs])
        turned = raw
        for turn in range(1, halves):
            other = jnp.concatenate((raw[-turn * half :], raw[: -turn * half]), axis=0)
            turned = jnp.where(lax.axis_index("head") == turn, other, turned)
        raw = turned + own_ref[at, :]
        if c < kv:
            mean_square = jnp.mean(raw * raw, axis=1, keepdims=True)
            raw = raw * lax.rsqrt(mean_square + norm_epsilon) * gain_ref[...]
        out_ref[at, :] = raw.astype(bf16)
    messages = [mine_ref[...]] + [ref[fresh_rows:, :] for ref in term_refs]
    on_diagonal = diagonal(query_rows)
    logs = [read_logs(message, query_rows) for message in messages]
    top = functools.reduce(jnp.maximum, logs)
    shares = [jnp.exp(log - top) for log in logs]
    whole = functools.reduce(jnp.add, shares)
    merged = None
    for share, message in zip(shares, messages):
        term = as_column(share / whole, on_diagonal) * message[:query_rows].astype(f32)
        merged = term if merged is None else merged + term
    out_ref[fresh_rows : fresh_rows + query_rows, :] = merged.astype(bf16)
    store_logs(out_ref, fresh_rows, query_rows, top + jnp.log(whole))


def final_body(blocks, text_rows, kv, scale, block_keys, heads, sections, *refs):
    message_refs = refs[:blocks]
    fresh_refs = refs[blocks : 2 * blocks]
    weight_ref, sent_ref, kept_ref, rows_ref, product_ref = refs[2 * blocks :]
    depth = message_refs[0].shape[1]
    query_rows = message_refs[0].shape[0] - 16
    unit = query_rows // kv
    group = unit // text_rows
    fresh_rows = fresh_refs[0].shape[0] - query_rows - 16
    keys = fresh_rows // (2 * kv)
    me = lax.axis_index("seq")
    places = [lax.rem(me + (blocks - by), blocks) for by in range(blocks)]
    columns = lax.broadcasted_iota(jnp.int32, (1, keys), 1) + (block_keys - keys)
    position = jnp.concatenate([columns + place * block_keys for place in places], axis=1)
    on_diagonal = diagonal(query_rows)
    step = min(blocks, 4)
    for start in range(0, blocks, step):
        span = range(start, start + step)
        some = [message_refs[i] for i in span]
        visible = position < row_limits(some, text_rows, query_rows, group)
        logs = [
            as_column(read_logs(fresh_refs[i][fresh_rows:, :], query_rows), on_diagonal) for i in span
        ]
        for c in range(kv):
            part = slice(c * unit, (c + 1) * unit)
            key_part = slice(c * keys, (c + 1) * keys)
            value_part = slice((kv + c) * keys, (kv + c + 1) * keys)
            query = jnp.concatenate([ref[part, :] for ref in some], axis=0)
            key = jnp.concatenate([ref[key_part, :] for ref in fresh_refs], axis=0)
            value = jnp.concatenate([ref[value_part, :] for ref in fresh_refs], axis=0)
            scores = lax.dot_general(
                query, key, (((1,), (1,)), ((), ())), preferred_element_type=f32
            ) * scale
            scores = jnp.where(visible, scores, masked_score)
            old_log = jnp.concatenate([log[part] for log in logs], axis=0)
            peak = jnp.maximum(jnp.max(scores, axis=1, keepdims=True), old_log)
            weights = jnp.where(visible, jnp.exp(scores - peak), 0.0)
            share = jnp.exp(old_log - peak)
            total = share + jnp.sum(weights, axis=1, keepdims=True)
            old_part = slice(fresh_rows + c * unit, fresh_rows + (c + 1) * unit)
            old = jnp.concatenate([fresh_refs[i][old_part, :] for i in span], axis=0).astype(f32)
            summed = share * old + jnp.dot(
                weights.astype(bf16), value, preferred_element_type=f32
            )
            attended = summed / total
            for i in span:
                at = pl.ds(pl.multiple_of(places[i] * text_rows, text_rows), text_rows)
                for g in range(group):
                    row = (i - start) * unit + g * text_rows
                    col = (c * group + g) * depth
                    rows_ref[at, col : col + depth] = attended[row : row + text_rows]
    rows = rows_ref[...].astype(bf16)
    product_ref[...] = jnp.dot(rows, weight_ref[...], preferred_element_type=f32)
    count = product_ref.shape[0] // (heads * sections)
    mine = lax.axis_index("head")
    for s in range(sections):
        here = slice(s * count, (s + 1) * count)
        keep_at = pl.multiple_of((s * heads + mine) * count, count)
        kept_ref[here, :] = product_ref[pl.ds(keep_at, count), :]
        for by in range(1, heads):
            to = lax.rem(mine + by, heads)
            send_at = pl.multiple_of((s * heads + to) * count, count)
            there = slice(((by - 1) * sections + s) * count, ((by - 1) * sections + s + 1) * count)
            sent_ref[there, :] = product_ref[pl.ds(send_at, count), :].astype(bf16)


def on_device(
    queries,
    key_cache,
    value_cache,
    new_features,
    key_weight,
    value_weight,
    key_gain,
    out_weight,
    frame_length,
    text_frame,
):
    cached_rows, local_kv, head_depth = key_cache.shape
    kv_width = key_weight.shape[1]
    depth = key_weight.shape[0]
    new_rows = new_features.shape[0]
    text_rows, local_heads, _ = queries.shape
    query_rows = text_rows * local_heads
    seq_size = lax.axis_size("seq")
    head_size = lax.axis_size("head")
    section_size = lax.axis_size("section")
    half_rows = new_rows // head_size
    sds = jax.ShapeDtypeStruct

    pieces = seq_size - 1
    prepare = pl.pallas_call(
        functools.partial(prepare_body, pieces),
        out_shape=(sds((half_rows, depth), bf16),) * pieces
        + (sds((query_rows + 16, head_depth), bf16),),
        in_specs=[hbm] * 4,
        out_specs=(vmem,) * seq_size,
        scratch_shapes=[
            pltpu.VMEM((query_rows, head_depth), bf16),
            pltpu.VMEM((1, frame_length.shape[0]), jnp.int32),
            pltpu.VMEM((1, text_rows), jnp.int32),
            pltpu.VMEM((query_rows, head_depth), f32),
            pltpu.SemaphoreType.DMA((pieces + 3,)),
        ],
        name="prepare",
        cost_estimate=pl.CostEstimate(
            flops=0, bytes_accessed=8 * half_rows * depth, transcendentals=0
        ),
        compiler_params=pltpu.CompilerParams(vmem_limit_bytes=8 << 20),
    )
    sources = (
        new_features,
        queries.reshape(query_rows, head_depth),
        frame_length.reshape(1, -1),
        text_frame.reshape(1, -1),
    )
    *sent_pieces, message = prepare(
        *[pltpu.with_memory_space_constraint(w, pltpu.HBM) for w in sources],
    )
    arrived = [shifted(part, "seq", by + 1) for by, part in enumerate(sent_pieces)]
    messages = [message] + [shifted(message, "seq", by) for by in range(1, seq_size)]

    key_cache = key_cache.reshape(cached_rows, kv_width)
    value_cache = value_cache.reshape(cached_rows, kv_width)
    flops = 4 * new_rows * depth * kv_width

    kv_blocks = 2 * local_kv

    def project(rows, dtype, extra=()):
        extra_rows = sum(part.shape[0] for part in extra)
        return call(
            functools.partial(project_body, len(rows), kv_blocks),
            sds((kv_blocks * new_rows + extra_rows, head_depth), dtype),
            flops,
            4 * depth * kv_width,
            len(rows) + 2 + len(extra),
        )(*rows, key_weight, value_weight, *extra)

    sources = (new_features, key_weight, value_weight, out_weight)
    load = pl.pallas_call(
        functools.partial(own_body, kv_blocks),
        out_shape=(
            *(sds(w.shape, bf16) for w in sources[1:]),
            sds((kv_blocks * new_rows, head_depth), f32),
        ),
        in_specs=[hbm] * 4,
        out_specs=(vmem,) * 4,
        scratch_shapes=[pltpu.VMEM((new_rows, depth), bf16), pltpu.SemaphoreType.DMA((4,))],
        name="own",
        cost_estimate=pl.CostEstimate(
            flops=flops, bytes_accessed=4 * sum(w.size for w in sources[1:]), transcendentals=0
        ),
        compiler_params=pltpu.CompilerParams(vmem_limit_bytes=16 << 20),
    )
    sources = [pltpu.with_memory_space_constraint(w, pltpu.HBM) for w in sources]
    key_weight, value_weight, out_weight, own_term = load(*sources)

    score_scale = head_depth ** (-0.5)
    block_keys = cached_rows + new_rows
    attend_flops = 4 * seq_size * query_rows * head_depth * cached_rows
    message_shape = sds(message.shape, bf16)
    attend_cached = call(
        functools.partial(cached_body, seq_size, text_rows, local_kv, score_scale, block_keys),
        (message_shape,) * seq_size,
        attend_flops,
        4 * cached_rows * kv_width,
        seq_size + 2,
        limit=24 << 20,
    )
    cached = attend_cached(*messages, key_cache, value_cache)
    terms = []
    for by, half in enumerate(arrived):
        halves = [half] + [shifted(half, "head", head_size - turn) for turn in range(1, head_size)]
        term = project(halves, bf16, (cached[by + 1],))
        terms.append(shifted(term, "seq", seq_size - (by + 1)))
    fresh_rows = kv_blocks * new_rows
    fresh = call(
        functools.partial(owner_body, local_kv, head_size),
        sds((fresh_rows + query_rows + 16, head_depth), bf16),
        8 * new_rows * kv_width,
        4 * seq_size * new_rows * kv_width,
        seq_size + 2,
    )(
        own_term,
        key_gain.reshape(1, head_depth),
        cached[0],
        *terms,
    )
    fresh_all = [fresh] + [shifted(fresh, "seq", by) for by in range(1, seq_size)]
    made = fresh[:fresh_rows].reshape(2, local_kv, new_rows, head_depth)
    new_keys, new_values = (jnp.swapaxes(part, 0, 1) for part in made)

    all_rows = seq_size * text_rows
    out_width = out_weight.shape[1]
    out_rows = all_rows // (section_size * head_size)
    sent, kept = call(
        functools.partial(
            final_body,
            seq_size,
            text_rows,
            local_kv,
            score_scale,
            block_keys,
            head_size,
            section_size,
        ),
        (
            sds(((head_size - 1) * section_size * out_rows, out_width), bf16),
            sds((section_size * out_rows, out_width), f32),
        ),
        2 * all_rows * out_weight.size,
        2 * out_weight.size,
        2 * seq_size + 1,
        scratch=[
            pltpu.VMEM((all_rows, local_heads * head_depth), f32),
            pltpu.VMEM((all_rows, out_width), f32),
        ],
        limit=24 << 20,
    )(
        *messages,
        *fresh_all,
        out_weight,
    )
    sent = sent.reshape(head_size - 1, section_size * out_rows, out_width)
    for by in range(1, head_size):
        kept = kept + shifted(sent[by - 1], "head", by).astype(f32)
    layer_output = summed_rows(kept.reshape(section_size, out_rows, out_width), "section")
    return (layer_output.astype(bf16), new_keys, new_values)


def solution(mesh):
    placed = (
        P(("groups", "seq"), ("section", "head"), None),
        P(("groups", "seq"), ("section", "head"), None),
        P(("groups", "seq"), ("section", "head"), None),
        P(("groups", "seq"), None),
        P("seq", ("section", "head")),
        P("seq", ("section", "head")),
        P(),
        P(("section", "head"), "seq"),
        P("groups"),
        P(("groups", "seq")),
    )
    return jax.shard_map(
        on_device,
        mesh=mesh,
        in_specs=placed,
        out_specs=(
            P(("groups", "section", "head"), "seq"),
            P(("groups", "seq"), ("section", "head"), None),
            P(("groups", "seq"), ("section", "head"), None),
        ),
        check_vma=False,
    )
```

time: 144 us -> 61.9 us (0.43)
  waiting for transfers between devices: 84 us -> 21.2 us
  between operations: 14.3 us -> 0.78 us
  blocking collectives: 13.3 us -> 0 us
  Pallas kernels: 0 us -> 11.7 us
  starting transfers between devices: 15.2 us -> 24.2 us
  matrix products: 8.47 us -> 0 us
  other arithmetic: 2.99 us -> 0.64 us
  local copies, waits for them, and re-layouts: 5.37 us -> 3.16 us
    reduce_scatter x2 -> x0, waiting for transfers between devices: 24.3 us -> none  [the longest x1 17.3 us: on_device(): lax.psum_scatter(partial_terms.astype(jnp.bfloat16), ('section', 'head'),...]
    all_to_all x1 -> x0, waiting for transfers between devices: 22.7 us -> none  [on_device(): lax.all_to_all(new_features, 'seq', split_axis=1, concat_axis=0, tiled=True)]
    ppermute x17, waiting for transfers between devices: 36.9 us -> 21.2 us  [shifted(): lax.ppermute(part, axis, [(i, (i + by) % peers) for i in range(peers)])]
    ppermute x17, starting transfers between devices: 8.83 us -> 24.2 us  [shifted(): lax.ppermute(part, axis, [(i, (i + by) % peers) for i in range(peers)])]
    all_gather x1 -> x0, blocking collectives: 13.3 us -> none  [on_device(): lax.all_gather(attended, 'seq', axis=0, tiled=True)]
    pallas_call x0 -> x8, Pallas kernels: none -> 11.7 us  [the longest x1 4.16 us: on_device(): key_weight, value_weight, out_weight, own_term = load(*sources)]
    dot_general x10 -> x0, matrix products: 8.47 us -> none  [the longest x1 2.38 us: on_device(): jnp.dot(spread, stacked_weight, preferred_element_type=jnp.float32)]
    all_to_all x1 -> x0, starting transfers between devices: 6.35 us -> none  [on_device(): lax.all_to_all(new_features, 'seq', split_axis=1, concat_axis=0, tiled=True)]
  transfers between devices with their start and end apart: 20 -> 17, of which waited for: 13 -> 9; matrix products, arithmetic and copies ran while one was open for 8% -> 5% of each run, Pallas kernels for 0% -> 13%
where the time goes in v3:
time: 61.9 us; the launch traced here: 61.7 us
  starting transfers between devices  24.2 us (39%)
  waiting for transfers between devices  21.2 us (34%)
  Pallas kernels  11.7 us (19%)
  local copies, waits for them, and re-layouts  3.16 us (5%)
  between operations  0.78 us (1%)
  other arithmetic  0.64 us (1%)
    ppermute x17, starting transfers between devices, shifted(): lax.ppermute(part, axis, [(i, (i + by) % peers) for i in range(peers)])  24.2 us
    ppermute x17, waiting for transfers between devices, shifted(): lax.ppermute(part, axis, [(i, (i + by) % peers) for i in range(peers)])  21.2 us
    pallas_call x1, Pallas kernels, on_device(): key_weight, value_weight, out_weight, own_term = load(*sources)  4.16 us
    pallas_call x1, Pallas kernels, on_device(): call(functools.partial(final_body, seq_size, text_rows, local_kv, score_s...  2.48 us
    pallas_call x1, Pallas kernels, on_device(): cached = attend_cached(*messages, key_cache, value_cache)  2.29 us
    reshape x1, local copies, waits for them, and re-layouts, on_device(): value_cache = value_cache.reshape(cached_rows, kv_width)  1.84 us
    pallas_call x3, Pallas kernels, project(): call(functools.partial(project_body, len(rows), kv_blocks), sds((kv_block...  1.44 us
    another operation x3, local copies, waits for them, and re-layouts, on_device(): new_keys, new_values = (jnp.swapaxes(part, 0, 1) for part in made)  1.3 us
  transfers between devices with their start and end apart: 17, of which 9 were waited for; matrix products, arithmetic and copies ran while one was open for 5% of the time, Pallas kernels for 13%

profile of v3, /device:TPU:0, one launch (start us, length us, event | category | flops | bytes accessed | tf_op | source)
XLA Modules:
  0.0 61.7 jit_solution(6257575456039631580)
XLA Ops:
  0.6 1.1 %prepare.1 = (bf16[32,2048]{1,0:T(8,128)(2,1)S(1)}, bf16[32,2048]{1,0:T(8,128)(2,1)S(1)}, bf16[32,2048]{1,0:T(8,128)(2,1)S(1)}, bf16[144,128]{1,0:T(8,128)(2,1)S(1)}) custom-call(bf16[64,8192]{1,0:T(8,128)(2,1)} %refs_0_.3, bf16[128,128]{1,0:T(8,128)(2,1)} %bitcast.31, s32[1,64]{1,0:T(1,128)} %bitcast.34, s32[1,8]{1,0:T(1,128)} %bitcast.35), custom_call_target="tpu_custom_call" | custom-call | bytes 524288 | tf_op jit(solution)/shard_map/prepare/pallas_call | solution.py:351
  1.8 5.1 %collective-permute-start.9 = (bf16[32,2048]{1,0:T(8,128)(2,1)S(1)}, bf16[32,2048]{1,0:T(8,128)(2,1)S(1)}, u32[]{:S(2)}, u32[]{:S(2)}) collective-permute-start(bf16[32,2048]{1,0:T(8,128)(2,1)S(1)} %get-tuple-element.26), channel_id=1, source_target_pairs={{0,12},{4,0},{8,4},{12,8},{1,13},{5,1},{9,5},{13,9},{2,14},{6,2},{... | collective-permute-start | bytes 393224 | tf_op jit(solution)/shard_map/ppermute | solution.py:19
  6.9 0.0 collective-permute-start.6
  6.9 1.0 %collective-permute-start.3 = (bf16[32,2048]{1,0:T(8,128)(2,1)S(1)}, bf16[32,2048]{1,0:T(8,128)(2,1)S(1)}, u32[]{:S(2)}, u32[]{:S(2)}) collective-permute-start(bf16[32,2048]{1,0:T(8,128)(2,1)S(1)} %get-tuple-element.20), channel_id=1, source_target_pairs={{0,4},{4,8},{8,12},{12,0},{1,5},{5,9},{9,13},{13,1},{2,6},{6,10},{... | collective-permute-start | bytes 393224 | tf_op jit(solution)/shard_map/ppermute | solution.py:19
  7.9 2.5 %collective-permute-start = (bf16[144,128]{1,0:T(8,128)(2,1)S(1)}, bf16[144,128]{1,0:T(8,128)(2,1)S(1)}, u32[]{:S(2)}, u32[]{:S(2)}) collective-permute-start(bf16[144,128]{1,0:T(8,128)(2,1)S(1)} %get-tuple-element.17.refs_0_), channel_id=1, source_target_pairs={{0,4},{4,8},{8,12},{12,0},{1,5},{5,9},{9,13},{13,1},{2,6},{6,10},{... | collective-permute-start | bytes 110600 | tf_op jit(solution)/shard_map/ppermute | solution.py:19
  10.4 0.9 %collective-permute-start.1 = (bf16[144,128]{1,0:T(8,128)(2,1)S(1)}, bf16[144,128]{1,0:T(8,128)(2,1)S(1)}, u32[]{:S(2)}, u32[]{:S(2)}) collective-permute-start(bf16[144,128]{1,0:T(8,128)(2,1)S(1)} %get-tuple-element.17.refs_0_), channel_id=1, source_target_pairs={{0,8},{4,12},{8,0},{12,4},{1,9},{5,13},{9,1},{13,5},{2,10},{6,14},... | collective-permute-start | bytes 110600 | tf_op jit(solution)/shard_map/ppermute | solution.py:19
  11.3 6.2 %collective-permute-done.refs_1_ = bf16[144,128]{1,0:T(8,128)(2,1)S(1)} collective-permute-done((bf16[144,128]{1,0:T(8,128)(2,1)S(1)}, bf16[144,128]{1,0:T(8,128)(2,1)S(1)}, u32[]{:S(2)}, u32[]{:S(2)}) %collective-permute-start) | collective-permute-done | bytes 36896 | tf_op jit(solution)/shard_map/ppermute | solution.py:19
  17.5 2.0 %collective-permute-start.2 = (bf16[144,128]{1,0:T(8,128)(2,1)S(1)}, bf16[144,128]{1,0:T(8,128)(2,1)S(1)}, u32[]{:S(2)}, u32[]{:S(2)}) collective-permute-start(bf16[144,128]{1,0:T(8,128)(2,1)S(1)} %get-tuple-element.17.refs_0_), channel_id=1, source_target_pairs={{0,12},{4,0},{8,4},{12,8},{1,13},{5,1},{9,5},{13,9},{2,14},{6,2},{... | collective-permute-start | bytes 110600 | tf_op jit(solution)/shard_map/ppermute | solution.py:19
  19.5 0.0 collective-permute-done.9.refs_0_
  19.5 0.0 collective-permute-start.10
  19.5 0.6 collective-permute-done.6.refs_0_
  20.1 0.0 collective-permute-start.7
  20.1 0.0 collective-permute-done.3.refs_0_
  20.1 0.5 collective-permute-start.4
  20.6 1.8 %copy_bitcast_fusion = (bf16[1984,256]{1,0:T(8,128)(2,1)S(1)}, bf16[1984,256]{1,0:T(8,128)(2,1)S(1)}) fusion(bf16[248,8,2,128]{3,2,1,0:T(2,128)(2,1)} %bitcast.27, bf16[248,8,2,128]{3,2,1,0:T(2,128)(2,1)} %bitcast.28), kind=kLoop, calls=%fused_computation | loop fusion | bytes 4063232 | tf_op jit(solution)/shard_map/reshape | solution.py:358
  22.5 0.0 copy-start
  22.5 4.2 %own.1 = (bf16[2048,256]{1,0:T(8,128)(2,1)S(1)}, bf16[2048,256]{1,0:T(8,128)(2,1)S(1)}, bf16[2048,2048]{1,0:T(8,128)(2,1)S(1)}, f32[256,128]{1,0:T(8,128)S(1)}) custom-call(bf16[64,8192]{1,0:T(8,128)(2,1)} %refs_0_.3, bf16[2048,256]{1,0:T(8,128)(2,1)} %refs_1_.1, bf16[2048,256]{1,0:T(8,128)(2,1)} %refs_2_.1, bf16[2048,2048]{1,0:T(8,128)(2,1)} %refs_3_.1), custom_call_target="tpu_custom_call" | custom-call | flops 134217728 | bytes 20971520 | tf_op jit(solution)/shard_map/own/pallas_call | solution.py:390
  26.6 0.0 collective-permute-done.1.refs_2_
  26.6 0.0 collective-permute-done.2.refs_3_
  26.7 2.3 %shard_map.121 = (bf16[144,128]{1,0:T(8,128)(2,1)S(1)}, bf16[144,128]{1,0:T(8,128)(2,1)S(1)}, bf16[144,128]{1,0:T(8,128)(2,1)S(1)}, bf16[144,128]{1,0:T(8,128)(2,1)S(1)}) custom-call(bf16[144,128]{1,0:T(8,128)(2,1)S(1)} %get-tuple-element.17.refs_0_, bf16[144,128]{1,0:T(8,128)(2,1)S(1)} %collective-permute-done.refs_1_, ...), custom_call_target="tpu_custom_call" | custom-call | flops 520093696 | bytes 2031616 | tf_op jit(solution)/shard_map/pallas_call | solution.py:404
  28.9 0.0 collective-permute-done.10.refs_1_
  29.0 0.5 shard_map.124
  29.4 0.8 %collective-permute-start.11 = (bf16[400,128]{1,0:T(8,128)(2,1)S(1)}, bf16[400,128]{1,0:T(8,128)(2,1)S(1)}, u32[]{:S(2)}, u32[]{:S(2)}) collective-permute-start(bf16[400,128]{1,0:T(8,128)(2,1)S(1)} %shard_map.124), channel_id=1, source_target_pairs={{0,4},{4,8},{8,12},{12,0},{1,5},{5,9},{9,13},{13,1},{2,6},{6,10},{... | collective-permute-start | bytes 307208 | tf_op jit(solution)/shard_map/ppermute | solution.py:19
  30.3 0.0 collective-permute-done.7.refs_1_
  30.3 0.5 shard_map.123
  30.8 4.0 %collective-permute-start.8 = (bf16[400,128]{1,0:T(8,128)(2,1)S(1)}, bf16[400,128]{1,0:T(8,128)(2,1)S(1)}, u32[]{:S(2)}, u32[]{:S(2)}) collective-permute-start(bf16[400,128]{1,0:T(8,128)(2,1)S(1)} %shard_map.123), channel_id=1, source_target_pairs={{0,8},{4,12},{8,0},{12,4},{1,9},{5,13},{9,1},{13,5},{2,10},{6,14},... | collective-permute-start | bytes 307208 | tf_op jit(solution)/shard_map/ppermute | solution.py:19
  34.8 0.0 collective-permute-done.4.refs_1_
  34.8 0.5 shard_map.122
  35.3 1.0 %collective-permute-start.5 = (bf16[400,128]{1,0:T(8,128)(2,1)S(1)}, bf16[400,128]{1,0:T(8,128)(2,1)S(1)}, u32[]{:S(2)}, u32[]{:S(2)}) collective-permute-start(bf16[400,128]{1,0:T(8,128)(2,1)S(1)} %shard_map.122), channel_id=1, source_target_pairs={{0,12},{4,0},{8,4},{12,8},{1,13},{5,1},{9,5},{13,9},{2,14},{6,2},{... | collective-permute-start | bytes 307208 | tf_op jit(solution)/shard_map/ppermute | solution.py:19
  36.2 1.3 %collective-permute-done.11.refs_2_ = bf16[400,128]{1,0:T(8,128)(2,1)S(1)} collective-permute-done((bf16[400,128]{1,0:T(8,128)(2,1)S(1)}, bf16[400,128]{1,0:T(8,128)(2,1)S(1)}, u32[]{:S(2)}, u32[]{:S(2)}) %collective-permute-start.11) | collective-permute-done | bytes 102432 | tf_op jit(solution)/shard_map/ppermute | solution.py:19
  37.5 4.1 %collective-permute-done.8.refs_1_ = bf16[400,128]{1,0:T(8,128)(2,1)S(1)} collective-permute-done((bf16[400,128]{1,0:T(8,128)(2,1)S(1)}, bf16[400,128]{1,0:T(8,128)(2,1)S(1)}, u32[]{:S(2)}, u32[]{:S(2)}) %collective-permute-start.8) | collective-permute-done | bytes 102432 | tf_op jit(solution)/shard_map/ppermute | solution.py:19
  41.6 0.4 collective-permute-done.5.refs_0_
  42.1 0.0 copy-done
  42.1 0.2 shard_map.125.refs_4_
  42.3 2.3 %collective-permute-start.12 = (bf16[400,128]{1,0:T(8,128)(2,1)S(1)}, bf16[400,128]{1,0:T(8,128)(2,1)S(1)}, u32[]{:S(2)}, u32[]{:S(2)}) collective-permute-start(bf16[400,128]{1,0:T(8,128)(2,1)S(1)} %shard_map.125.refs_4_), channel_id=1, source_target_pairs={{0,4},{4,8},{8,12},{12,0},{1,5},{5,9},{9,13},{13,1},{2,6},{6,10},{... | collective-permute-start | bytes 307208 | tf_op jit(solution)/shard_map/ppermute | solution.py:19
  44.6 1.1 %collective-permute-start.13 = (bf16[400,128]{1,0:T(8,128)(2,1)S(1)}, bf16[400,128]{1,0:T(8,128)(2,1)S(1)}, u32[]{:S(2)}, u32[]{:S(2)}) collective-permute-start(bf16[400,128]{1,0:T(8,128)(2,1)S(1)} %shard_map.125.refs_4_), channel_id=1, source_target_pairs={{0,8},{4,12},{8,0},{12,4},{1,9},{5,13},{9,1},{13,5},{2,10},{6,14},... | collective-permute-start | bytes 307208 | tf_op jit(solution)/shard_map/ppermute | solution.py:19
  45.7 1.3 %collective-permute-start.14 = (bf16[400,128]{1,0:T(8,128)(2,1)S(1)}, bf16[400,128]{1,0:T(8,128)(2,1)S(1)}, u32[]{:S(2)}, u32[]{:S(2)}) collective-permute-start(bf16[400,128]{1,0:T(8,128)(2,1)S(1)} %shard_map.125.refs_4_), channel_id=1, source_target_pairs={{0,12},{4,0},{8,4},{12,8},{1,13},{5,1},{9,5},{13,9},{2,14},{6,2},{... | collective-permute-start | bytes 307208 | tf_op jit(solution)/shard_map/ppermute | solution.py:19
  47.0 2.9 %collective-permute-done.12.refs_5_ = bf16[400,128]{1,0:T(8,128)(2,1)S(1)} collective-permute-done((bf16[400,128]{1,0:T(8,128)(2,1)S(1)}, bf16[400,128]{1,0:T(8,128)(2,1)S(1)}, u32[]{:S(2)}, u32[]{:S(2)}) %collective-permute-start.12) | collective-permute-done | bytes 102432 | tf_op jit(solution)/shard_map/ppermute | solution.py:19
  50.0 3.3 %collective-permute-done.13.refs_6_ = bf16[400,128]{1,0:T(8,128)(2,1)S(1)} collective-permute-done((bf16[400,128]{1,0:T(8,128)(2,1)S(1)}, bf16[400,128]{1,0:T(8,128)(2,1)S(1)}, u32[]{:S(2)}, u32[]{:S(2)}) %collective-permute-start.13) | collective-permute-done | bytes 102432 | tf_op jit(solution)/shard_map/ppermute | solution.py:19
  53.3 0.0 collective-permute-done.14.refs_7_
  53.3 2.5 %shard_map.126 = (bf16[16,2048]{1,0:T(8,128)(2,1)S(1)}, f32[16,2048]{1,0:T(8,128)S(1)}) custom-call(bf16[144,128]{1,0:T(8,128)(2,1)S(1)} %get-tuple-element.17.refs_0_, bf16[144,128]{1,0:T(8,128)(2,1)S(1)} %collective-permute-done.refs_1_, bf16[144,128]{1,0:T(8,128)(2,1)S(1)} %collective-permute-done.1.refs_2_, ...), custom_call_target="tpu_custom_call" | custom-call | flops 268435456 | bytes 8388608 | tf_op jit(solution)/shard_map/pallas_call | solution.py:430
  55.7 0.1 collective-permute-start.15
  55.8 1.2 %collective-permute-done.15 = bf16[16,2048]{1,0:T(8,128)(2,1)S(1)} collective-permute-done((bf16[16,2048]{1,0:T(8,128)(2,1)S(1)}, bf16[16,2048]{1,0:T(8,128)(2,1)S(1)}, u32[]{:S(2)}, u32[]{:S(2)}) %collective-permute-start.15) | collective-permute-done | bytes 65568 | tf_op jit(solution)/shard_map/ppermute | solution.py:19
  57.1 1.6 %collective-permute-start.16 = (bf16[8,2048]{1,0:T(8,128)(2,1)S(1)}, bf16[8,2048]{1,0:T(8,128)(2,1)S(1)}, u32[]{:S(2)}, u32[]{:S(2)}) collective-permute-start(bf16[8,2048]{1,0:T(8,128)(2,1)S(1)} %fusion.1), channel_id=1, source_target_pairs={{0,2},{2,0},{1,3},{3,1},{4,6},{6,4},{5,7},{7,5},{8,10},{10,8},{9,1... | collective-permute-start | bytes 98312 | tf_op jit(solution)/shard_map/ppermute | solution.py:19
  58.7 0.6 %copy.21 = bf16[2,64,128]{2,0,1:T(2,128)(2,1)} copy(bf16[2,64,128]{2,1,0:T(8,128)(2,1)S(1)} %bitcast.30) | data formatting | bytes 65536 | tf_op jit(solution)/shard_map/unstack | solution.py:425
  59.3 0.6 %copy.22 = bf16[2,64,128]{2,0,1:T(2,128)(2,1)} copy(bf16[2,64,128]{2,1,0:T(8,128)(2,1)S(1)} %bitcast.29) | data formatting | bytes 65536 | tf_op jit(solution)/shard_map/unstack | solution.py:425
  60.0 1.1 %collective-permute-done.16 = bf16[8,2048]{1,0:T(8,128)(2,1)S(1)} collective-permute-done((bf16[8,2048]{1,0:T(8,128)(2,1)S(1)}, bf16[8,2048]{1,0:T(8,128)(2,1)S(1)}, u32[]{:S(2)}, u32[]{:S(2)}) %collective-permute-start.16) | collective-permute-done | bytes 32800 | tf_op jit(solution)/shard_map/ppermute | solution.py:19
  61.1 0.6 %fusion = bf16[8,2048]{1,0:T(8,128)(2,1)} fusion(bf16[8,2048]{1,0:T(8,128)(2,1)S(1)} %collective-permute-done.16, f32[2,8,2048]{2,1,0:T(8,128)S(1)} %add_bitcast_fusion, s32[]{:T(128)S(6)} %select_n.14), kind=kLoop, calls=%fused_computation.4 | loop fusion | flops 49152 | bytes 131076 | tf_op jit(solution)/shard_map/convert_element_type | solution.py:462
  (3 shorter events, 0.0 us)
Async XLA Ops:
  1.8 17.7 %collective-permute-start.9 = (bf16[32,2048]{1,0:T(8,128)(2,1)S(1)}, bf16[32,2048]{1,0:T(8,128)(2,1)S(1)}, u32[]{:S(2)}, u32[]{:S(2)}) collective-permute-start(bf16[32,2048]{1,0:T(8,128)(2,1)S(1)} %get-tuple-element.26), channel_id=1, source_target_pairs={{0,12},{4,0},{8,4},{12,8},{1,13},{5,1},{9,5},{13,9},{2,14},{6,2},{... | collective-permute-start | bytes 393224 | tf_op jit(solution)/shard_map/ppermute | solution.py:19
  6.9 13.2 %collective-permute-start.6 = (bf16[32,2048]{1,0:T(8,128)(2,1)S(1)}, bf16[32,2048]{1,0:T(8,128)(2,1)S(1)}, u32[]{:S(2)}, u32[]{:S(2)}) collective-permute-start(bf16[32,2048]{1,0:T(8,128)(2,1)S(1)} %get-tuple-element.24), channel_id=1, source_target_pairs={{0,8},{4,12},{8,0},{12,4},{1,9},{5,13},{9,1},{13,5},{2,10},{6,14},... | collective-permute-start | bytes 393224 | tf_op jit(solution)/shard_map/ppermute | solution.py:19
  6.9 13.2 %collective-permute-start.3 = (bf16[32,2048]{1,0:T(8,128)(2,1)S(1)}, bf16[32,2048]{1,0:T(8,128)(2,1)S(1)}, u32[]{:S(2)}, u32[]{:S(2)}) collective-permute-start(bf16[32,2048]{1,0:T(8,128)(2,1)S(1)} %get-tuple-element.20), channel_id=1, source_target_pairs={{0,4},{4,8},{8,12},{12,0},{1,5},{5,9},{9,13},{13,1},{2,6},{6,10},{... | collective-permute-start | bytes 393224 | tf_op jit(solution)/shard_map/ppermute | solution.py:19
  7.9 9.5 %collective-permute-start = (bf16[144,128]{1,0:T(8,128)(2,1)S(1)}, bf16[144,128]{1,0:T(8,128)(2,1)S(1)}, u32[]{:S(2)}, u32[]{:S(2)}) collective-permute-start(bf16[144,128]{1,0:T(8,128)(2,1)S(1)} %get-tuple-element.17.refs_0_), channel_id=1, source_target_pairs={{0,4},{4,8},{8,12},{12,0},{1,5},{5,9},{9,13},{13,1},{2,6},{6,10},{... | collective-permute-start | bytes 110600 | tf_op jit(solution)/shard_map/ppermute | solution.py:19
  10.4 16.2 %collective-permute-start.1 = (bf16[144,128]{1,0:T(8,128)(2,1)S(1)}, bf16[144,128]{1,0:T(8,128)(2,1)S(1)}, u32[]{:S(2)}, u32[]{:S(2)}) collective-permute-start(bf16[144,128]{1,0:T(8,128)(2,1)S(1)} %get-tuple-element.17.refs_0_), channel_id=1, source_target_pairs={{0,8},{4,12},{8,0},{12,4},{1,9},{5,13},{9,1},{13,5},{2,10},{6,14},... | collective-permute-start | bytes 110600 | tf_op jit(solution)/shard_map/ppermute | solution.py:19
  17.5 9.2 %collective-permute-start.2 = (bf16[144,128]{1,0:T(8,128)(2,1)S(1)}, bf16[144,128]{1,0:T(8,128)(2,1)S(1)}, u32[]{:S(2)}, u32[]{:S(2)}) collective-permute-start(bf16[144,128]{1,0:T(8,128)(2,1)S(1)} %get-tuple-element.17.refs_0_), channel_id=1, source_target_pairs={{0,12},{4,0},{8,4},{12,8},{1,13},{5,1},{9,5},{13,9},{2,14},{6,2},{... | collective-permute-start | bytes 110600 | tf_op jit(solution)/shard_map/ppermute | solution.py:19
  19.5 9.5 %collective-permute-start.10 = (bf16[32,2048]{1,0:T(8,128)(2,1)S(1)}, bf16[32,2048]{1,0:T(8,128)(2,1)S(1)}, u32[]{:S(2)}, u32[]{:S(2)}) collective-permute-start(bf16[32,2048]{1,0:T(8,128)(2,1)S(1)} %collective-permute-done.9.refs_0_), channel_id=1, source_target_pairs={{0,1},{1,0},{2,3},{3,2},{4,5},{5,4},{6,7},{7,6},{8,9},{9,8},{10,11... | collective-permute-start | bytes 393224 | tf_op jit(solution)/shard_map/ppermute | solution.py:19
  20.1 10.2 %collective-permute-start.7 = (bf16[32,2048]{1,0:T(8,128)(2,1)S(1)}, bf16[32,2048]{1,0:T(8,128)(2,1)S(1)}, u32[]{:S(2)}, u32[]{:S(2)}) collective-permute-start(bf16[32,2048]{1,0:T(8,128)(2,1)S(1)} %collective-permute-done.6.refs_0_), channel_id=1, source_target_pairs={{0,1},{1,0},{2,3},{3,2},{4,5},{5,4},{6,7},{7,6},{8,9},{9,8},{10,11... | collective-permute-start | bytes 393224 | tf_op jit(solution)/shard_map/ppermute | solution.py:19
  20.1 14.7 %collective-permute-start.4 = (bf16[32,2048]{1,0:T(8,128)(2,1)S(1)}, bf16[32,2048]{1,0:T(8,128)(2,1)S(1)}, u32[]{:S(2)}, u32[]{:S(2)}) collective-permute-start(bf16[32,2048]{1,0:T(8,128)(2,1)S(1)} %collective-permute-done.3.refs_0_), channel_id=1, source_target_pairs={{0,1},{1,0},{2,3},{3,2},{4,5},{5,4},{6,7},{7,6},{8,9},{9,8},{10,11... | collective-permute-start | bytes 393224 | tf_op jit(solution)/shard_map/ppermute | solution.py:19
  22.5 19.6 %copy-start = (f32[128]{0:T(128)S(1)}, f32[128]{0:T(128)}, u32[]{:S(2)}) copy-start(f32[128]{0:T(128)} %param.16) | copy-start | bytes 1540
  29.4 8.0 %collective-permute-start.11 = (bf16[400,128]{1,0:T(8,128)(2,1)S(1)}, bf16[400,128]{1,0:T(8,128)(2,1)S(1)}, u32[]{:S(2)}, u32[]{:S(2)}) collective-permute-start(bf16[400,128]{1,0:T(8,128)(2,1)S(1)} %shard_map.124), channel_id=1, source_target_pairs={{0,4},{4,8},{8,12},{12,0},{1,5},{5,9},{9,13},{13,1},{2,6},{6,10},{... | collective-permute-start | bytes 307208 | tf_op jit(solution)/shard_map/ppermute | solution.py:19
  30.8 10.9 %collective-permute-start.8 = (bf16[400,128]{1,0:T(8,128)(2,1)S(1)}, bf16[400,128]{1,0:T(8,128)(2,1)S(1)}, u32[]{:S(2)}, u32[]{:S(2)}) collective-permute-start(bf16[400,128]{1,0:T(8,128)(2,1)S(1)} %shard_map.123), channel_id=1, source_target_pairs={{0,8},{4,12},{8,0},{12,4},{1,9},{5,13},{9,1},{13,5},{2,10},{6,14},... | collective-permute-start | bytes 307208 | tf_op jit(solution)/shard_map/ppermute | solution.py:19
  35.3 6.8 %collective-permute-start.5 = (bf16[400,128]{1,0:T(8,128)(2,1)S(1)}, bf16[400,128]{1,0:T(8,128)(2,1)S(1)}, u32[]{:S(2)}, u32[]{:S(2)}) collective-permute-start(bf16[400,128]{1,0:T(8,128)(2,1)S(1)} %shard_map.122), channel_id=1, source_target_pairs={{0,12},{4,0},{8,4},{12,8},{1,13},{5,1},{9,5},{13,9},{2,14},{6,2},{... | collective-permute-start | bytes 307208 | tf_op jit(solution)/shard_map/ppermute | solution.py:19
  42.3 7.7 %collective-permute-start.12 = (bf16[400,128]{1,0:T(8,128)(2,1)S(1)}, bf16[400,128]{1,0:T(8,128)(2,1)S(1)}, u32[]{:S(2)}, u32[]{:S(2)}) collective-permute-start(bf16[400,128]{1,0:T(8,128)(2,1)S(1)} %shard_map.125.refs_4_), channel_id=1, source_target_pairs={{0,4},{4,8},{8,12},{12,0},{1,5},{5,9},{9,13},{13,1},{2,6},{6,10},{... | collective-permute-start | bytes 307208 | tf_op jit(solution)/shard_map/ppermute | solution.py:19
  44.6 8.7 %collective-permute-start.13 = (bf16[400,128]{1,0:T(8,128)(2,1)S(1)}, bf16[400,128]{1,0:T(8,128)(2,1)S(1)}, u32[]{:S(2)}, u32[]{:S(2)}) collective-permute-start(bf16[400,128]{1,0:T(8,128)(2,1)S(1)} %shard_map.125.refs_4_), channel_id=1, source_target_pairs={{0,8},{4,12},{8,0},{12,4},{1,9},{5,13},{9,1},{13,5},{2,10},{6,14},... | collective-permute-start | bytes 307208 | tf_op jit(solution)/shard_map/ppermute | solution.py:19
  45.7 7.5 %collective-permute-start.14 = (bf16[400,128]{1,0:T(8,128)(2,1)S(1)}, bf16[400,128]{1,0:T(8,128)(2,1)S(1)}, u32[]{:S(2)}, u32[]{:S(2)}) collective-permute-start(bf16[400,128]{1,0:T(8,128)(2,1)S(1)} %shard_map.125.refs_4_), channel_id=1, source_target_pairs={{0,12},{4,0},{8,4},{12,8},{1,13},{5,1},{9,5},{13,9},{2,14},{6,2},{... | collective-permute-start | bytes 307208 | tf_op jit(solution)/shard_map/ppermute | solution.py:19
  55.7 1.3 %collective-permute-start.15 = (bf16[16,2048]{1,0:T(8,128)(2,1)S(1)}, bf16[16,2048]{1,0:T(8,128)(2,1)S(1)}, u32[]{:S(2)}, u32[]{:S(2)}) collective-permute-start(bf16[16,2048]{1,0:T(8,128)(2,1)S(1)} %get-tuple-element.30), channel_id=1, source_target_pairs={{0,1},{1,0},{2,3},{3,2},{4,5},{5,4},{6,7},{7,6},{8,9},{9,8},{10,11... | collective-permute-start | bytes 196616 | tf_op jit(solution)/shard_map/ppermute | solution.py:19
  57.1 4.0 %collective-permute-start.16 = (bf16[8,2048]{1,0:T(8,128)(2,1)S(1)}, bf16[8,2048]{1,0:T(8,128)(2,1)S(1)}, u32[]{:S(2)}, u32[]{:S(2)}) collective-permute-start(bf16[8,2048]{1,0:T(8,128)(2,1)S(1)} %fusion.1), channel_id=1, source_target_pairs={{0,2},{2,0},{1,3},{3,1},{4,6},{6,4},{5,7},{7,5},{8,10},{10,8},{9,1... | collective-permute-start | bytes 98312 | tf_op jit(solution)/shard_map/ppermute | solution.py:19

commit v4 on v3

v4 whole, which is shorter than its diff:
```python
import functools

import jax
import jax.numpy as jnp
from jax import lax
from jax.experimental import pallas as pl
from jax.experimental.pallas import tpu as pltpu
from jax.sharding import PartitionSpec as P


masked_score = -1e30
norm_epsilon = 1e-05
extra_rows = 8
bf16 = jnp.bfloat16
f32 = jnp.float32


def shifted(part, axis, by):
    peers = lax.axis_size(axis)
    return lax.ppermute(part, axis, [(i, (i + by) % peers) for i in range(peers)])


def swapped(part, by):
    peers = lax.axis_size("seq")
    return lax.ppermute(part, "seq", [(i, i ^ by) for i in range(peers)])


vmem = pl.BlockSpec(memory_space=pltpu.VMEM)
hbm = pl.BlockSpec(memory_space=pltpu.HBM)


def call(body, outs, flops, moved, n_in, scratch=(), limit=None):
    return pl.pallas_call(
        body,
        out_shape=outs,
        in_specs=[vmem] * n_in,
        out_specs=jax.tree.map(lambda _: vmem, outs),
        scratch_shapes=list(scratch),
        cost_estimate=pl.CostEstimate(flops=flops, bytes_accessed=moved, transcendentals=0),
        compiler_params=pltpu.CompilerParams(vmem_limit_bytes=limit or (16 << 20)),
    )


def project_body(pieces, halves, blocks, *refs):
    row_refs, (key_ref, value_ref) = refs[: pieces * halves], refs[pieces * halves :][:2]
    rest = refs[pieces * halves + 2 :]
    extra_refs, out_refs = rest[:-pieces], rest[-pieces:]
    rows = jnp.concatenate([ref[...] for ref in row_refs], axis=0)
    count = rows.shape[0] // pieces
    depth = out_refs[0].shape[1]
    kv = blocks // 2
    for i, ref in enumerate((key_ref, value_ref)):
        part = jnp.dot(rows, ref[...], preferred_element_type=f32).astype(out_refs[0].dtype)
        for c in range(kv):
            at = (i * kv + c) * count
            lanes = slice(c * depth, (c + 1) * depth)
            for piece, out_ref in enumerate(out_refs):
                out_ref[at : at + count, :] = part[piece * count : (piece + 1) * count, lanes]
    for ref, out_ref in zip(extra_refs, out_refs):
        out_ref[blocks * count :, :] = ref[...]


def prepare_body(pieces, *refs):
    feature_ref, query_ref, length_ref, frame_ref = refs[:4]
    piece_refs, message_ref = refs[4 : 4 + pieces], refs[4 + pieces]
    query_in, length_in, frame_in, query_wide, sems = refs[5 + pieces :]
    half_rows, depth = piece_refs[0].shape
    rows = pl.ds(pl.multiple_of(lax.axis_index("head") * half_rows, half_rows), half_rows)
    copies = []
    for i, (source, target) in enumerate(
        ((query_ref, query_in), (length_ref, length_in), (frame_ref, frame_in))
    ):
        copies.append(pltpu.make_async_copy(source, target, sems.at[i]))
    for by, target in enumerate(piece_refs):
        at = lax.axis_index("seq") ^ (by + 1)
        source = feature_ref.at[rows, pl.ds(pl.multiple_of(at * depth, depth), depth)]
        copies.append(pltpu.make_async_copy(source, target, sems.at[3 + by]))
    for copy in copies:
        copy.start()
    for copy in copies[:3]:
        copy.wait()
    text_rows = frame_in.shape[1]
    query_rows = query_in.shape[0]
    heads = query_rows // text_rows
    frames = length_in.shape[1]
    column = as_column(frame_in[...].astype(f32), diagonal(text_rows)).astype(jnp.int32)
    index = lax.broadcasted_iota(jnp.int32, (text_rows, frames), 1)
    seen = jnp.where(index <= column, length_in[...].astype(f32), 0.0)
    limit = jnp.sum(seen, axis=1, keepdims=True).astype(jnp.int32)
    lane = lax.broadcasted_iota(jnp.int32, (text_rows, query_in.shape[1]), 1)
    digits = jnp.where(lane == 0, limit & 255, 0)
    digits = jnp.where(lane == 1, (limit >> 8) & 255, digits)
    digits = jnp.where(lane == 2, limit >> 16, digits).astype(f32)
    message_ref[query_rows:, :] = digits.astype(bf16)
    query_wide[...] = query_in[...].astype(f32)
    for head in range(0, heads, 2):
        pair = [query_wide[pl.ds(head + i, text_rows, stride=heads), :] for i in range(2)]
        message_ref[head * text_rows : (head + 2) * text_rows, :] = jnp.concatenate(
            pair, axis=0
        ).astype(bf16)
    for copy in copies[3:]:
        copy.wait()


def own_body(blocks, *refs):
    feature_ref, *sources = refs[:4]
    *targets, term_ref, rows_ref, sems = refs[4:]
    depth = rows_ref.shape[1]
    columns = pl.ds(pl.multiple_of(lax.axis_index("seq") * depth, depth), depth)
    copies = [pltpu.make_async_copy(feature_ref.at[:, columns], rows_ref, sems.at[0])]
    for i in range(3):
        copies.append(pltpu.make_async_copy(sources[i], targets[i], sems.at[1 + i]))
    for copy in copies:
        copy.start()
    for copy in copies[:3]:
        copy.wait()
    project_body(1, 1, blocks, rows_ref, targets[0], targets[1], term_ref)
    copies[3].wait()


def row_limits(message_refs, text_rows, query_rows, group):
    columns = []
    for ref in message_refs:
        digits = ref[query_rows:, :].astype(f32)[:text_rows]
        limit = digits[:, 0:1] + 256.0 * digits[:, 1:2] + 65536.0 * digits[:, 2:3]
        columns.extend([limit] * group)
    return jnp.concatenate(columns, axis=0).astype(jnp.int32)


def diagonal(size):
    shape = (size, size)
    return lax.broadcasted_iota(jnp.int32, shape, 0) == lax.broadcasted_iota(jnp.int32, shape, 1)


def store_logs(out_ref, start, query_rows, log):
    depth = out_ref.shape[1]
    if log.shape[1] < depth:
        log = jnp.concatenate((log, jnp.zeros((1, depth - log.shape[1]), f32)), axis=1)
    high = log.astype(bf16).astype(f32)
    middle = (log - high).astype(bf16).astype(f32)
    low = log - high - middle
    pieces = jnp.concatenate((high, middle, low, jnp.zeros((extra_rows - 3, depth), f32)), axis=0)
    out_ref[start + query_rows :, :] = pieces.astype(bf16)


def read_logs(message, query_rows):
    pieces = message[query_rows:].astype(f32)
    return (pieces[0:1] + pieces[1:2] + pieces[2:3])[:, :query_rows]


def as_column(row, on_diagonal):
    return jnp.sum(jnp.where(on_diagonal, row, 0.0), axis=1, keepdims=True)


def cached_body(blocks, text_rows, kv, scale, block_keys, *refs):
    message_refs = refs[:blocks]
    key_ref, value_ref, mean_ref, log_ref = refs[blocks:]
    depth = message_refs[0].shape[1]
    query_rows = message_refs[0].shape[0] - extra_rows
    unit = query_rows // kv
    group = unit // text_rows
    keys = key_ref.shape[0]
    step = min(blocks, 4)
    base = lax.axis_index("seq") * block_keys
    position = lax.broadcasted_iota(jnp.int32, (step * unit, keys), 1) + base
    for start in range(0, blocks, step):
        some = message_refs[start : start + step]
        visible = position < row_limits(some, text_rows, query_rows, group)
        at = slice(start * unit, (start + step) * unit)
        for c in range(kv):
            query = jnp.concatenate([ref[c * unit : (c + 1) * unit, :] for ref in some], axis=0)
            lanes = slice(c * depth, (c + 1) * depth)
            scores = lax.dot_general(
                query, key_ref[:, lanes], (((1,), (1,)), ((), ())), preferred_element_type=f32
            ) * scale
            scores = jnp.where(visible, scores, masked_score)
            peak = jnp.max(scores, axis=1, keepdims=True)
            weights = jnp.where(visible, jnp.exp(scores - peak), 0.0)
            total = jnp.sum(weights, axis=1, keepdims=True)
            summed = jnp.dot(weights.astype(bf16), value_ref[:, lanes], preferred_element_type=f32)
            some_seen = total > 0.0
            safe = jnp.where(some_seen, total, 1.0)
            mean_ref[c, at, :] = summed / safe
            log = jnp.where(some_seen, peak + jnp.log(safe), masked_score)
            log_ref[c, at, :] = jnp.broadcast_to(log, summed.shape)


def fresh_body(blocks, text_rows, kv, halves, scale, block_keys, own_ref, gain_ref, *refs):
    term_refs, message_refs = refs[: blocks - 1], refs[blocks - 1 : 2 * blocks - 1]
    mean_ref, log_ref, fresh_ref, *out_refs = refs[2 * blocks - 1 :]
    keys = own_ref.shape[0] // (2 * kv)
    query_rows = message_refs[0].shape[0] - extra_rows
    unit = query_rows // kv
    group = unit // text_rows
    half = keys // halves
    parts = []
    for c in range(2 * kv):
        at = slice(c * keys, (c + 1) * keys)
        raw = functools.reduce(jnp.add, [ref[at, :].astype(f32) for ref in term_refs])
        turned = raw
        for turn in range(1, halves):
            other = jnp.concatenate((raw[-turn * half :], raw[: -turn * half]), axis=0)
            turned = jnp.where(lax.axis_index("head") == turn, other, turned)
        raw = turned + own_ref[at, :]
        if c < kv:
            mean_square = jnp.mean(raw * raw, axis=1, keepdims=True)
            raw = raw * lax.rsqrt(mean_square + norm_epsilon) * gain_ref[...]
        parts.append(raw.astype(bf16))
        fresh_ref[at, :] = parts[-1]
    step = min(blocks, 4)
    base = lax.axis_index("seq") * block_keys + (block_keys - keys)
    position = lax.broadcasted_iota(jnp.int32, (step * unit, keys), 1) + base
    on_diagonal = diagonal(unit)
    for start in range(0, blocks, step):
        some = message_refs[start : start + step]
        visible = position < row_limits(some, text_rows, query_rows, group)
        at = slice(start * unit, (start + step) * unit)
        logs = [[] for _ in some]
        for c in range(kv):
            query = jnp.concatenate([ref[c * unit : (c + 1) * unit, :] for ref in some], axis=0)
            scores = lax.dot_general(
                query, parts[c], (((1,), (1,)), ((), ())), preferred_element_type=f32
            ) * scale
            scores = jnp.where(visible, scores, masked_score)
            old_log = log_ref[c, at, :1]
            peak = jnp.maximum(jnp.max(scores, axis=1, keepdims=True), old_log)
            weights = jnp.where(visible, jnp.exp(scores - peak), 0.0)
            share = jnp.exp(old_log - peak)
            total = share + jnp.sum(weights, axis=1, keepdims=True)
            summed = share * mean_ref[c, at, :] + jnp.dot(
                weights.astype(bf16), parts[kv + c], preferred_element_type=f32
            )
            mean = (summed / total).astype(bf16)
            log = peak + jnp.log(total)
            for i in range(len(some)):
                rows = slice(i * unit, (i + 1) * unit)
                out_refs[start + i][c * unit : (c + 1) * unit, :] = mean[rows]
                logs[i].append(
                    jnp.sum(jnp.where(on_diagonal, log[rows], 0.0), axis=0, keepdims=True)
                )
        for i in range(len(some)):
            store_logs(out_refs[start + i], 0, query_rows, jnp.concatenate(logs[i], axis=1))


def merge_body(blocks, text_rows, *refs):
    message_refs, out_ref = refs[:blocks], refs[blocks]
    depth = message_refs[0].shape[1]
    query_rows = message_refs[0].shape[0] - extra_rows
    on_diagonal = diagonal(query_rows)
    logs = [read_logs(ref[...], query_rows) for ref in message_refs]
    top = functools.reduce(jnp.maximum, logs)
    shares = [jnp.exp(log - top) for log in logs]
    whole = functools.reduce(jnp.add, shares)
    merged = None
    for share, ref in zip(shares, message_refs):
        term = as_column(share / whole, on_diagonal) * ref[:query_rows, :].astype(f32)
        merged = term if merged is None else merged + term
    for head in range(query_rows // text_rows):
        lanes = slice(head * depth, (head + 1) * depth)
        out_ref[:, lanes] = merged[head * text_rows : (head + 1) * text_rows].astype(bf16)


def output_body(blocks, heads, sections, *refs):
    row_refs = refs[:blocks]
    weight_ref, sent_ref, kept_ref, rows_ref, product_ref = refs[blocks:]
    count = row_refs[0].shape[0]
    for by, ref in enumerate(row_refs):
        place = lax.axis_index("seq") ^ by
        at = pl.ds(pl.multiple_of(place * count, count), count)
        rows_ref[at, :] = ref[...].astype(f32)
    rows = rows_ref[...].astype(bf16)
    product_ref[...] = jnp.dot(rows, weight_ref[...], preferred_element_type=f32)
    count = product_ref.shape[0] // (heads * sections)
    mine = lax.axis_index("head")
    for s in range(sections):
        here = slice(s * count, (s + 1) * count)
        keep_at = pl.multiple_of((s * heads + mine) * count, count)
        kept_ref[here, :] = product_ref[pl.ds(keep_at, count), :]
        for by in range(1, heads):
            to = lax.rem(mine + by, heads)
            send_at = pl.multiple_of((s * heads + to) * count, count)
            there = slice(((by - 1) * sections + s) * count, ((by - 1) * sections + s + 1) * count)
            sent_ref[there, :] = product_ref[pl.ds(send_at, count), :].astype(bf16)


def turn_body(sections, kept_ref, *refs):
    got_refs, (sent_ref, own_ref, whole_ref) = refs[:-3], refs[-3:]
    total = kept_ref[...]
    for ref in got_refs:
        total = total + ref[...].astype(f32)
    whole_ref[...] = total
    count = own_ref.shape[0]
    me = lax.axis_index("section")
    own_ref[...] = whole_ref[pl.ds(pl.multiple_of(me * count, count), count), :]
    for by in range(1, sections):
        to = lax.rem(me + by, sections)
        there = slice((by - 1) * count, by * count)
        sent_ref[there, :] = whole_ref[pl.ds(pl.multiple_of(to * count, count), count), :].astype(bf16)


def on_device(
    queries,
    key_cache,
    value_cache,
    new_features,
    key_weight,
    value_weight,
    key_gain,
    out_weight,
    frame_length,
    text_frame,
):
    cached_rows, local_kv, head_depth = key_cache.shape
    kv_width = key_weight.shape[1]
    depth = key_weight.shape[0]
    new_rows = new_features.shape[0]
    text_rows, local_heads, _ = queries.shape
    query_rows = text_rows * local_heads
    seq_size = lax.axis_size("seq")
    head_size = lax.axis_size("head")
    section_size = lax.axis_size("section")
    half_rows = new_rows // head_size
    if seq_size & (seq_size - 1):
        raise ValueError("seq size")
    sds = jax.ShapeDtypeStruct

    pieces = seq_size - 1
    prepare = pl.pallas_call(
        functools.partial(prepare_body, pieces),
        out_shape=(sds((half_rows, depth), bf16),) * pieces
        + (sds((query_rows + extra_rows, head_depth), bf16),),
        in_specs=[hbm] * 4,
        out_specs=(vmem,) * seq_size,
        scratch_shapes=[
            pltpu.VMEM((query_rows, head_depth), bf16),
            pltpu.VMEM((1, frame_length.shape[0]), jnp.int32),
            pltpu.VMEM((1, text_rows), jnp.int32),
            pltpu.VMEM((query_rows, head_depth), f32),
            pltpu.SemaphoreType.DMA((pieces + 3,)),
        ],
        name="prepare",
        cost_estimate=pl.CostEstimate(
            flops=0, bytes_accessed=8 * half_rows * depth, transcendentals=0
        ),
        compiler_params=pltpu.CompilerParams(vmem_limit_bytes=8 << 20),
    )
    sources = (
        new_features,
        queries.reshape(query_rows, head_depth),
        frame_length.reshape(1, -1),
        text_frame.reshape(1, -1),
    )
    *sent_pieces, message = prepare(
        *[pltpu.with_memory_space_constraint(w, pltpu.HBM) for w in sources],
    )
    arrived = [swapped(part, by + 1) for by, part in enumerate(sent_pieces)]
    messages = [message] + [swapped(message, by) for by in range(1, seq_size)]

    key_cache = key_cache.reshape(cached_rows, kv_width)
    value_cache = value_cache.reshape(cached_rows, kv_width)
    flops = 4 * new_rows * depth * kv_width

    kv_blocks = 2 * local_kv

    sources = (new_features, key_weight, value_weight, out_weight)
    load = pl.pallas_call(
        functools.partial(own_body, kv_blocks),
        out_shape=(
            *(sds(w.shape, bf16) for w in sources[1:]),
            sds((kv_blocks * new_rows, head_depth), f32),
        ),
        in_specs=[hbm] * 4,
        out_specs=(vmem,) * 4,
        scratch_shapes=[pltpu.VMEM((new_rows, depth), bf16), pltpu.SemaphoreType.DMA((4,))],
        name="own",
        cost_estimate=pl.CostEstimate(
            flops=flops, bytes_accessed=4 * sum(w.size for w in sources[1:]), transcendentals=0
        ),
        compiler_params=pltpu.CompilerParams(vmem_limit_bytes=16 << 20),
    )
    sources = [pltpu.with_memory_space_constraint(w, pltpu.HBM) for w in sources]
    key_weight, value_weight, out_weight, own_term = load(*sources)

    score_scale = head_depth ** (-0.5)
    block_keys = cached_rows + new_rows
    attend_flops = 4 * seq_size * query_rows * head_depth * cached_rows
    every_row = seq_size * query_rows // local_kv
    state = sds((local_kv, every_row, head_depth), f32)
    attend_cached = call(
        functools.partial(cached_body, seq_size, text_rows, local_kv, score_scale, block_keys),
        (state, state),
        attend_flops,
        4 * cached_rows * kv_width,
        seq_size + 2,
        limit=24 << 20,
    )
    cached = attend_cached(*messages, key_cache, value_cache)
    rows = []
    for half in arrived:
        rows.append(half)
        for turn in range(1, head_size):
            rows.append(shifted(half, "head", head_size - turn))
    term_shape = sds((kv_blocks * new_rows, head_depth), bf16)
    terms = call(
        functools.partial(project_body, pieces, head_size, kv_blocks),
        (term_shape,) * pieces,
        flops * pieces,
        4 * depth * kv_width,
        pieces * head_size + 2,
    )(*rows, key_weight, value_weight)
    terms = [swapped(term, by + 1) for by, term in enumerate(terms)]
    fresh, *outgoing = call(
        functools.partial(
            fresh_body, seq_size, text_rows, local_kv, head_size, score_scale, block_keys
        ),
        (sds((kv_blocks * new_rows, head_depth), bf16),)
        + (sds(message.shape, bf16),) * seq_size,
        attend_flops * new_rows // cached_rows,
        8 * every_row * kv_width,
        2 * seq_size + 3,
    )(own_term, key_gain.reshape(1, head_depth), *terms, *messages, *cached)
    made = fresh.reshape(2, local_kv, new_rows, head_depth)
    new_keys, new_values = (jnp.swapaxes(part, 0, 1) for part in made)
    crossed = [outgoing[0]] + [swapped(outgoing[by], by) for by in range(1, seq_size)]
    attended = call(
        functools.partial(merge_body, seq_size, text_rows),
        sds((text_rows, local_heads * head_depth), bf16),
        seq_size * query_rows * head_depth,
        2 * seq_size * query_rows * head_depth,
        seq_size,
    )(*crossed)
    every = [attended] + [swapped(attended, by) for by in range(1, seq_size)]

    all_rows = seq_size * text_rows
    out_width = out_weight.shape[1]
    out_rows = all_rows // (section_size * head_size)
    sent, kept = call(
        functools.partial(output_body, seq_size, head_size, section_size),
        (
            sds(((head_size - 1) * section_size * out_rows, out_width), bf16),
            sds((section_size * out_rows, out_width), f32),
        ),
        2 * all_rows * out_weight.size,
        2 * out_weight.size,
        seq_size + 1,
        scratch=[
            pltpu.VMEM((all_rows, local_heads * head_depth), f32),
            pltpu.VMEM((all_rows, out_width), f32),
        ],
        limit=24 << 20,
    )(
        *every,
        out_weight,
    )
    sent = sent.reshape(head_size - 1, section_size * out_rows, out_width)
    got = [shifted(sent[by - 1], "head", by) for by in range(1, head_size)]
    sent, own_rows = call(
        functools.partial(turn_body, section_size),
        (
            sds(((section_size - 1) * out_rows, out_width), bf16),
            sds((out_rows, out_width), f32),
        ),
        kept.size,
        8 * kept.size,
        head_size,
        scratch=[pltpu.VMEM(kept.shape, f32)],
    )(kept, *got)
    sent = sent.reshape(section_size - 1, out_rows, out_width)
    for by in range(1, section_size):
        own_rows = own_rows + shifted(sent[by - 1], "section", by).astype(f32)
    return (own_rows.astype(bf16), new_keys, new_values)


def solution(mesh):
    placed = (
        P(("groups", "seq"), ("section", "head"), None),
        P(("groups", "seq"), ("section", "head"), None),
        P(("groups", "seq"), ("section", "head"), None),
        P(("groups", "seq"), None),
        P("seq", ("section", "head")),
        P("seq", ("section", "head")),
        P(),
        P(("section", "head"), "seq"),
        P("groups"),
        P(("groups", "seq")),
    )
    return jax.shard_map(
        on_device,
        mesh=mesh,
        in_specs=placed,
        out_specs=(
            P(("groups", "section", "head"), "seq"),
            P(("groups", "seq"), ("section", "head"), None),
            P(("groups", "seq"), ("section", "head"), None),
        ),
        check_vma=False,
    )
```

time: 61.9 us -> 62.3 us (level)
  local copies, waits for them, and re-layouts: 3.16 us -> 1.73 us
  starting transfers between devices: 24.2 us -> 25.6 us
  waiting for transfers between devices: 21.2 us -> 22.3 us
  Pallas kernels: 11.7 us -> 11 us
    ppermute x0 -> x15, starting transfers between devices: none -> 23.5 us  [swapped(): return lax.ppermute(part, 'seq', [(i, i ^ by) for i in range(peers)])]
    ppermute x17 -> x5, starting transfers between devices: 24.2 us -> 2.14 us  [shifted(): lax.ppermute(part, axis, [(i, (i + by) % peers) for i in range(peers)])]
    ppermute x0 -> x15, waiting for transfers between devices: none -> 19.9 us  [swapped(): return lax.ppermute(part, 'seq', [(i, i ^ by) for i in range(peers)])]
    ppermute x17 -> x5, waiting for transfers between devices: 21.2 us -> 2.37 us  [shifted(): lax.ppermute(part, axis, [(i, (i + by) % peers) for i in range(peers)])]
    reshape x1, local copies, waits for them, and re-layouts: 1.84 us -> 0.42 us  [on_device(): value_cache = value_cache.reshape(cached_rows, kv_width)]
    pallas_call x5, Pallas kernels: 4.12 us -> 3.37 us  [the longest x1 1.57 us: on_device(): call(functools.partial(output_body, seq_size, head_size, section_size), (...]
  transfers between devices with their start and end apart: 17 -> 20, of which waited for: 9 -> 10; matrix products, arithmetic and copies ran while one was open for 5% -> 3% of each run, Pallas kernels for 13% -> 11%
where the time goes in v4:
time: 62.3 us; the launch traced here: 62.1 us
  starting transfers between devices  25.6 us (41%)
  waiting for transfers between devices  22.3 us (36%)
  Pallas kernels  11 us (18%)
  local copies, waits for them, and re-layouts  1.73 us (3%)
  between operations  0.77 us (1%)
    ppermute x15, starting transfers between devices, swapped(): return lax.ppermute(part, 'seq', [(i, i ^ by) for i in range(peers)])  23.5 us
    ppermute x15, waiting for transfers between devices, swapped(): return lax.ppermute(part, 'seq', [(i, i ^ by) for i in range(peers)])  19.9 us
    pallas_call x1, Pallas kernels, on_device(): key_weight, value_weight, out_weight, own_term = load(*sources)  4.14 us
    ppermute x5, waiting for transfers between devices, shifted(): lax.ppermute(part, axis, [(i, (i + by) % peers) for i in range(peers)])  2.37 us
    pallas_call x1, Pallas kernels, on_device(): cached = attend_cached(*messages, key_cache, value_cache)  2.24 us
    ppermute x5, starting transfers between devices, shifted(): lax.ppermute(part, axis, [(i, (i + by) % peers) for i in range(peers)])  2.14 us
    pallas_call x1, Pallas kernels, on_device(): call(functools.partial(output_body, seq_size, head_size, section_size), (...  1.57 us
    another operation x3, local copies, waits for them, and re-layouts, on_device(): new_keys, new_values = (jnp.swapaxes(part, 0, 1) for part in made)  1.3 us
  transfers between devices with their start and end apart: 20, of which 10 were waited for; matrix products, arithmetic and copies ran while one was open for 3% of the time, Pallas kernels for 11%

profile of v4, /device:TPU:0, one launch (start us, length us, event | category | flops | bytes accessed | tf_op | source)
XLA Modules:
  0.0 62.1 jit_solution(6255474838434856975)
XLA Ops:
  0.7 1.3 %prepare.1 = (bf16[32,2048]{1,0:T(8,128)(2,1)S(1)}, bf16[32,2048]{1,0:T(8,128)(2,1)S(1)}, bf16[32,2048]{1,0:T(8,128)(2,1)S(1)}, bf16[136,128]{1,0:T(8,128)(2,1)S(1)}) custom-call(bf16[64,8192]{1,0:T(8,128)(2,1)} %refs_0_.3, bf16[128,128]{1,0:T(8,128)(2,1)} %bitcast.23, s32[1,64]{1,0:T(1,128)} %bitcast.26, s32[1,8]{1,0:T(1,128)} %bitcast.27), custom_call_target="tpu_custom_call" | custom-call | bytes 524288 | tf_op jit(solution)/shard_map/prepare/pallas_call | solution.py:353
  1.9 3.1 %collective-permute-start = (bf16[32,2048]{1,0:T(8,128)(2,1)S(1)}, bf16[32,2048]{1,0:T(8,128)(2,1)S(1)}, u32[]{:S(2)}, u32[]{:S(2)}) collective-permute-start(bf16[32,2048]{1,0:T(8,128)(2,1)S(1)} %get-tuple-element.26), channel_id=1, source_target_pairs={{0,4},{4,0},{8,12},{12,8},{1,5},{5,1},{9,13},{13,9},{2,6},{6,2},{1... | collective-permute-start | bytes 393224 | tf_op jit(solution)/shard_map/ppermute | solution.py:25
  5.1 2.6 %collective-permute-start.2 = (bf16[32,2048]{1,0:T(8,128)(2,1)S(1)}, bf16[32,2048]{1,0:T(8,128)(2,1)S(1)}, u32[]{:S(2)}, u32[]{:S(2)}) collective-permute-start(bf16[32,2048]{1,0:T(8,128)(2,1)S(1)} %get-tuple-element.27), channel_id=1, source_target_pairs={{0,8},{4,12},{8,0},{12,4},{1,9},{5,13},{9,1},{13,5},{2,10},{6,14},... | collective-permute-start | bytes 393224 | tf_op jit(solution)/shard_map/ppermute | solution.py:25
  7.6 0.0 collective-permute-start.4
  7.6 2.5 %collective-permute-done.refs_0_ = bf16[32,2048]{1,0:T(8,128)(2,1)S(1)} collective-permute-done((bf16[32,2048]{1,0:T(8,128)(2,1)S(1)}, bf16[32,2048]{1,0:T(8,128)(2,1)S(1)}, u32[]{:S(2)}, u32[]{:S(2)}) %collective-permute-start) | collective-permute-done | bytes 131104 | tf_op jit(solution)/shard_map/ppermute | solution.py:25
  10.1 0.0 collective-permute-start.1
  10.1 7.8 %collective-permute-done.2.refs_2_ = bf16[32,2048]{1,0:T(8,128)(2,1)S(1)} collective-permute-done((bf16[32,2048]{1,0:T(8,128)(2,1)S(1)}, bf16[32,2048]{1,0:T(8,128)(2,1)S(1)}, u32[]{:S(2)}, u32[]{:S(2)}) %collective-permute-start.2) | collective-permute-done | bytes 131104 | tf_op jit(solution)/shard_map/ppermute | solution.py:25
  17.9 0.0 collective-permute-start.3
  17.9 0.0 collective-permute-done.4.refs_4_
  17.9 0.5 collective-permute-start.5
  18.5 1.5 %collective-permute-start.9 = (bf16[136,128]{1,0:T(8,128)(2,1)S(1)}, bf16[136,128]{1,0:T(8,128)(2,1)S(1)}, u32[]{:S(2)}, u32[]{:S(2)}) collective-permute-start(bf16[136,128]{1,0:T(8,128)(2,1)S(1)} %get-tuple-element.34.refs_0_.refs_3_), channel_id=1, source_target_pairs={{0,4},{4,0},{8,12},{12,8},{1,5},{5,1},{9,13},{13,9},{2,6},{6,2},{1... | collective-permute-start | bytes 104456 | tf_op jit(solution)/shard_map/ppermute | solution.py:25
  20.0 1.3 %collective-permute-start.10 = (bf16[136,128]{1,0:T(8,128)(2,1)S(1)}, bf16[136,128]{1,0:T(8,128)(2,1)S(1)}, u32[]{:S(2)}, u32[]{:S(2)}) collective-permute-start(bf16[136,128]{1,0:T(8,128)(2,1)S(1)} %get-tuple-element.34.refs_0_.refs_3_), channel_id=1, source_target_pairs={{0,8},{4,12},{8,0},{12,4},{1,9},{5,13},{9,1},{13,5},{2,10},{6,14},... | collective-permute-start | bytes 104456 | tf_op jit(solution)/shard_map/ppermute | solution.py:25
  21.3 4.1 %own.1 = (bf16[2048,256]{1,0:T(8,128)(2,1)S(1)}, bf16[2048,256]{1,0:T(8,128)(2,1)S(1)}, bf16[2048,2048]{1,0:T(8,128)(2,1)S(1)}, f32[256,128]{1,0:T(8,128)S(1)}) custom-call(bf16[64,8192]{1,0:T(8,128)(2,1)} %refs_0_.3, bf16[2048,256]{1,0:T(8,128)(2,1)} %refs_1_.1, bf16[2048,256]{1,0:T(8,128)(2,1)} %refs_2_.1, bf16[2048,2048]{1,0:T(8,128)(2,1)} %refs_3_.1), custom_call_target="tpu_custom_call" | custom-call | flops 134217728 | bytes 20971520 | tf_op jit(solution)/shard_map/own/pallas_call | solution.py:382
  25.4 0.0 collective-permute-done.1.refs_1_
  25.5 1.6 %collective-permute-start.11 = (bf16[136,128]{1,0:T(8,128)(2,1)S(1)}, bf16[136,128]{1,0:T(8,128)(2,1)S(1)}, u32[]{:S(2)}, u32[]{:S(2)}) collective-permute-start(bf16[136,128]{1,0:T(8,128)(2,1)S(1)} %get-tuple-element.34.refs_0_.refs_3_), channel_id=1, source_target_pairs={{0,12},{4,8},{8,4},{12,0},{1,13},{5,9},{9,5},{13,1},{2,14},{6,10},... | collective-permute-start | bytes 104456 | tf_op jit(solution)/shard_map/ppermute | solution.py:25
  27.1 0.0 collective-permute-done.3.refs_3_
  27.1 0.0 collective-permute-done.5.refs_5_
  27.1 0.6 shard_map.121
  27.7 0.7 %collective-permute-start.6 = (bf16[256,128]{1,0:T(8,128)(2,1)S(1)}, bf16[256,128]{1,0:T(8,128)(2,1)S(1)}, u32[]{:S(2)}, u32[]{:S(2)}) collective-permute-start(bf16[256,128]{1,0:T(8,128)(2,1)S(1)} %get-tuple-element.31), channel_id=1, source_target_pairs={{0,4},{4,0},{8,12},{12,8},{1,5},{5,1},{9,13},{13,9},{2,6},{6,2},{1... | collective-permute-start | bytes 196616 | tf_op jit(solution)/shard_map/ppermute | solution.py:25
  28.3 2.2 %collective-permute-start.7 = (bf16[256,128]{1,0:T(8,128)(2,1)S(1)}, bf16[256,128]{1,0:T(8,128)(2,1)S(1)}, u32[]{:S(2)}, u32[]{:S(2)}) collective-permute-start(bf16[256,128]{1,0:T(8,128)(2,1)S(1)} %get-tuple-element.32), channel_id=1, source_target_pairs={{0,8},{4,12},{8,0},{12,4},{1,9},{5,13},{9,1},{13,5},{2,10},{6,14},... | collective-permute-start | bytes 196616 | tf_op jit(solution)/shard_map/ppermute | solution.py:25
  30.6 1.6 %collective-permute-start.8 = (bf16[256,128]{1,0:T(8,128)(2,1)S(1)}, bf16[256,128]{1,0:T(8,128)(2,1)S(1)}, u32[]{:S(2)}, u32[]{:S(2)}) collective-permute-start(bf16[256,128]{1,0:T(8,128)(2,1)S(1)} %get-tuple-element.33), channel_id=1, source_target_pairs={{0,12},{4,8},{8,4},{12,0},{1,13},{5,9},{9,5},{13,1},{2,14},{6,10},... | collective-permute-start | bytes 196616 | tf_op jit(solution)/shard_map/ppermute | solution.py:25
  32.1 0.4 copy_bitcast_fusion
  32.5 0.0 collective-permute-done.10.refs_2_.refs_5_
  32.6 2.2 %shard_map.122 = (f32[2,256,128]{2,1,0:T(8,128)S(1)}, f32[2,256,128]{2,1,0:T(8,128)S(1)}) custom-call(bf16[136,128]{1,0:T(8,128)(2,1)S(1)} %get-tuple-element.34.refs_0_.refs_3_, bf16[136,128]{1,0:T(8,128)(2,1)S(1)} %collective-permute-done.9.refs_1_.refs_4_, bf16[136,128]{1,0:T(8,128)(2,1)S(1)} %collective-permute-done.10.refs_2_.refs_5_, ...), custom_call_target="tpu_custom_call" | custom-call | flops 520093696 | bytes 2031616 | tf_op jit(solution)/shard_map/pallas_call | solution.py:397
  34.8 0.7 %collective-permute-done.7.refs_1_ = bf16[256,128]{1,0:T(8,128)(2,1)S(1)} collective-permute-done((bf16[256,128]{1,0:T(8,128)(2,1)S(1)}, bf16[256,128]{1,0:T(8,128)(2,1)S(1)}, u32[]{:S(2)}, u32[]{:S(2)}) %collective-permute-start.7) | collective-permute-done | bytes 65568 | tf_op jit(solution)/shard_map/ppermute | solution.py:25
  35.6 1.2 %collective-permute-done.8.refs_2_ = bf16[256,128]{1,0:T(8,128)(2,1)S(1)} collective-permute-done((bf16[256,128]{1,0:T(8,128)(2,1)S(1)}, bf16[256,128]{1,0:T(8,128)(2,1)S(1)}, u32[]{:S(2)}, u32[]{:S(2)}) %collective-permute-start.8) | collective-permute-done | bytes 65568 | tf_op jit(solution)/shard_map/ppermute | solution.py:25
  36.7 1.0 %shard_map.123 = (bf16[256,128]{1,0:T(8,128)(2,1)S(1)}, bf16[136,128]{1,0:T(8,128)(2,1)S(1)}, bf16[136,128]{1,0:T(8,128)(2,1)S(1)}, bf16[136,128]{1,0:T(8,128)(2,1)S(1)}, bf16[136,128]{1,0:T(8,128)(2,1)S(1)}) custom-call(f32[256,128]{1,0:T(8,128)S(1)} %get-tuple-element.25.own_ref, f32[1,128]{1,0:T(1,128)S(1)} %bitcast.18, ...), custom_call_target="tpu_custom_call" | custom-call | flops 16777216 | bytes 524288 | tf_op jit(solution)/shard_map/pallas_call | solution.py:412
  37.8 0.9 %collective-permute-start.12 = (bf16[136,128]{1,0:T(8,128)(2,1)S(1)}, bf16[136,128]{1,0:T(8,128)(2,1)S(1)}, u32[]{:S(2)}, u32[]{:S(2)}) collective-permute-start(bf16[136,128]{1,0:T(8,128)(2,1)S(1)} %get-tuple-element.38), channel_id=1, source_target_pairs={{0,4},{4,0},{8,12},{12,8},{1,5},{5,1},{9,13},{13,9},{2,6},{6,2},{1... | collective-permute-start | bytes 104456 | tf_op jit(solution)/shard_map/ppermute | solution.py:25
  38.6 1.6 %collective-permute-start.13 = (bf16[136,128]{1,0:T(8,128)(2,1)S(1)}, bf16[136,128]{1,0:T(8,128)(2,1)S(1)}, u32[]{:S(2)}, u32[]{:S(2)}) collective-permute-start(bf16[136,128]{1,0:T(8,128)(2,1)S(1)} %get-tuple-element.39), channel_id=1, source_target_pairs={{0,8},{4,12},{8,0},{12,4},{1,9},{5,13},{9,1},{13,5},{2,10},{6,14},... | collective-permute-start | bytes 104456 | tf_op jit(solution)/shard_map/ppermute | solution.py:25
  40.3 2.0 %collective-permute-start.14 = (bf16[136,128]{1,0:T(8,128)(2,1)S(1)}, bf16[136,128]{1,0:T(8,128)(2,1)S(1)}, u32[]{:S(2)}, u32[]{:S(2)}) collective-permute-start(bf16[136,128]{1,0:T(8,128)(2,1)S(1)} %get-tuple-element.40), channel_id=1, source_target_pairs={{0,12},{4,8},{8,4},{12,0},{1,13},{5,9},{9,5},{13,1},{2,14},{6,10},... | collective-permute-start | bytes 104456 | tf_op jit(solution)/shard_map/ppermute | solution.py:25
  42.2 0.0 collective-permute-done.12.refs_1_
  42.2 1.4 %collective-permute-done.13.refs_2_ = bf16[136,128]{1,0:T(8,128)(2,1)S(1)} collective-permute-done((bf16[136,128]{1,0:T(8,128)(2,1)S(1)}, bf16[136,128]{1,0:T(8,128)(2,1)S(1)}, u32[]{:S(2)}, u32[]{:S(2)}) %collective-permute-start.13) | collective-permute-done | bytes 34848 | tf_op jit(solution)/shard_map/ppermute | solution.py:25
  43.6 2.7 %collective-permute-done.14.refs_3_ = bf16[136,128]{1,0:T(8,128)(2,1)S(1)} collective-permute-done((bf16[136,128]{1,0:T(8,128)(2,1)S(1)}, bf16[136,128]{1,0:T(8,128)(2,1)S(1)}, u32[]{:S(2)}, u32[]{:S(2)}) %collective-permute-start.14) | collective-permute-done | bytes 34848 | tf_op jit(solution)/shard_map/ppermute | solution.py:25
  46.3 0.2 shard_map.124.refs_0_
  46.5 0.1 collective-permute-start.15
  46.6 2.3 %collective-permute-start.16 = (bf16[8,2048]{1,0:T(8,128)(2,1)S(1)}, bf16[8,2048]{1,0:T(8,128)(2,1)S(1)}, u32[]{:S(2)}, u32[]{:S(2)}) collective-permute-start(bf16[8,2048]{1,0:T(8,128)(2,1)S(1)} %shard_map.124.refs_0_), channel_id=1, source_target_pairs={{0,8},{4,12},{8,0},{12,4},{1,9},{5,13},{9,1},{13,5},{2,10},{6,14},... | collective-permute-start | bytes 98312 | tf_op jit(solution)/shard_map/ppermute | solution.py:25
  48.9 2.1 %collective-permute-start.17 = (bf16[8,2048]{1,0:T(8,128)(2,1)S(1)}, bf16[8,2048]{1,0:T(8,128)(2,1)S(1)}, u32[]{:S(2)}, u32[]{:S(2)}) collective-permute-start(bf16[8,2048]{1,0:T(8,128)(2,1)S(1)} %shard_map.124.refs_0_), channel_id=1, source_target_pairs={{0,12},{4,8},{8,4},{12,0},{1,13},{5,9},{9,5},{13,1},{2,14},{6,10},... | collective-permute-start | bytes 98312 | tf_op jit(solution)/shard_map/ppermute | solution.py:25
  51.0 0.0 collective-permute-done.15.refs_1_
  51.0 0.5 collective-permute-done.16.refs_2_
  51.5 3.1 %collective-permute-done.17.refs_3_ = bf16[8,2048]{1,0:T(8,128)(2,1)S(1)} collective-permute-done((bf16[8,2048]{1,0:T(8,128)(2,1)S(1)}, bf16[8,2048]{1,0:T(8,128)(2,1)S(1)}, u32[]{:S(2)}, u32[]{:S(2)}) %collective-permute-start.17) | collective-permute-done | bytes 32800 | tf_op jit(solution)/shard_map/ppermute | solution.py:25
  54.6 1.6 %shard_map.125 = (bf16[16,2048]{1,0:T(8,128)(2,1)S(1)}, f32[16,2048]{1,0:T(8,128)S(1)}) custom-call(bf16[8,2048]{1,0:T(8,128)(2,1)S(1)} %shard_map.124.refs_0_, bf16[8,2048]{1,0:T(8,128)(2,1)S(1)} %collective-permute-done.15.refs_1_, bf16[8,2048]{1,0:T(8,128)(2,1)S(1)} %collective-permute-done.16.refs_2_, ...), custom_call_target="tpu_custom_call" | custom-call | flops 268435456 | bytes 8388608 | tf_op jit(solution)/shard_map/pallas_call | solution.py:437
  56.2 0.1 collective-permute-start.18
  56.2 1.2 %collective-permute-done.18.refs_0_ = bf16[16,2048]{1,0:T(8,128)(2,1)S(1)} collective-permute-done((bf16[16,2048]{1,0:T(8,128)(2,1)S(1)}, bf16[16,2048]{1,0:T(8,128)(2,1)S(1)}, u32[]{:S(2)}, u32[]{:S(2)}) %collective-permute-start.18) | collective-permute-done | bytes 65568 | tf_op jit(solution)/shard_map/ppermute | solution.py:20
  57.5 1.6 %collective-permute-start.19 = (bf16[8,2048]{1,0:T(8,128)(2,1)S(1)}, bf16[8,2048]{1,0:T(8,128)(2,1)S(1)}, u32[]{:S(2)}, u32[]{:S(2)}) collective-permute-start(bf16[8,2048]{1,0:T(8,128)(2,1)S(1)} %get-tuple-element.45), channel_id=1, source_target_pairs={{0,2},{2,0},{1,3},{3,1},{4,6},{6,4},{5,7},{7,5},{8,10},{10,8},{9,1... | collective-permute-start | bytes 98312 | tf_op jit(solution)/shard_map/ppermute | solution.py:20
  59.1 0.7 %copy.22 = bf16[2,64,128]{2,0,1:T(2,128)(2,1)} copy(bf16[2,64,128]{2,1,0:T(8,128)(2,1)S(1)} %bitcast.22) | data formatting | bytes 65536 | tf_op jit(solution)/shard_map/unstack | solution.py:423
  59.7 0.6 %copy.21 = bf16[2,64,128]{2,0,1:T(2,128)(2,1)} copy(bf16[2,64,128]{2,1,0:T(8,128)(2,1)S(1)} %bitcast.21) | data formatting | bytes 65536 | tf_op jit(solution)/shard_map/unstack | solution.py:423
  60.4 1.1 %collective-permute-done.19 = bf16[8,2048]{1,0:T(8,128)(2,1)S(1)} collective-permute-done((bf16[8,2048]{1,0:T(8,128)(2,1)S(1)}, bf16[8,2048]{1,0:T(8,128)(2,1)S(1)}, u32[]{:S(2)}, u32[]{:S(2)}) %collective-permute-start.19) | collective-permute-done | bytes 32800 | tf_op jit(solution)/shard_map/ppermute | solution.py:20
  61.5 0.6 %add_convert_fusion = bf16[8,2048]{1,0:T(8,128)(2,1)} fusion(f32[8,2048]{1,0:T(8,128)S(1)} %get-tuple-element.44, bf16[8,2048]{1,0:T(8,128)(2,1)S(1)} %collective-permute-done.19), kind=kLoop, calls=%fused_computation.2 | loop fusion | flops 49152 | bytes 131072 | tf_op jit(solution)/shard_map/convert_element_type | solution.py:471
  (11 shorter events, 0.0 us)
Async XLA Ops:
  0.6 31.5 %copy-start.1 = (bf16[1984,2,128]{2,1,0:T(2,128)(2,1)S(1)}, bf16[1984,2,128]{2,1,0:T(2,128)(2,1)}, u32[]{:S(2)}) copy-start(bf16[1984,2,128]{2,1,0:T(2,128)(2,1)} %param.12) | copy-start | bytes 3047428
  0.6 31.5 %copy-start.2 = (bf16[1984,2,128]{2,1,0:T(2,128)(2,1)S(1)}, bf16[1984,2,128]{2,1,0:T(2,128)(2,1)}, u32[]{:S(2)}) copy-start(bf16[1984,2,128]{2,1,0:T(2,128)(2,1)} %param.11) | copy-start | bytes 3047428
  1.9 8.2 %collective-permute-start = (bf16[32,2048]{1,0:T(8,128)(2,1)S(1)}, bf16[32,2048]{1,0:T(8,128)(2,1)S(1)}, u32[]{:S(2)}, u32[]{:S(2)}) collective-permute-start(bf16[32,2048]{1,0:T(8,128)(2,1)S(1)} %get-tuple-element.26), channel_id=1, source_target_pairs={{0,4},{4,0},{8,12},{12,8},{1,5},{5,1},{9,13},{13,9},{2,6},{6,2},{1... | collective-permute-start | bytes 393224 | tf_op jit(solution)/shard_map/ppermute | solution.py:25
  5.1 12.9 %collective-permute-start.2 = (bf16[32,2048]{1,0:T(8,128)(2,1)S(1)}, bf16[32,2048]{1,0:T(8,128)(2,1)S(1)}, u32[]{:S(2)}, u32[]{:S(2)}) collective-permute-start(bf16[32,2048]{1,0:T(8,128)(2,1)S(1)} %get-tuple-element.27), channel_id=1, source_target_pairs={{0,8},{4,12},{8,0},{12,4},{1,9},{5,13},{9,1},{13,5},{2,10},{6,14},... | collective-permute-start | bytes 393224 | tf_op jit(solution)/shard_map/ppermute | solution.py:25
  7.6 10.3 %collective-permute-start.4 = (bf16[32,2048]{1,0:T(8,128)(2,1)S(1)}, bf16[32,2048]{1,0:T(8,128)(2,1)S(1)}, u32[]{:S(2)}, u32[]{:S(2)}) collective-permute-start(bf16[32,2048]{1,0:T(8,128)(2,1)S(1)} %get-tuple-element.28), channel_id=1, source_target_pairs={{0,12},{4,8},{8,4},{12,0},{1,13},{5,9},{9,5},{13,1},{2,14},{6,10},... | collective-permute-start | bytes 393224 | tf_op jit(solution)/shard_map/ppermute | solution.py:25
  10.1 15.3 %collective-permute-start.1 = (bf16[32,2048]{1,0:T(8,128)(2,1)S(1)}, bf16[32,2048]{1,0:T(8,128)(2,1)S(1)}, u32[]{:S(2)}, u32[]{:S(2)}) collective-permute-start(bf16[32,2048]{1,0:T(8,128)(2,1)S(1)} %collective-permute-done.refs_0_), channel_id=1, source_target_pairs={{0,1},{1,0},{2,3},{3,2},{4,5},{5,4},{6,7},{7,6},{8,9},{9,8},{10,11... | collective-permute-start | bytes 393224 | tf_op jit(solution)/shard_map/ppermute | solution.py:20
  17.9 9.1 %collective-permute-start.3 = (bf16[32,2048]{1,0:T(8,128)(2,1)S(1)}, bf16[32,2048]{1,0:T(8,128)(2,1)S(1)}, u32[]{:S(2)}, u32[]{:S(2)}) collective-permute-start(bf16[32,2048]{1,0:T(8,128)(2,1)S(1)} %collective-permute-done.2.refs_2_), channel_id=1, source_target_pairs={{0,1},{1,0},{2,3},{3,2},{4,5},{5,4},{6,7},{7,6},{8,9},{9,8},{10,11... | collective-permute-start | bytes 393224 | tf_op jit(solution)/shard_map/ppermute | solution.py:20
  17.9 9.1 %collective-permute-start.5 = (bf16[32,2048]{1,0:T(8,128)(2,1)S(1)}, bf16[32,2048]{1,0:T(8,128)(2,1)S(1)}, u32[]{:S(2)}, u32[]{:S(2)}) collective-permute-start(bf16[32,2048]{1,0:T(8,128)(2,1)S(1)} %collective-permute-done.4.refs_4_), channel_id=1, source_target_pairs={{0,1},{1,0},{2,3},{3,2},{4,5},{5,4},{6,7},{7,6},{8,9},{9,8},{10,11... | collective-permute-start | bytes 393224 | tf_op jit(solution)/shard_map/ppermute | solution.py:20
  18.5 18.3 %copy-start = (f32[128]{0:T(128)S(1)}, f32[128]{0:T(128)}, u32[]{:S(2)}) copy-start(f32[128]{0:T(128)} %param.16) | copy-start | bytes 1540
  18.5 12.1 %collective-permute-start.9 = (bf16[136,128]{1,0:T(8,128)(2,1)S(1)}, bf16[136,128]{1,0:T(8,128)(2,1)S(1)}, u32[]{:S(2)}, u32[]{:S(2)}) collective-permute-start(bf16[136,128]{1,0:T(8,128)(2,1)S(1)} %get-tuple-element.34.refs_0_.refs_3_), channel_id=1, source_target_pairs={{0,4},{4,0},{8,12},{12,8},{1,5},{5,1},{9,13},{13,9},{2,6},{6,2},{1... | collective-permute-start | bytes 104456 | tf_op jit(solution)/shard_map/ppermute | solution.py:25
  20.0 12.6 %collective-permute-start.10 = (bf16[136,128]{1,0:T(8,128)(2,1)S(1)}, bf16[136,128]{1,0:T(8,128)(2,1)S(1)}, u32[]{:S(2)}, u32[]{:S(2)}) collective-permute-start(bf16[136,128]{1,0:T(8,128)(2,1)S(1)} %get-tuple-element.34.refs_0_.refs_3_), channel_id=1, source_target_pairs={{0,8},{4,12},{8,0},{12,4},{1,9},{5,13},{9,1},{13,5},{2,10},{6,14},... | collective-permute-start | bytes 104456 | tf_op jit(solution)/shard_map/ppermute | solution.py:25
  25.5 7.1 %collective-permute-start.11 = (bf16[136,128]{1,0:T(8,128)(2,1)S(1)}, bf16[136,128]{1,0:T(8,128)(2,1)S(1)}, u32[]{:S(2)}, u32[]{:S(2)}) collective-permute-start(bf16[136,128]{1,0:T(8,128)(2,1)S(1)} %get-tuple-element.34.refs_0_.refs_3_), channel_id=1, source_target_pairs={{0,12},{4,8},{8,4},{12,0},{1,13},{5,9},{9,5},{13,1},{2,14},{6,10},... | collective-permute-start | bytes 104456 | tf_op jit(solution)/shard_map/ppermute | solution.py:25
  27.7 7.1 %collective-permute-start.6 = (bf16[256,128]{1,0:T(8,128)(2,1)S(1)}, bf16[256,128]{1,0:T(8,128)(2,1)S(1)}, u32[]{:S(2)}, u32[]{:S(2)}) collective-permute-start(bf16[256,128]{1,0:T(8,128)(2,1)S(1)} %get-tuple-element.31), channel_id=1, source_target_pairs={{0,4},{4,0},{8,12},{12,8},{1,5},{5,1},{9,13},{13,9},{2,6},{6,2},{1... | collective-permute-start | bytes 196616 | tf_op jit(solution)/shard_map/ppermute | solution.py:25
  28.3 7.2 %collective-permute-start.7 = (bf16[256,128]{1,0:T(8,128)(2,1)S(1)}, bf16[256,128]{1,0:T(8,128)(2,1)S(1)}, u32[]{:S(2)}, u32[]{:S(2)}) collective-permute-start(bf16[256,128]{1,0:T(8,128)(2,1)S(1)} %get-tuple-element.32), channel_id=1, source_target_pairs={{0,8},{4,12},{8,0},{12,4},{1,9},{5,13},{9,1},{13,5},{2,10},{6,14},... | collective-permute-start | bytes 196616 | tf_op jit(solution)/shard_map/ppermute | solution.py:25
  30.6 6.2 %collective-permute-start.8 = (bf16[256,128]{1,0:T(8,128)(2,1)S(1)}, bf16[256,128]{1,0:T(8,128)(2,1)S(1)}, u32[]{:S(2)}, u32[]{:S(2)}) collective-permute-start(bf16[256,128]{1,0:T(8,128)(2,1)S(1)} %get-tuple-element.33), channel_id=1, source_target_pairs={{0,12},{4,8},{8,4},{12,0},{1,13},{5,9},{9,5},{13,1},{2,14},{6,10},... | collective-permute-start | bytes 196616 | tf_op jit(solution)/shard_map/ppermute | solution.py:25
  37.8 4.5 %collective-permute-start.12 = (bf16[136,128]{1,0:T(8,128)(2,1)S(1)}, bf16[136,128]{1,0:T(8,128)(2,1)S(1)}, u32[]{:S(2)}, u32[]{:S(2)}) collective-permute-start(bf16[136,128]{1,0:T(8,128)(2,1)S(1)} %get-tuple-element.38), channel_id=1, source_target_pairs={{0,4},{4,0},{8,12},{12,8},{1,5},{5,1},{9,13},{13,9},{2,6},{6,2},{1... | collective-permute-start | bytes 104456 | tf_op jit(solution)/shard_map/ppermute | solution.py:25
  38.6 5.0 %collective-permute-start.13 = (bf16[136,128]{1,0:T(8,128)(2,1)S(1)}, bf16[136,128]{1,0:T(8,128)(2,1)S(1)}, u32[]{:S(2)}, u32[]{:S(2)}) collective-permute-start(bf16[136,128]{1,0:T(8,128)(2,1)S(1)} %get-tuple-element.39), channel_id=1, source_target_pairs={{0,8},{4,12},{8,0},{12,4},{1,9},{5,13},{9,1},{13,5},{2,10},{6,14},... | collective-permute-start | bytes 104456 | tf_op jit(solution)/shard_map/ppermute | solution.py:25
  40.3 6.1 %collective-permute-start.14 = (bf16[136,128]{1,0:T(8,128)(2,1)S(1)}, bf16[136,128]{1,0:T(8,128)(2,1)S(1)}, u32[]{:S(2)}, u32[]{:S(2)}) collective-permute-start(bf16[136,128]{1,0:T(8,128)(2,1)S(1)} %get-tuple-element.40), channel_id=1, source_target_pairs={{0,12},{4,8},{8,4},{12,0},{1,13},{5,9},{9,5},{13,1},{2,14},{6,10},... | collective-permute-start | bytes 104456 | tf_op jit(solution)/shard_map/ppermute | solution.py:25
  46.5 4.5 %collective-permute-start.15 = (bf16[8,2048]{1,0:T(8,128)(2,1)S(1)}, bf16[8,2048]{1,0:T(8,128)(2,1)S(1)}, u32[]{:S(2)}, u32[]{:S(2)}) collective-permute-start(bf16[8,2048]{1,0:T(8,128)(2,1)S(1)} %shard_map.124.refs_0_), channel_id=1, source_target_pairs={{0,4},{4,0},{8,12},{12,8},{1,5},{5,1},{9,13},{13,9},{2,6},{6,2},{1... | collective-permute-start | bytes 98312 | tf_op jit(solution)/shard_map/ppermute | solution.py:25
  46.6 4.9 %collective-permute-start.16 = (bf16[8,2048]{1,0:T(8,128)(2,1)S(1)}, bf16[8,2048]{1,0:T(8,128)(2,1)S(1)}, u32[]{:S(2)}, u32[]{:S(2)}) collective-permute-start(bf16[8,2048]{1,0:T(8,128)(2,1)S(1)} %shard_map.124.refs_0_), channel_id=1, source_target_pairs={{0,8},{4,12},{8,0},{12,4},{1,9},{5,13},{9,1},{13,5},{2,10},{6,14},... | collective-permute-start | bytes 98312 | tf_op jit(solution)/shard_map/ppermute | solution.py:25
  48.9 5.7 %collective-permute-start.17 = (bf16[8,2048]{1,0:T(8,128)(2,1)S(1)}, bf16[8,2048]{1,0:T(8,128)(2,1)S(1)}, u32[]{:S(2)}, u32[]{:S(2)}) collective-permute-start(bf16[8,2048]{1,0:T(8,128)(2,1)S(1)} %shard_map.124.refs_0_), channel_id=1, source_target_pairs={{0,12},{4,8},{8,4},{12,0},{1,13},{5,9},{9,5},{13,1},{2,14},{6,10},... | collective-permute-start | bytes 98312 | tf_op jit(solution)/shard_map/ppermute | solution.py:25
  56.2 1.3 %collective-permute-start.18 = (bf16[16,2048]{1,0:T(8,128)(2,1)S(1)}, bf16[16,2048]{1,0:T(8,128)(2,1)S(1)}, u32[]{:S(2)}, u32[]{:S(2)}) collective-permute-start(bf16[16,2048]{1,0:T(8,128)(2,1)S(1)} %get-tuple-element.43), channel_id=1, source_target_pairs={{0,1},{1,0},{2,3},{3,2},{4,5},{5,4},{6,7},{7,6},{8,9},{9,8},{10,11... | collective-permute-start | bytes 196616 | tf_op jit(solution)/shard_map/ppermute | solution.py:20
  57.5 4.0 %collective-permute-start.19 = (bf16[8,2048]{1,0:T(8,128)(2,1)S(1)}, bf16[8,2048]{1,0:T(8,128)(2,1)S(1)}, u32[]{:S(2)}, u32[]{:S(2)}) collective-permute-start(bf16[8,2048]{1,0:T(8,128)(2,1)S(1)} %get-tuple-element.45), channel_id=1, source_target_pairs={{0,2},{2,0},{1,3},{3,1},{4,6},{6,4},{5,7},{7,5},{8,10},{10,8},{9,1... | collective-permute-start | bytes 98312 | tf_op jit(solution)/shard_map/ppermute | solution.py:20
